TPU v7x, 32 devices: a whole 2x2x4 slice. The times are simulated.
32 devices in a mesh: dp: 8 (over z, x), tensor: 4 (over y, core).
Axes of the slice: x: 2, y: 2, z: 4, core: 2. Of those that a mesh axis runs over, the one named last changes fastest.
Arguments:
- block_in: bfloat16 [2048, 8, 1024], P('tensor', 'dp'), may hold values from -6 to 6
- lengths: int32 [8, 8], P('dp'), may hold values from 1 to 2041, as said below
- qkv_weight: bfloat16 [1024, 3, 1024], P(None, None, 'tensor'), may hold values from -0.1875 to 0.1875
- out_weight: bfloat16 [1024, 1024], P('tensor'), may hold values from -0.1875 to 0.1875
- up_weight: bfloat16 [1024, 4096], P(None, 'tensor'), may hold values from -0.1875 to 0.1875
- down_weight: bfloat16 [4096, 1024], P('tensor'), may hold values from -0.09375 to 0.09375
- norm_gain: float32 [4, 1024], replicated, may hold values from 0.25 to 1.75
- norm_bias: float32 [4, 1024], replicated, may hold values from -2 to 2
- cotangent: bfloat16 [2048, 8, 1024], P('tensor', 'dp'), may hold values from -6 to 6
Outputs:
- block_out: bfloat16 [2048, 8, 1024], P('tensor', 'dp')
- input_grad: float32 [2048, 8, 1024], P('tensor', 'dp')
- qkv_grad: float32 [1024, 3, 1024], P(None, None, 'tensor')
- out_grad: float32 [1024, 1024], P('tensor')
- up_grad: float32 [1024, 4096], P(None, 'tensor')
- down_grad: float32 [4096, 1024], P('tensor')
- gain_grad: float32 [4, 1024], replicated
- bias_grad: float32 [4, 1024], replicated
Inputs may be any that keep to these rules, and one draw needn't show every extreme that they name: The 8 lengths of a row sum to 2048; one document of each row is longer than all others of the row together.
All inputs are finite; a program needn't handle non-finite values.
Results may differ from a plain program's by a relative error of at most 0.015.
Values may be sent and summed in bfloat16 or wider, within the bound.
A program may use at most 192 MiB of HBM per device.

v0:
```python
import jax
import jax.numpy as jnp
from jax import lax
from jax.sharding import PartitionSpec as P

HD = 64


EPSILON = 1e-05
ROPE_BASE = 10000.0


def layer_norm(values, gain, shift):
    centre = values - jnp.mean(values, axis=-1, keepdims=True)
    spread = jnp.mean(centre * centre, axis=-1, keepdims=True)
    return centre * lax.rsqrt(spread + EPSILON) * gain + shift


def doc_layout(lengths, length_total):
    finish = jnp.cumsum(lengths, axis=1)
    begin = finish - lengths
    places = jnp.arange(length_total, dtype=jnp.int32)
    segment = jnp.sum((places[:, None, None] >= finish[None, :, :]).astype(jnp.int32), axis=2)
    picked = segment[:, :, None] == jnp.arange(lengths.shape[1], dtype=jnp.int32)[None, None, :]
    position = places[:, None] - jnp.sum(jnp.where(picked, begin[None, :, :], 0), axis=2)
    return (segment, position)


def rope_tables(position, head_size):
    half_size = head_size // 2
    inverse = ROPE_BASE ** (-jnp.arange(half_size, dtype=jnp.float32) * 2.0 / head_size)
    angles = position.astype(jnp.float32)[..., None] * inverse
    return (jnp.cos(angles), jnp.sin(angles))


def rotate(values, cosine, sine):
    half_size = values.shape[-1] // 2
    first = values[..., :half_size]
    second = values[..., half_size:]
    return jnp.concatenate(
        [first * cosine - second * sine, second * cosine + first * sine], axis=-1
    )


def masked_scores(query_block, keys, segment_block, place_block, segment, places):
    scores = jnp.einsum(
        "qrhd,krhd->rhqk", query_block, keys, preferred_element_type=jnp.float32
    ) * HD ** (-0.5)
    visible = (segment_block.T[:, None, :, None] == segment.T[:, None, None, :]) & (
        places[None, None, None, :] <= place_block[None, None, :, None]
    )
    return jnp.where(visible, scores, -1e30)


def attend_forward(queries, keys, values, segment):
    length_total, row_count, head_count, head_size = queries.shape
    block_rows = min(512, length_total)
    blocks = length_total // block_rows
    places = jnp.arange(length_total, dtype=jnp.int32)

    def one_block(pieces):
        query_block, segment_block, place_block = pieces
        scores = masked_scores(query_block, keys, segment_block, place_block, segment, places)
        top_score = jnp.max(scores, axis=-1, keepdims=True)
        weights_exp = jnp.exp(scores - top_score)
        total_exp = jnp.sum(weights_exp, axis=-1, keepdims=True)
        probs = weights_exp / total_exp
        mixed = jnp.einsum(
            "rhqk,krhd->qrhd",
            probs.astype(jnp.bfloat16),
            values,
            preferred_element_type=jnp.float32,
        )
        return (mixed, (top_score + jnp.log(total_exp))[..., 0])

    mixed, log_totals = lax.map(
        one_block,
        (
            queries.reshape(blocks, block_rows, row_count, head_count, head_size),
            segment.reshape(blocks, block_rows, row_count),
            places.reshape(blocks, block_rows),
        ),
    )
    return (mixed.reshape(length_total, row_count, head_count * head_size), log_totals)


def attend_backward(queries, keys, values, grad_heads, log_totals, segment):
    length_total, row_count, head_count, head_size = queries.shape
    block_rows = min(512, length_total)
    blocks = length_total // block_rows
    places = jnp.arange(length_total, dtype=jnp.int32)
    scale_factor = HD ** (-0.5)

    def one_block(carry, pieces):
        key_total, value_total = carry
        query_block, grad_block, log_block, segment_block, place_block = pieces
        scores = masked_scores(query_block, keys, segment_block, place_block, segment, places)
        probs = jnp.exp(scores - log_block[..., None])
        grad_probs = jnp.einsum(
            "qrhd,krhd->rhqk", grad_block, values, preferred_element_type=jnp.float32
        )
        inner_sum = jnp.sum(probs * grad_probs, axis=-1, keepdims=True)
        grad_scores = (probs * (grad_probs - inner_sum)).astype(jnp.bfloat16)
        grad_query = (
            jnp.einsum("rhqk,krhd->qrhd", grad_scores, keys, preferred_element_type=jnp.float32)
            * scale_factor
        )
        key_total = (
            key_total
            + jnp.einsum(
                "rhqk,qrhd->krhd", grad_scores, query_block, preferred_element_type=jnp.float32
            )
            * scale_factor
        )
        value_total = value_total + jnp.einsum(
            "rhqk,qrhd->krhd",
            probs.astype(jnp.bfloat16),
            grad_block,
            preferred_element_type=jnp.float32,
        )
        return ((key_total, value_total), grad_query)

    start_totals = (jnp.zeros(keys.shape, jnp.float32), jnp.zeros(values.shape, jnp.float32))
    (grad_keys, grad_values), grad_queries = lax.scan(
        one_block,
        start_totals,
        (
            queries.reshape(blocks, block_rows, row_count, head_count, head_size),
            grad_heads.reshape(blocks, block_rows, row_count, head_count, head_size),
            log_totals,
            segment.reshape(blocks, block_rows, row_count),
            places.reshape(blocks, block_rows),
        ),
    )
    return (
        grad_queries.reshape(length_total, row_count, head_count, head_size),
        grad_keys,
        grad_values,
    )


def body(
    block_in,
    lengths,
    qkv_weight,
    out_weight,
    up_weight,
    down_weight,
    norm_gain,
    norm_bias,
    cotangent,
):
    local_len, row_count, width = block_in.shape
    length_total = local_len * lax.axis_size("tensor")
    local_width = out_weight.shape[0]
    head_count = local_width // HD
    segment, position = doc_layout(lengths, length_total)
    cosine, sine = rope_tables(position, HD)
    cosine = cosine[:, :, None, :]
    sine = sine[:, :, None, :]
    residual_in = block_in.astype(jnp.float32)
    attn_norm, attn_norm_pull = jax.vjp(layer_norm, residual_in, norm_gain[0], norm_bias[0])
    attn_input = lax.all_gather(attn_norm.astype(jnp.bfloat16), "tensor", axis=0, tiled=True)
    qkv_flat = qkv_weight.reshape(width, 3 * local_width)
    project = jnp.einsum("srd,dk->srk", attn_input, qkv_flat, preferred_element_type=jnp.float32)
    project = project.reshape(length_total, row_count, 3, head_count, HD)
    queries = rotate(project[:, :, 0], cosine, sine).astype(jnp.bfloat16)
    keys_rotated = rotate(project[:, :, 1], cosine, sine).astype(jnp.bfloat16)
    values_low = project[:, :, 2].astype(jnp.bfloat16)
    heads_out, log_totals = attend_forward(queries, keys_rotated, values_low, segment)
    heads_low = heads_out.astype(jnp.bfloat16)
    attn_proj = lax.psum_scatter(
        jnp.einsum("srk,kd->srd", heads_low, out_weight, preferred_element_type=jnp.float32),
        "tensor",
        scatter_dimension=0,
        tiled=True,
    )
    attn_branch, attn_branch_pull = jax.vjp(layer_norm, attn_proj, norm_gain[1], norm_bias[1])
    middle = residual_in + attn_branch
    mlp_norm, mlp_norm_pull = jax.vjp(layer_norm, middle, norm_gain[2], norm_bias[2])
    mlp_input = lax.all_gather(mlp_norm.astype(jnp.bfloat16), "tensor", axis=0, tiled=True)
    upward = jnp.einsum("srd,df->srf", mlp_input, up_weight, preferred_element_type=jnp.float32)
    activated, gelu_pull = jax.vjp(jax.nn.gelu, upward)
    hidden = activated.astype(jnp.bfloat16)
    mlp_proj = lax.psum_scatter(
        jnp.einsum("srf,fd->srd", hidden, down_weight, preferred_element_type=jnp.float32),
        "tensor",
        scatter_dimension=0,
        tiled=True,
    )
    mlp_branch, mlp_branch_pull = jax.vjp(layer_norm, mlp_proj, norm_gain[3], norm_bias[3])
    block_out = (middle + mlp_branch).astype(jnp.bfloat16)
    grad_out_rows = cotangent.astype(jnp.float32)
    grad_mlp_proj, gain_three, shift_three = mlp_branch_pull(grad_out_rows)
    grad_mlp_full = lax.all_gather(grad_mlp_proj.astype(jnp.bfloat16), "tensor", axis=0, tiled=True)
    down_grad = jnp.einsum("srf,srd->fd", hidden, grad_mlp_full, preferred_element_type=jnp.float32)
    grad_hidden = jnp.einsum(
        "srd,fd->srf", grad_mlp_full, down_weight, preferred_element_type=jnp.float32
    )
    grad_upward = gelu_pull(grad_hidden)[0].astype(jnp.bfloat16)
    up_grad = jnp.einsum("srd,srf->df", mlp_input, grad_upward, preferred_element_type=jnp.float32)
    grad_mlp_norm = lax.psum_scatter(
        jnp.einsum("srf,df->srd", grad_upward, up_weight, preferred_element_type=jnp.float32),
        "tensor",
        scatter_dimension=0,
        tiled=True,
    )
    grad_from_norm, gain_two, shift_two = mlp_norm_pull(grad_mlp_norm)
    grad_middle = grad_out_rows + grad_from_norm
    grad_attn_proj, gain_one, shift_one = attn_branch_pull(grad_middle)
    grad_attn_full = lax.all_gather(
        grad_attn_proj.astype(jnp.bfloat16), "tensor", axis=0, tiled=True
    )
    out_grad = jnp.einsum(
        "srk,srd->kd", heads_low, grad_attn_full, preferred_element_type=jnp.float32
    )
    grad_heads = jnp.einsum(
        "srd,kd->srk", grad_attn_full, out_weight, preferred_element_type=jnp.float32
    )
    grad_heads = grad_heads.astype(jnp.bfloat16).reshape(length_total, row_count, head_count, HD)
    grad_queries, grad_keys, grad_values = attend_backward(
        queries, keys_rotated, values_low, grad_heads, log_totals, segment
    )
    grad_project = (
        jnp.stack(
            [rotate(grad_queries, cosine, -sine), rotate(grad_keys, cosine, -sine), grad_values],
            axis=2,
        )
        .astype(jnp.bfloat16)
        .reshape(length_total, row_count, 3 * local_width)
    )
    qkv_grad = jnp.einsum(
        "srd,srk->dk", attn_input, grad_project, preferred_element_type=jnp.float32
    ).reshape(width, 3, local_width)
    grad_attn_norm = lax.psum_scatter(
        jnp.einsum(
            "srk,dk->srd", grad_project, qkv_flat, preferred_element_type=jnp.float32
        ).astype(jnp.bfloat16),
        "tensor",
        scatter_dimension=0,
        tiled=True,
    ).astype(jnp.float32)
    grad_from_first, gain_zero, shift_zero = attn_norm_pull(grad_attn_norm)
    input_grad = grad_middle + grad_from_first
    gain_terms = jnp.stack([gain_zero, gain_one, gain_two, gain_three])
    shift_terms = jnp.stack([shift_zero, shift_one, shift_two, shift_three])
    gain_grad, bias_grad = lax.psum((gain_terms, shift_terms), ("dp", "tensor"))
    qkv_grad, out_grad, up_grad, down_grad = lax.psum(
        (qkv_grad, out_grad, up_grad, down_grad), "dp"
    )
    return (block_out, input_grad, qkv_grad, out_grad, up_grad, down_grad, gain_grad, bias_grad)


def solution(mesh):
    return jax.shard_map(
        body,
        mesh=mesh,
        in_specs=(
            P("tensor", "dp", None),
            P("dp", None),
            P(None, None, "tensor"),
            P("tensor", None),
            P(None, "tensor"),
            P("tensor", None),
            P(),
            P(),
            P("tensor", "dp", None),
        ),
        out_specs=(
            P("tensor", "dp", None),
            P("tensor", "dp", None),
            P(None, None, "tensor"),
            P("tensor", None),
            P(None, "tensor"),
            P("tensor", None),
            P(),
            P(),
        ),
        check_vma=False,
    )
```

profile of v0, /device:TPU:20, one launch (start us, length us, event | category | flops | bytes accessed | tf_op | source)
XLA Modules:
  0.0 1242.6 jit_solution(6349986049035437628)
XLA Ops:
  18.7 29.9 %all-gather.5.cloned.1.call-done = bf16[2048,1,1024]{2,0,1:T(8,128)(2,1)} async-done(((bf16[512,1,1024]{2,0,1:T(8,128)(2,1)}), bf16[2048,1,1024]{2,0,1:T(8,128)(2,1)}) %all-gather.5.cloned.1.call-update) | async-done | bytes 4194320 | tf_op jit(solution)/shard_map/all_gather | solution.py:163
  48.6 5.7 fusion.74
  57.7 63.6 %while.28 = (s32[]{:T(128)}, bf16[4,512,1,4,64]{1,4,3,2,0:T(8,128)(2,1)}, f32[4,1,4,512]{3,2,1,0:T(4,128)}, s32[4,512,1]{1,2,0:T(1,128)S(1)}, s32[2048,1]{0,1:T(...) while((s32[]{:T(128)}, ...), condition=%wide.region_8.9_spmd.clone, body=%wide.region_5.8_spmd.clone.sunk | while | flops 1127217152 | bytes 70078680 | solution.py:76
  58.9 4.5 fusion.146
  63.5 4.3 fusion.147
  67.8 4.8 fusion.148
  74.8 4.5 fusion.146
  79.3 4.3 fusion.147
  83.7 4.8 fusion.148
  90.7 4.5 fusion.146
  95.2 4.3 fusion.147
  99.6 4.8 fusion.148
  106.5 4.5 fusion.146
  111.1 4.3 fusion.147
  115.4 4.8 fusion.148
  124.7 4.5 convolution_bitcast_fusion.2
  129.3 71.8 %reduce-scatter.5.cloned.1.call-done = f32[512,1,1024]{2,0,1:T(8,128)} async-done(((f32[2048,1,1024]{2,0,1:T(8,128)}), f32[512,1,1024]{2,0,1:T(8,128)}) %reduce-scatter.5.cloned.1.call-update) | async-done | bytes 2097168 | tf_op jit(solution)/shard_map/reduce_scatter | solution.py:172
  209.9 34.6 %all-gather.7.cloned.1.call-done = bf16[2048,1,1024]{2,0,1:T(8,128)(2,1)} async-done(((bf16[512,1,1024]{2,0,1:T(8,128)(2,1)}), bf16[2048,1,1024]{2,0,1:T(8,128)(2,1)}) %all-gather.7.cloned.1.call-update) | async-done | bytes 4194320 | tf_op jit(solution)/shard_map/all_gather | solution.py:181
  244.4 6.9 fusion.72
  254.6 7.3 convolution_bitcast_fusion.1
  261.9 71.8 %reduce-scatter.7.cloned.1.call-done = f32[512,1,1024]{2,0,1:T(8,128)} async-done(((f32[2048,1,1024]{2,0,1:T(8,128)}), f32[512,1,1024]{2,0,1:T(8,128)}) %reduce-scatter.7.cloned.1.call-update) | async-done | bytes 2097168 | tf_op jit(solution)/shard_map/reduce_scatter | solution.py:185
  343.7 34.6 %all-gather.9.cloned.1.call-done = bf16[2048,1,1024]{2,0,1:T(8,128)(2,1)} async-done(((bf16[512,1,1024]{2,0,1:T(8,128)(2,1)}), bf16[2048,1,1024]{2,0,1:T(8,128)(2,1)}) %all-gather.9.cloned.1.call-update) | async-done | bytes 4194320 | tf_op jit(solution)/shard_map/all_gather | solution.py:195
  378.3 12.4 fusion.57
  392.7 7.0 convolution_bitcast_fusion
  399.7 71.8 %reduce-scatter.9.cloned.1.call-done = f32[512,1,1024]{2,0,1:T(8,128)} async-done(((f32[2048,1,1024]{2,0,1:T(8,128)}), f32[512,1,1024]{2,0,1:T(8,128)}) %reduce-scatter.9.cloned.1.call-update) | async-done | bytes 2097168 | tf_op jit(solution)/shard_map/reduce_scatter | solution.py:202
  480.7 34.6 %all-gather.11.cloned.1.call-done = bf16[2048,1,1024]{2,0,1:T(8,128)(2,1)} async-done(((bf16[512,1,1024]{2,0,1:T(8,128)(2,1)}), bf16[2048,1,1024]{2,0,1:T(8,128)(2,1)}) %all-gather.11.cloned.1.call-update) | async-done | bytes 4194320 | tf_op jit(solution)/shard_map/all_gather | solution.py:211
  515.3 4.5 fusion.83
  525.4 233.8 %while.29 = (s32[]{:T(128)}, f32[2048,1,4,64]{0,3,2,1:T(8,128)}, f32[2048,1,4,64]{0,3,2,1:T(8,128)}, f32[4,512,1,4,64]{1,0,4,3,2:T(4,128)}, bf16[4,512,1,4,64]{1...) while((s32[]{:T(128)}, f32[2048,1,4,64]{0,3,2,1:T(8,128)}, ...), condition=%wide.region_26.27_spmd.clone, body=%wide.region_24.26_spmd.clone.sunk | while | flops 2753165312 | bytes 183185760 | solution.py:124
  531.9 7.2 fusion.160
  539.1 11.5 multiply_reduce_fusion.9
  550.6 10.9 multiply_convert_fusion.5
  561.5 6.2 fusion.161
  567.8 3.9 fusion.159
  572.2 11.1 dynamic_update_slice.21
  585.8 3.5 fusion.157
  589.3 7.6 fusion.160
  597.0 11.5 multiply_reduce_fusion.9
  608.4 10.9 multiply_convert_fusion.5
  619.4 6.2 fusion.161
  625.6 4.6 fusion.159
  630.8 11.1 dynamic_update_slice.21
  644.4 3.5 fusion.157
  647.9 7.6 fusion.160
  655.5 11.5 multiply_reduce_fusion.9
  667.0 10.9 multiply_convert_fusion.5
  678.0 6.2 fusion.161
  684.2 4.6 fusion.159
  689.4 11.1 dynamic_update_slice.21
  703.0 3.5 fusion.157
  706.5 7.6 fusion.160
  714.1 11.5 multiply_reduce_fusion.9
  725.6 10.9 multiply_convert_fusion.5
  736.5 6.2 fusion.161
  742.8 4.6 fusion.159
  748.0 11.1 dynamic_update_slice.21
  759.2 3.8 reshape.1007
  767.5 5.1 convert_bitcast_fusion
  772.7 10.6 fusion.70
  783.3 11.4 fusion.66
  797.1 5.4 fusion.58
  802.5 14.8 %reduce-scatter.11.cloned.1.call-done = bf16[512,1,1024]{2,0,1:T(8,128)(2,1)} async-done(((bf16[2048,1,1024]{2,0,1:T(8,128)(2,1)}), bf16[512,1,1024]{2,0,1:T(8,128)(2,1)}) %reduce-scatter.11.cloned.1.call-update) | async-done | bytes 1048592 | tf_op jit(solution)/shard_map/reduce_scatter | solution.py:235
  826.2 45.8 %all-reduce = (f32[4,1024]{1,0:T(4,128)}, f32[4,1024]{1,0:T(4,128)}) all-reduce(f32[4,1024]{1,0:T(4,128)S(1)} %pad_maximum_fusion.1, f32[4,1024]{1,0:T(4,128)S(1)} %pad_maximum_fusion.2), channel_id=1, replica_groups=mesh['dp'=8,'tensor'=4] {'dp','tensor'}, use_global_device_ids=true, to_apply=%region_38.39 | all-reduce | flops 8192 | bytes 65536 | tf_op jit(solution)/shard_map/psum | solution.py:247
  872.0 352.1 %all-reduce.4.cloned.1.call-done = (f32[1024,3,256]{2,0,1:T(8,128)}, f32[256,1024]{1,0:T(8,128)}, f32[1024,1024]{1,0:T(8,128)}, f32[1024,1024]{1,0:T(8,128)}) async-done(((f32[1024,3,256]{2,0,1:T(8,128)}, f32[256,1024]{1,0:T(8,128)}, f32[1024,1024]{1,0:T(8,128)}, f32[1024,1024]{1,0:T(8,128)}), (f32[1024,3,256]{2,0,1:T(8,128)}, f32[256,1024]{1,0:T(8,128)}, f32[1024,1024]{1,0:T(8,128)}, ...) | async-done | bytes 12582928 | tf_op jit(solution)/shard_map/psum | solution.py:248
  1224.1 3.9 copy.108
  (316 shorter events, 104.4 us)
Async XLA Ops:
  7.2 247.4 %copy-start = (bf16[1024,1024]{1,0:T(8,128)(2,1)S(1)}, bf16[1024,1024]{1,0:T(8,128)(2,1)}, u32[]{:S(2)}) copy-start(bf16[1024,1024]{1,0:T(8,128)(2,1)} %param.18) | copy-start | bytes 6291460
  7.2 5.2 copy-start.10
  7.2 3.9 copy-start.55
  7.2 4.5 copy-start.56
  7.2 41.3 %all-gather.5.cloned.1.call-start = ((), (), s32[]{:S(2)}) async-start(), calls=%async_computation.4 | async-start | bytes 5242880 | tf_op jit(solution)/shard_map/all_gather | solution.py:163
  8.9 5.0 copy-start.64
  13.8 187.3 %reduce-scatter.5.cloned.1.call-start = ((), (), s32[]{:S(2)}) async-start(), calls=%async_computation.5 | async-start | bytes 10485760 | tf_op jit(solution)/shard_map/reduce_scatter | solution.py:172
  18.7 37.2 %copy-start.25 = (f32[2048,32]{0,1:T(8,128)}, f32[2048,32]{0,1:T(8,128)S(1)}, u32[]{:S(2)}) copy-start(f32[2048,32]{0,1:T(8,128)S(1)} %get-tuple-element.355) | copy-start | bytes 786436
  63.5 4.4 copy-start.12
  63.5 4.4 copy-start.31
  79.3 4.4 copy-start.12
  79.3 4.4 copy-start.31
  95.2 4.4 copy-start.12
  95.2 4.4 copy-start.31
  111.0 4.4 copy-start.12
  111.0 4.4 copy-start.31
  129.3 75.8 %copy-start.42 = (f32[1,1024]{1,0:T(1,128)S(1)}, f32[1,1024]{1,0:T(1,128)}, u32[]{:S(2)}) copy-start(f32[1,1024]{1,0:T(1,128)} %get-tuple-element.346) | copy-start | bytes 12292
  129.3 75.8 %copy-start.59 = (f32[1,1024]{1,0:T(1,128)S(1)}, f32[1,1024]{1,0:T(1,128)}, u32[]{:S(2)}) copy-start(f32[1,1024]{1,0:T(1,128)} %get-tuple-element.350) | copy-start | bytes 12292
  129.3 115.2 %all-gather.7.cloned.1.call-start = ((), (), s32[]{:S(2)}) async-start(), calls=%async_computation.6 | async-start | bytes 5242880 | tf_op jit(solution)/shard_map/all_gather | solution.py:181
  209.8 123.9 %reduce-scatter.7.cloned.1.call-start = ((), (), s32[]{:S(2)}) async-start(), calls=%async_computation.7 | async-start | bytes 10485760 | tf_op jit(solution)/shard_map/reduce_scatter | solution.py:185
  261.9 75.8 %copy-start.44 = (f32[1,1024]{1,0:T(1,128)S(1)}, f32[1,1024]{1,0:T(1,128)}, u32[]{:S(2)}) copy-start(f32[1,1024]{1,0:T(1,128)} %get-tuple-element.345) | copy-start | bytes 12292
  261.9 116.4 %all-gather.9.cloned.1.call-start = ((), (), s32[]{:S(2)}) async-start(), calls=%async_computation.8 | async-start | bytes 5242880 | tf_op jit(solution)/shard_map/all_gather | solution.py:195
  343.6 127.9 %reduce-scatter.9.cloned.1.call-start = ((), (), s32[]{:S(2)}) async-start(), calls=%async_computation.9 | async-start | bytes 10485760 | tf_op jit(solution)/shard_map/reduce_scatter | solution.py:202
  378.3 14.4 %copy-start.63 = (bf16[1024,1024]{1,0:T(8,128)(2,1)S(1)}, bf16[1024,1024]{1,0:T(8,128)(2,1)}, u32[]{:S(2)}) copy-start(bf16[1024,1024]{1,0:T(8,128)(2,1)} %param.17) | copy-start | bytes 6291460
  399.7 71.9 %copy-start.7 = (f32[512,1,1024]{2,0,1:T(8,128)S(1)}, f32[512,1,1024]{2,0,1:T(8,128)}, u32[]{:S(2)}) copy-start(f32[512,1,1024]{2,0,1:T(8,128)} %copy-done.5) | copy-start | bytes 6291460
  399.7 115.6 %all-gather.11.cloned.1.call-start = ((), (), s32[]{:S(2)}) async-start(), calls=%async_computation.10 | async-start | bytes 5242880 | tf_op jit(solution)/shard_map/all_gather | solution.py:211
  479.5 35.8 %copy-start.35 = (bf16[256,1024]{1,0:T(8,128)(2,1)S(1)}, bf16[256,1024]{1,0:T(8,128)(2,1)}, u32[]{:S(2)}) copy-start(bf16[256,1024]{1,0:T(8,128)(2,1)} %param.16) | copy-start | bytes 1572868
  480.7 336.7 %reduce-scatter.11.cloned.1.call-start = ((), (), s32[]{:S(2)}) async-start(), calls=%async_computation.11 | async-start | bytes 5242880 | tf_op jit(solution)/shard_map/reduce_scatter | solution.py:235
  561.5 6.2 copy-start.2
  571.7 11.6 copy-start.28
  571.7 11.6 copy-start.39
  585.8 3.5 copy-start.3
  619.4 6.2 copy-start.2
  630.3 11.6 copy-start.28
  630.3 11.6 copy-start.39
  644.4 3.5 copy-start.3
  677.9 6.2 copy-start.2
  688.8 11.6 copy-start.28
  688.8 11.6 copy-start.39
  702.9 3.5 copy-start.3
  736.5 6.2 copy-start.2
  747.4 11.6 copy-start.28
  747.4 11.6 copy-start.39
  759.2 3.8 copy-start.4
  759.2 3.8 copy-start.26
  759.2 3.8 copy-start.33
  772.7 451.4 %all-reduce.4.cloned.1.call-start = ((), (), s32[]{:S(2)}) async-start(), calls=%async_computation.12 | async-start | bytes 25165824 | tf_op jit(solution)/shard_map/psum | solution.py:248
  772.7 10.6 copy-start.61
  783.3 11.5 copy-start.22
  783.3 11.5 copy-start.62
  802.5 14.9 %copy-start.11 = (bf16[512,1,1024]{2,0,1:T(8,128)(2,1)S(1)}, bf16[512,1,1024]{2,0,1:T(8,128)(2,1)}, u32[]{:S(2)}) copy-start(bf16[512,1,1024]{2,0,1:T(8,128)(2,1)} %param.13) | copy-start | bytes 3145732
  802.5 14.9 %copy-start.37 = (f32[1,1024]{1,0:T(1,128)S(1)}, f32[1,1024]{1,0:T(1,128)}, u32[]{:S(2)}) copy-start(f32[1,1024]{1,0:T(1,128)} %copy-done.36) | copy-start | bytes 12292
  802.5 14.9 %copy-start.41 = (f32[512]{0:T(512)S(1)}, f32[512]{0:T(512)}, u32[]{:S(2)}) copy-start(f32[512]{0:T(512)} %copy-done.40) | copy-start | bytes 6148
  802.5 16.9 %copy-start.48 = (f32[512]{0:T(512)S(1)}, f32[512]{0:T(512)}, u32[]{:S(2)}) copy-start(f32[512]{0:T(512)} %copy-done.47) | copy-start | bytes 6148
  802.5 16.9 %copy-start.46 = (f32[512]{0:T(512)S(1)}, f32[512]{0:T(512)}, u32[]{:S(2)}) copy-start(f32[512]{0:T(512)} %copy-done.45) | copy-start | bytes 6148
  802.5 19.3 %copy-start.16 = (f32[512,1,1024]{2,0,1:T(8,128)S(1)}, f32[512,1,1024]{2,0,1:T(8,128)}, u32[]{:S(2)}) copy-start(f32[512,1,1024]{2,0,1:T(8,128)} %copy-done.15) | copy-start | bytes 6291460
  817.4 4.5 copy-start.17
  822.6 3.5 copy-start.50
  822.6 3.5 copy-start.49
  822.6 3.5 copy-start.51
  822.6 3.5 copy-start.57
  1224.1 3.9 copy-start.30
  1224.1 4.9 copy-start.24
  1229.0 3.7 copy-start.23
  (39 other events, 71.1 us)
Sparse Core Ops, SparseCore 0:
  13.9 34.5 all-gather.4
  129.4 71.7 reduce-scatter.4
  209.9 34.4 all-gather.6
  262.0 71.6 reduce-scatter.6
  343.8 34.4 all-gather.8
  399.8 71.7 reduce-scatter.8
  480.8 34.4 all-gather.10
  772.8 44.5 reduce-scatter.10
  822.7 401.3 all-reduce.3
where the time goes:
time: 1260 us; the launch traced here: 1240 us
  waiting for transfers between devices  716 us (57%)
  matrix products  253 us (20%)
  other arithmetic  115 us (9%)
  local copies, waits for them, and re-layouts  96.1 us (8%)
  blocking collectives  45.8 us (4%)
  between operations  14.8 us (1%)
    psum x1, waiting for transfers between devices, body(): lax.psum((qkv_grad, out_grad, up_grad, down_grad), 'dp')  352 us
    reduce_scatter x1, waiting for transfers between devices, body(): lax.psum_scatter(jnp.einsum('srf,df->srd', grad_upward, up_weight, prefer...  71.8 us
    reduce_scatter x1, waiting for transfers between devices, body(): lax.psum_scatter(jnp.einsum('srk,kd->srd', heads_low, out_weight, preferr...  71.8 us
    reduce_scatter x1, waiting for transfers between devices, body(): lax.psum_scatter(jnp.einsum('srf,fd->srd', hidden, down_weight, preferred...  71.8 us
    dynamic_update_slice x8, local copies, waits for them, and re-layouts, attend_forward(): lax.map(one_block, (queries.reshape(blocks, block_rows, row_count, head_c...  46.5 us
    dot_general x4, matrix products, one_block(): jnp.einsum('qrhd,krhd->rhqk', grad_block, values, preferred_element_type=...  45.9 us
    psum x1, blocking collectives, body(): gain_grad, bias_grad = lax.psum((gain_terms, shift_terms), ('dp', 'tensor'))  45.8 us
    convert_element_type x4, other arithmetic, one_block(): grad_scores = (probs * (grad_probs - inner_sum)).astype(jnp.bfloat16)  43.7 us
  transfers between devices with their start and end apart: 9, of which 9 were waited for; matrix products, arithmetic and copies ran while one was open for 3% of the time, Pallas kernels for 0%

commit v1 on v0

v1 whole, which is shorter than its diff:
```python
import functools

import jax
import jax.numpy as jnp
from jax import lax
from jax.experimental import pallas as pl
from jax.experimental.pallas import tpu as pltpu
from jax.sharding import PartitionSpec as P

HD = 64
PAIR = 128
EPSILON = 1e-05
ROPE_BASE = 10000.0
NEG = -1e30
BF = jnp.bfloat16
F32 = jnp.float32
NT = (((1,), (1,)), ((), ()))
NN = (((1,), (0,)), ((), ()))
TN = (((0,), (0,)), ((), ()))


def dot(a, b, dims=NN):
    return lax.dot_general(a, b, dims, preferred_element_type=F32)


def layer_norm(values, gain, shift):
    centre = values - jnp.mean(values, axis=-1, keepdims=True)
    spread = jnp.mean(centre * centre, axis=-1, keepdims=True)
    return centre * lax.rsqrt(spread + EPSILON) * gain + shift


def swap(value, axis, offset):
    size = lax.axis_size(axis)
    return lax.ppermute(value, axis, [(i, i ^ offset) for i in range(size)])


def gather_tensor(value):
    parts = [value]
    size = lax.axis_size("tensor")
    step = size // 2
    found = {0: value}
    while step >= 1:
        for place in sorted(found):
            found[place ^ step] = swap(found[place], "tensor", step)
        step //= 2
    parts = [found[d] for d in range(size)]
    return parts


def reduce_scatter_tensor(parts):
    size = lax.axis_size("tensor")
    terms = {d: parts[d] for d in range(size)}
    step = 1
    while step < size:
        kept = {}
        for d in sorted(terms):
            if d & step == 0:
                got = swap(terms[d ^ step].astype(BF), "tensor", step)
                kept[d] = terms[d].astype(F32) + got.astype(F32)
        terms = kept
        step *= 2
    return terms[0]


def tree_sum(parts):
    parts = [part.astype(F32) for part in parts]
    while len(parts) > 1:
        parts = [parts[i] + parts[i + 1] for i in range(0, len(parts), 2)]
    return parts[0]


def sum_all(value):
    for axis in ("tensor", "dp"):
        size = lax.axis_size(axis)
        value = tree_sum([value] + [swap(value, axis, d) for d in range(1, size)])
    return value


def in_order(parts, index):
    size = len(parts)
    step = 1
    while step < size:
        flip = (index & step) != 0
        parts = [jnp.where(flip, parts[d ^ step], parts[d]) for d in range(size)]
        step *= 2
    return parts


def reduce_dp(partial, direct):
    size = lax.axis_size("dp")
    index = lax.axis_index("dp")
    rows = partial.shape[0]
    shift = 0
    if not direct:
        half = rows // 2
        bit = index & 1
        there = lax.dynamic_slice_in_dim(partial, (1 - bit) * half, half, 0).astype(BF)
        here = lax.dynamic_slice_in_dim(partial, bit * half, half, 0)
        got = swap(there, "dp", 1)
        partial = (here.astype(F32) + got.astype(F32)).astype(BF)
        rows, shift = half, 1
    group = size >> shift
    place = index >> shift
    piece = rows // group
    parts = [lax.dynamic_slice_in_dim(partial, place * piece, piece, 0)]
    for d in range(1, group):
        part = lax.dynamic_slice_in_dim(partial, (place ^ d) * piece, piece, 0).astype(BF)
        parts.append(swap(part, "dp", d << shift))
    total = tree_sum(parts).astype(BF)
    parts = [total] + [swap(total, "dp", d << shift) for d in range(1, group)]
    full = jnp.concatenate(in_order(parts, place), axis=0)
    if not direct:
        got = swap(full, "dp", 1)
        flip = (index & 1) != 0
        full = jnp.concatenate([jnp.where(flip, got, full), jnp.where(flip, full, got)], axis=0)
    return full.astype(F32)


def turn(values, cosine, signed_sine):
    lane = lax.broadcasted_iota(jnp.int32, values.shape, 1)
    other = jnp.where(lane % HD < HD // 2, pltpu.roll(values, PAIR - HD // 2, 1), pltpu.roll(values, HD // 2, 1))
    return values * cosine + other * signed_sine


def qkv_kernel(pairs, place_ref, x_ref, w_ref, cos_ref, sin_ref, out_ref):
    x = x_ref[...]
    for part in range(3):
        project = dot(x, w_ref[part])
        for pair in range(pairs):
            piece = project[:, pair * PAIR : (pair + 1) * PAIR]
            if part < 2:
                piece = turn(piece, cos_ref[...], sin_ref[...])
            out_ref[part * pairs + pair] = piece.astype(BF)


def project_qkv(place, tokens, weight, cosine, sine, block):
    length, width = tokens.shape
    columns = weight.shape[2]
    pairs = columns // PAIR
    real = lambda d, place: (d ^ place[0], 0)
    return pl.pallas_call(
        functools.partial(qkv_kernel, pairs),
        out_shape=jax.ShapeDtypeStruct((3 * pairs, length, PAIR), BF),
        grid_spec=pltpu.PrefetchScalarGridSpec(
            num_scalar_prefetch=1,
            grid=(length // block,),
            in_specs=[
                pl.BlockSpec((block, width), lambda d, place: (d, 0)),
                pl.BlockSpec((3, width, columns), lambda d, place: (0, 0, 0)),
                pl.BlockSpec((block, PAIR), real),
                pl.BlockSpec((block, PAIR), real),
            ],
            out_specs=pl.BlockSpec((3 * pairs, block, PAIR), lambda d, place: (0, d, 0)),
        ),
        compiler_params=pltpu.CompilerParams(vmem_limit_bytes=40 << 20),
        cost_estimate=pl.CostEstimate(flops=2 * length * width * 3 * columns, bytes_accessed=2 * length * width, transcendentals=0),
        name="project_qkv",
    )(place, tokens, weight, cosine, sine)


def head_mask(shape, head):
    lane = lax.broadcasted_iota(jnp.int32, shape, 1)
    return lane // HD == head


def forward_kernel(block, place_ref, q_ref, k_ref, v_ref, start_ref, out_ref, log_ref, scores_ref):
    mine = place_ref[0]
    row_block = pl.program_id(0) ^ mine
    queries = q_ref[...] * HD**-0.5
    start = start_ref[...]
    mixed = None
    for head in range(PAIR // HD):
        mask = head_mask(queries.shape, head)
        query = jnp.where(mask, queries, jnp.zeros_like(queries))

        def score(j, top, last):
            keys = k_ref[pl.ds(pl.multiple_of((j ^ mine) * block, block), block), :]
            s = dot(query, keys, NT)
            column = lax.broadcasted_iota(jnp.int32, s.shape, 1)
            visible = column >= start - j * block
            if last:
                visible &= column <= lax.broadcasted_iota(jnp.int32, s.shape, 0)
            s = jnp.where(visible, s, NEG)
            scores_ref[j] = s
            for c in range(0, block, 128):
                top = jnp.maximum(top, s[:, c : c + 128])
            return top

        top = jnp.full((block, 128), NEG, F32)
        top = lax.fori_loop(0, row_block, lambda j, top: score(j, top, False), top)
        top = score(row_block, top, True)
        top = jnp.max(top, axis=1, keepdims=True)

        def mix(j, carry):
            total, acc = carry
            weights = jnp.exp(scores_ref[j] - top)
            for c in range(0, block, 128):
                total = total + weights[:, c : c + 128]
            values = v_ref[pl.ds(pl.multiple_of((j ^ mine) * block, block), block), :]
            return total, acc + dot(weights.astype(BF), values)

        total, acc = lax.fori_loop(
            0, row_block + 1, mix, (jnp.zeros((block, 128), F32), jnp.zeros((block, PAIR), F32))
        )
        total = jnp.sum(total, axis=1, keepdims=True)
        acc = acc / total
        mixed = acc if mixed is None else jnp.where(mask, acc, mixed)
        logs = jnp.broadcast_to(top + jnp.log(total), (block, 128))
        log_ref[head : head + 1, :] = jnp.transpose(logs)[0:1, :]
    out_ref[...] = mixed.astype(BF)


def attend_forward(place, qkv, pair, starts, block):
    pairs3, length, _ = qkv.shape
    pairs = pairs3 // 3
    blocks = length // block
    return pl.pallas_call(
        functools.partial(forward_kernel, block),
        out_shape=(
            jax.ShapeDtypeStruct((length, PAIR), BF),
            jax.ShapeDtypeStruct((8, length), F32),
        ),
        grid_spec=pltpu.PrefetchScalarGridSpec(
            num_scalar_prefetch=1,
            grid=(blocks,),
            in_specs=[
                pl.BlockSpec((None, block, PAIR), lambda d, place: (pair, d, 0)),
                pl.BlockSpec((None, length, PAIR), lambda d, place: (pairs + pair, 0, 0)),
                pl.BlockSpec((None, length, PAIR), lambda d, place: (2 * pairs + pair, 0, 0)),
                pl.BlockSpec((block, 1), lambda d, place: (d ^ place[0], 0)),
            ],
            out_specs=(
                pl.BlockSpec((block, PAIR), lambda d, place: (d, 0)),
                pl.BlockSpec((8, block), lambda d, place: (0, d)),
            ),
            scratch_shapes=[pltpu.VMEM((blocks, block, block), F32)],
        ),
        compiler_params=pltpu.CompilerParams(vmem_limit_bytes=40 << 20),
        cost_estimate=pl.CostEstimate(flops=20 * length * length * PAIR, bytes_accessed=4 * length * PAIR * 2, transcendentals=length * length),
        name="attend_forward",
    )(place, qkv, qkv, qkv, starts)


def backward_kernel(
    block, blocks, place_ref, q_ref, k_ref, v_ref, do_ref, o_ref, log_ref, start_ref, cos_ref, sin_ref, out_ref, dq_ref, inner_ref
):
    mine = place_ref[0]
    step = pl.program_id(0)
    key_block = step ^ mine
    heads = PAIR // HD

    @pl.when(step == 0)
    def _():
        dq_ref[...] = jnp.zeros_like(dq_ref)
        for b in range(blocks):
            rows = pl.ds(b * block, block)
            product = do_ref[rows, :].astype(F32) * o_ref[rows, :].astype(F32)
            high = product.astype(BF)
            low = (product - high.astype(F32)).astype(BF)
            for head in range(heads):
                ones = head_mask((16, PAIR), head).astype(F32).astype(BF)
                inner = dot(ones, high, NT) + dot(ones, low, NT)
                inner_ref[head : head + 1, rows] = inner[0:1, :]

    here = pl.ds(pl.multiple_of(step * block, block), block)
    keys = k_ref[here, :]
    values = v_ref[here, :]
    dk = jnp.zeros((block, PAIR), F32)
    dv = jnp.zeros((block, PAIR), F32)
    for head in range(heads):
        mask = head_mask(keys.shape, head)
        key = jnp.where(mask, keys * HD**-0.5, jnp.zeros_like(keys))
        value = jnp.where(mask, values, jnp.zeros_like(values))

        def one(i, carry, first):
            dk, dv = carry
            rows = pl.ds(pl.multiple_of((i ^ mine) * block, block), block)
            real = pl.ds(pl.multiple_of(i * block, block), block)
            query = q_ref[rows, :]
            grad = do_ref[rows, :]
            s = dot(key, query, NT)
            row = lax.broadcasted_iota(jnp.int32, s.shape, 0)
            visible = row >= start_ref[0:1, real] - key_block * block
            if first:
                visible &= row <= lax.broadcasted_iota(jnp.int32, s.shape, 1)
            probs = jnp.where(visible, jnp.exp(s - log_ref[head : head + 1, rows]), 0.0)
            grad_probs = dot(value, grad, NT)
            ds = (probs * (grad_probs - inner_ref[head : head + 1, rows])).astype(BF)
            zero = jnp.zeros_like(query)
            dv = dv + dot(probs.astype(BF), jnp.where(mask, grad, zero))
            dk = dk + dot(ds, jnp.where(mask, query, zero))
            dq_ref[rows, :] += dot(ds, key, TN)
            return dk, dv

        dk, dv = one(key_block, (dk, dv), True)
        dk, dv = lax.fori_loop(key_block + 1, blocks, lambda i, carry: one(i, carry, False), (dk, dv))
    real = pl.ds(pl.multiple_of(key_block * block, block), block)
    out_ref[1, here, :] = turn(dk * HD**-0.5, cos_ref[real, :], -sin_ref[real, :]).astype(BF)
    out_ref[2, here, :] = dv.astype(BF)

    @pl.when(step == blocks - 1)
    def _():
        for b in range(blocks):
            rows = pl.ds(b * block, block)
            real = pl.ds(pl.multiple_of((b ^ mine) * block, block), block)
            out_ref[0, rows, :] = turn(dq_ref[rows, :], cos_ref[real, :], -sin_ref[real, :]).astype(BF)


def attend_backward(place, qkv, pair, grad_heads, heads_out, logs, start_row, cosine, sine, block):
    pairs3, length, _ = qkv.shape
    pairs = pairs3 // 3
    blocks = length // block
    whole = lambda d, place: (0, 0)
    return pl.pallas_call(
        functools.partial(backward_kernel, block, blocks),
        out_shape=jax.ShapeDtypeStruct((3, length, PAIR), BF),
        grid_spec=pltpu.PrefetchScalarGridSpec(
            num_scalar_prefetch=1,
            grid=(blocks,),
            in_specs=[
                pl.BlockSpec((None, length, PAIR), lambda d, place: (pair, 0, 0)),
                pl.BlockSpec((None, length, PAIR), lambda d, place: (pairs + pair, 0, 0)),
                pl.BlockSpec((None, length, PAIR), lambda d, place: (2 * pairs + pair, 0, 0)),
                pl.BlockSpec((length, PAIR), whole),
                pl.BlockSpec((length, PAIR), whole),
                pl.BlockSpec((8, length), whole),
                pl.BlockSpec((1, length), whole),
                pl.BlockSpec((length, PAIR), whole),
                pl.BlockSpec((length, PAIR), whole),
            ],
            out_specs=pl.BlockSpec((3, length, PAIR), lambda d, place: (0, 0, 0)),
            scratch_shapes=[pltpu.VMEM((length, PAIR), F32), pltpu.VMEM((8, length), F32)],
        ),
        compiler_params=pltpu.CompilerParams(vmem_limit_bytes=40 << 20),
        cost_estimate=pl.CostEstimate(flops=50 * length * length * PAIR, bytes_accessed=8 * length * PAIR * 2, transcendentals=length * length),
        name="attend_backward",
    )(place, qkv, qkv, qkv, grad_heads, heads_out, logs, start_row, cosine, sine)


def body(block_in, lengths, qkv_weight, out_weight, up_weight, down_weight, norm_gain, norm_bias, cotangent):
    block, row_count, width = block_in.shape
    assert row_count == 1
    ranks = lax.axis_size("tensor")
    length = block * ranks
    local = out_weight.shape[0]
    pairs = local // PAIR
    mine = lax.axis_index("tensor")
    place = mine.astype(jnp.int32).reshape(1)

    residual_in = block_in.reshape(block, width).astype(F32)
    attn_norm, attn_norm_pull = jax.vjp(layer_norm, residual_in, norm_gain[0], norm_bias[0])
    attn_low = attn_norm.astype(BF)
    attn_parts = gather_tensor(attn_low)

    out_late, up_late, down_late, _ = lax.optimization_barrier((out_weight, up_weight, down_weight, attn_parts[ranks // 2]))
    up_parts = gather_tensor(up_late)
    out_parts = gather_tensor(out_late)
    down_parts = gather_tensor(down_late)

    finish = jnp.cumsum(lengths[0])
    begin = finish - lengths[0]
    places = jnp.arange(length, dtype=jnp.int32)
    segment = jnp.sum((places[:, None] >= finish[None, :]).astype(jnp.int32), axis=1)
    picked = segment[:, None] == jnp.arange(lengths.shape[1], dtype=jnp.int32)[None, :]
    starts = jnp.sum(jnp.where(picked, begin[None, :], 0), axis=1)
    position = (places - starts).astype(F32)
    lanes = jnp.arange(PAIR, dtype=jnp.int32)
    inverse = ROPE_BASE ** (-(lanes % (HD // 2)).astype(F32) * 2.0 / HD)
    angles = position[:, None] * inverse
    cosine = jnp.cos(angles)
    sine = jnp.sin(angles) * jnp.where(lanes % HD < HD // 2, -1.0, 1.0).astype(F32)
    start_column = starts.reshape(length, 1)
    start_row = starts.reshape(1, length)

    attn_full = jnp.concatenate(attn_parts, axis=0)
    qkv_swapped = jnp.transpose(qkv_weight, (1, 0, 2))
    qkv = project_qkv(place, attn_full, qkv_swapped, cosine, sine, block)

    heads_parts = [[] for _ in range(ranks)]
    heads_mixed, logs = [], []
    for pair in range(pairs):
        mixed, log_total = attend_forward(place, qkv, pair, start_column, block)
        heads_mixed.append(mixed)
        logs.append(log_total)
        for d in range(ranks):
            piece = mixed[d * block : (d + 1) * block]
            heads_parts[d].append(piece if d == 0 else swap(piece, "tensor", d))
    heads_local = jnp.concatenate([piece for parts in heads_parts for piece in parts], axis=1)

    out_full = jnp.concatenate(out_parts, axis=0)
    attn_proj = dot(heads_local, out_full)
    attn_branch, attn_branch_pull = jax.vjp(layer_norm, attn_proj, norm_gain[1], norm_bias[1])
    middle = residual_in + attn_branch
    mlp_norm, mlp_norm_pull = jax.vjp(layer_norm, middle, norm_gain[2], norm_bias[2])
    mlp_low = mlp_norm.astype(BF)
    mlp_parts = gather_tensor(mlp_low)

    upward = [dot(mlp_low, part) for part in up_parts]
    hidden, gelu_pull = jax.vjp(jax.nn.gelu, upward[0])
    pulls, mlp_proj = [], 0.0
    for d in range(ranks):
        hidden, pull = jax.vjp(jax.nn.gelu, upward[d])
        pulls.append(pull)
        mlp_proj = mlp_proj + dot(hidden.astype(BF), down_parts[d])
    mlp_branch, mlp_branch_pull = jax.vjp(layer_norm, mlp_proj, norm_gain[3], norm_bias[3])
    block_out = (middle + mlp_branch).astype(BF)

    grad_rows = cotangent.reshape(block, width).astype(F32)
    grad_mlp_proj, gain_three, shift_three = mlp_branch_pull(grad_rows)
    grad_mlp_low = grad_mlp_proj.astype(BF)
    grad_mlp_parts = gather_tensor(grad_mlp_low)
    grad_mlp_norm = 0.0
    for d in range(ranks):
        grad_hidden = dot(grad_mlp_low, down_parts[d], NT)
        grad_upward = pulls[d](grad_hidden)[0].astype(BF)
        grad_mlp_norm = grad_mlp_norm + dot(grad_upward, up_parts[d], NT)
    grad_from_norm, gain_two, shift_two = mlp_norm_pull(grad_mlp_norm)
    grad_middle = grad_rows + grad_from_norm
    grad_attn_proj, gain_one, shift_one = attn_branch_pull(grad_middle)
    grad_attn_low = grad_attn_proj.astype(BF)
    grad_heads = dot(grad_attn_low, out_full, NT).astype(BF)

    mlp_full = jnp.concatenate(mlp_parts, axis=0)
    grad_mlp_full = jnp.concatenate(grad_mlp_parts, axis=0)
    upward_own = dot(mlp_full, up_weight)
    hidden_own, gelu_own_pull = jax.vjp(jax.nn.gelu, upward_own)
    grad_hidden_own = dot(grad_mlp_full, down_weight, NT)
    grad_upward_own = gelu_own_pull(grad_hidden_own)[0].astype(BF)
    down_grad = reduce_dp(dot(hidden_own.astype(BF), grad_mlp_full, TN), False)
    up_grad = reduce_dp(dot(mlp_full, grad_upward_own, TN), False)

    out_partial = dot(heads_local, grad_attn_low, TN)
    out_terms = [out_partial[d * local : (d + 1) * local] for d in range(ranks)]
    out_grad = reduce_dp(reduce_scatter_tensor(out_terms), False)

    grad_project, qkv_grads = [], []
    for pair in range(pairs):
        parts = []
        for d in range(ranks):
            column = d * local + pair * PAIR
            piece = grad_heads[:, column : column + PAIR]
            parts.append(piece if d == 0 else swap(piece, "tensor", d))
        got = jnp.concatenate(parts, axis=0)
        grads = attend_backward(place, qkv, pair, got, heads_mixed[pair], logs[pair], start_row, cosine, sine, block)
        grad_project += [grads[c] for c in range(3)]
        wide = jnp.concatenate([grads[c] for c in range(3)], axis=1)
        qkv_grads.append(reduce_dp(dot(attn_full, wide, TN), pair == pairs - 1))
    order = [pair * 3 + c for c in range(3) for pair in range(pairs)]
    grad_wide = jnp.concatenate([grad_project[i] for i in order], axis=1)
    qkv_flat = qkv_weight.reshape(width, 3 * local)
    terms = [
        dot(grad_wide[d * block : (d + 1) * block], qkv_flat, NT) for d in range(ranks)
    ]
    grad_attn_norm = reduce_scatter_tensor(terms)
    grad_from_first, gain_zero, shift_zero = attn_norm_pull(grad_attn_norm)
    input_grad = grad_middle + grad_from_first

    late = sum_all(jnp.stack([gain_zero, shift_zero]))
    early = sum_all(jnp.stack([gain_one, gain_two, gain_three, shift_one, shift_two, shift_three]))
    gain_grad = jnp.concatenate([late[0:1], early[0:3]], axis=0)
    bias_grad = jnp.concatenate([late[1:2], early[3:6]], axis=0)
    qkv_grad = jnp.stack(
        [jnp.concatenate([g[:, c * PAIR : (c + 1) * PAIR] for g in qkv_grads], axis=1) for c in range(3)], axis=1
    )
    return (
        block_out.reshape(block_in.shape),
        input_grad.reshape(block_in.shape),
        qkv_grad,
        out_grad,
        up_grad,
        down_grad,
        gain_grad,
        bias_grad,
    )


def solution(mesh):
    tokens, rows, columns, copied = P("tensor", "dp", None), P("tensor", None), P(None, "tensor"), P()
    heads = P(None, None, "tensor")
    return jax.shard_map(
        body,
        mesh=mesh,
        in_specs=(tokens, P("dp", None), heads, rows, columns, rows, copied, copied, tokens),
        out_specs=(tokens, tokens, heads, rows, columns, rows, copied, copied),
        check_vma=False,
    )
```

time: 1260 us -> 639 us (0.51)
  waiting for transfers between devices: 716 us -> 263 us
  matrix products: 253 us -> 103 us
  starting transfers between devices: 0.37 us -> 110 us
  Pallas kernels: 0 us -> 85.2 us
  local copies, waits for them, and re-layouts: 96.1 us -> 18.6 us
  other arithmetic: 115 us -> 46.4 us
  blocking collectives: 45.8 us -> 0 us
    psum x1 -> x0, waiting for transfers between devices: 352 us -> none  [body(): lax.psum((qkv_grad, out_grad, up_grad, down_grad), 'dp')]
    ppermute x0 -> x102, waiting for transfers between devices: none -> 263 us  [swap(): return lax.ppermute(value, axis, [(i, i ^ offset) for i in range(size)])]
    reduce_scatter x4 -> x0, waiting for transfers between devices: 230 us -> none  [the longest x1 71.8 us: body(): lax.psum_scatter(jnp.einsum('srf,df->srd', grad_upward, up_weight, prefer...]
    dot_general x40 -> x24, matrix products: 253 us -> 103 us  [dot(): return lax.dot_general(a, b, dims, preferred_element_type=F32)]
    all_gather x4 -> x0, waiting for transfers between devices: 134 us -> none  [the longest x1 34.6 us: body(): lax.all_gather(grad_mlp_proj.astype(jnp.bfloat16), 'tensor', axis=0, tile...]
    ppermute x0 -> x102, starting transfers between devices: none -> 110 us  [swap(): return lax.ppermute(value, axis, [(i, i ^ offset) for i in range(size)])]
    pallas_call x0 -> x5, Pallas kernels: none -> 85.2 us  [the longest x2 46.2 us: attend_backward(): pl.pallas_call(functools.partial(backward_kernel, block, blocks), out_sha...]
    dynamic_update_slice x8 -> x0, local copies, waits for them, and re-layouts: 46.5 us -> none  [attend_forward(): lax.map(one_block, (queries.reshape(blocks, block_rows, row_count, head_c...]
  transfers between devices with their start and end apart: 9 -> 102, of which waited for: 9 -> 41; matrix products, arithmetic and copies ran while one was open for 3% -> 17% of each run, Pallas kernels for 0% -> 10%
where the time goes in v1:
time: 639 us; the launch traced here: 630 us
  waiting for transfers between devices  263 us (41%)
  starting transfers between devices  110 us (17%)
  matrix products  103 us (16%)
  Pallas kernels  85.2 us (13%)
  other arithmetic  46.4 us (7%)
  local copies, waits for them, and re-layouts  18.6 us (3%)
    ppermute x102, waiting for transfers between devices, swap(): return lax.ppermute(value, axis, [(i, i ^ offset) for i in range(size)])  263 us
    ppermute x102, starting transfers between devices, swap(): return lax.ppermute(value, axis, [(i, i ^ offset) for i in range(size)])  110 us
    dot_general x24, matrix products, dot(): return lax.dot_general(a, b, dims, preferred_element_type=F32)  103 us
    pallas_call x2, Pallas kernels, attend_backward(): pl.pallas_call(functools.partial(backward_kernel, block, blocks), out_sha...  46.2 us
    pallas_call x2, Pallas kernels, attend_forward(): pl.pallas_call(functools.partial(forward_kernel, block), out_shape=(jax.S...  34 us
    unnamed x123, local copies, waits for them, and re-layouts  13 us
  transfers between devices with their start and end apart: 102, of which 41 were waited for; matrix products, arithmetic and copies ran while one was open for 17% of the time, Pallas kernels for 10%

profile of v1, /device:TPU:20, one launch (start us, length us, event | category | flops | bytes accessed | tf_op | source)
XLA Modules:
  0.0 629.5 jit_solution(9505193859532977788)
XLA Ops:
  8.0 24.3 %collective-permute-done.1 = bf16[512,1024]{1,0:T(8,128)(2,1)} collective-permute-done((bf16[512,1024]{1,0:T(8,128)(2,1)}, bf16[512,1024]{1,0:T(8,128)(2,1)}, u32[]{:S(2)}, u32[]{:S(2)}) %collective-permute-start.1) | collective-permute-done | bytes 1048608 | tf_op jit(solution)/shard_map/ppermute | solution.py:34
  33.4 5.6 fusion.70
  45.4 2.3 collective-permute-done.10
  49.0 2.6 pad_maximum_fusion.x_ref
  51.7 5.1 project_qkv.1.q_ref.k_ref.v_ref
  56.8 16.9 %attend_forward.3 = (bf16[2048,128]{1,0:T(8,128)(2,1)S(1)}, f32[8,2048]{1,0:T(8,128)S(1)}) custom-call(s32[1]{0:T(128)} %bitcast.1.place_ref, bf16[6,2048,128]{2,1,0:T(8,128)(2,1)S(1)} %project_qkv.1.q_ref.k_ref.v_ref, bf16[6,2048,128]{2,1,0:T(8,128)(2,1)S(1)} %project_qkv.1.q_ref.k_ref.v_ref, bf16[6,2048,128]{2,1,0:T(8,128)(2,1)S(1)} %project_qkv.1.q_ref.k_ref.v_ref, ...), custom_call_target="tpu_custom_call" | custom-call | flops 10737418240 | bytes 2097152 | tf_op jit(solution)/shard_map/attend_forward/pallas_call | solution.py:217
  73.7 17.1 %attend_forward.2 = (bf16[2048,128]{1,0:T(8,128)(2,1)S(1)}, f32[8,2048]{1,0:T(8,128)S(1)}) custom-call(s32[1]{0:T(128)} %bitcast.1.place_ref, bf16[6,2048,128]{2,1,0:T(8,128)(2,1)S(1)} %project_qkv.1.q_ref.k_ref.v_ref, bf16[6,2048,128]{2,1,0:T(8,128)(2,1)S(1)} %project_qkv.1.q_ref.k_ref.v_ref, bf16[6,2048,128]{2,1,0:T(8,128)(2,1)S(1)} %project_qkv.1.q_ref.k_ref.v_ref, ...), custom_call_target="tpu_custom_call" | custom-call | flops 10737418240 | bytes 2097152 | tf_op jit(solution)/shard_map/attend_forward/pallas_call | solution.py:217
  94.8 45.6 %collective-permute-done.5 = bf16[512,128]{1,0:T(8,128)(2,1)S(1)} collective-permute-done((bf16[512,128]{1,0:T(8,128)(2,1)S(1)}, bf16[512,128]{1,0:T(8,128)(2,1)S(1)}, u32[]{:S(2)}, u32[]{:S(2)}) %collective-permute-start.5) | collective-permute-done | bytes 131104 | tf_op jit(solution)/shard_map/ppermute | solution.py:34
  142.3 3.1 collective-permute-done.7
  145.5 2.4 collective-permute-done.8
  158.8 18.9 %collective-permute-done.61 = bf16[512,1024]{1,0:T(8,128)(2,1)S(1)} collective-permute-done((bf16[512,1024]{1,0:T(8,128)(2,1)S(1)}, bf16[512,1024]{1,0:T(8,128)(2,1)S(1)}, u32[]{:S(2)}, u32[]{:S(2)}) %collective-permute-start.61) | collective-permute-done | bytes 1048608 | tf_op jit(solution)/shard_map/ppermute | solution.py:34
  183.1 11.0 %fusion.115 = f32[2048,1024]{1,0:T(8,128)} fusion(bf16[1024,1024]{1,0:T(8,128)(2,1)S(1)} %copy-done.37, bf16[512,1024]{1,0:T(8,128)(2,1)S(1)} %collective-permute-done.62, bf16[512,1024]{1,0:T(8,128)(2,1)S(1)} %collective-permute-done.61, bf16[512,1024]{1,0:T(8,128)(2,1)S(1)} %collective-permute-done.60, bf16[512,1024]{1,0:T(8,128)(2,1)S(1)} %add_convert_fusion.6), kind=kOutput, calls=%fused_computation.176 | convolution fusion | flops 4311744512 | bytes 14680064 | tf_op jit(solution)/shard_map/dot_general | solution.py:23
  202.6 7.4 %fusion.104 = f32[512,1024]{1,0:T(8,128)} fusion(bf16[1024,1024]{1,0:T(8,128)(2,1)} %param.13, f32[512,1024]{1,0:T(8,128)} %copy-done.51, bf16[512,1024]{1,0:T(8,128)(2,1)} %add_convert_fusion.4, bf16[1024,1024]{1,0:T(8,128)(2,1)} %param.14), kind=kOutput, calls=%fused_computation.165 | convolution fusion | flops 2157969408 | bytes 9437184 | tf_op jit(solution)/shard_map/dot_general | solution.py:23
  210.0 7.4 %fusion.100 = f32[512,1024]{1,0:T(8,128)} fusion(bf16[1024,1024]{1,0:T(8,128)(2,1)} %copy-done.41, f32[512,1024]{1,0:T(8,128)} %copy-done.52, bf16[512,1024]{1,0:T(8,128)(2,1)} %add_convert_fusion.4, bf16[1024,1024]{1,0:T(8,128)(2,1)} %copy-done.39), kind=kOutput, calls=%fused_computation.163 | convolution fusion | flops 2157969408 | bytes 9437184 | tf_op jit(solution)/shard_map/dot_general | solution.py:23
  217.4 7.8 %fusion.102 = f32[512,1024]{1,0:T(8,128)} fusion(bf16[1024,1024]{1,0:T(8,128)(2,1)} %copy-done.42, f32[512,1024]{1,0:T(8,128)} %copy-done.53, bf16[512,1024]{1,0:T(8,128)(2,1)} %add_convert_fusion.4, bf16[1024,1024]{1,0:T(8,128)(2,1)} %copy-done.40), kind=kOutput, calls=%fused_computation.164 | convolution fusion | flops 2157969408 | bytes 9437184 | tf_op jit(solution)/shard_map/dot_general | solution.py:23
  225.2 9.8 %multiply_reduce_fusion = (f32[1024]{0:T(1024)S(1)}, f32[512]{0:T(512)S(1)}, f32[1024]{0:T(1024)S(1)}, f32[512,1024]{1,0:T(8,128)}) fusion(f32[512,1024]{1,0:T(8,128)S(1)} %get-tuple-element.77, f32[512]{0:T(512)S(1)} %fusion.118, f32[512]{0:T(512)S(1)} %broadcast_multiply_fusion.1, f32[1024]{0:T(1024)S(1)} %bitcast.174, bf16[1024,1024]{1,0:T(8,128)(2,1)} %copy-done.43, ...), kind=kOutput, calls=%fused_computation.82 | convolution fusion | flops 2163734016 | bytes 17844224 | tf_op jit(solution)/shard_map/dot_general | solution.py:23
  235.1 2.5 fusion.185
  237.6 2.4 multiply_reduce_fusion.1
  242.2 2.4 fusion.183
  248.2 2.5 collective-permute-start.101
  250.7 2.2 collective-permute-start.98
  253.7 3.4 collective-permute-start.96
  264.7 2.9 collective-permute-done.19
  267.7 23.2 %attend_backward.2 = bf16[3,2048,128]{2,1,0:T(8,128)(2,1)S(1)} custom-call(s32[1]{0:T(128)} %bitcast.1.place_ref, bf16[6,2048,128]{2,1,0:T(8,128)(2,1)S(1)} %copy-done.6, bf16[6,2048,128]{2,1,0:T(8,128)(2,1)S(1)} %copy-done.6, bf16[6,2048,128]{2,1,0:T(8,128)(2,1)S(1)} %copy-done.6, bf16[2048,128]{1,0:T(8,128)(2,1)S(1)} %pad_maximum_fusion.14.do_ref, ...), custom_call_target="tpu_custom_call" | custom-call | flops 26843545600 | bytes 4194304 | tf_op jit(solution)/shard_map/attend_backward/pallas_call | solution.py:314
  291.2 23.0 %attend_backward.3 = bf16[3,2048,128]{2,1,0:T(8,128)(2,1)S(1)} custom-call(s32[1]{0:T(128)} %bitcast.1.place_ref, bf16[6,2048,128]{2,1,0:T(8,128)(2,1)S(1)} %copy-done.6, bf16[6,2048,128]{2,1,0:T(8,128)(2,1)S(1)} %copy-done.6, bf16[6,2048,128]{2,1,0:T(8,128)(2,1)S(1)} %copy-done.6, bf16[2048,128]{1,0:T(8,128)(2,1)S(1)} %pad_maximum_fusion.15.do_ref, ...), custom_call_target="tpu_custom_call" | custom-call | flops 26843545600 | bytes 4194304 | tf_op jit(solution)/shard_map/attend_backward/pallas_call | solution.py:314
  315.0 4.1 fusion.64
  322.1 3.0 collective-permute-start.39
  325.1 4.6 collective-permute-start.37
  329.7 4.6 fusion.58
  341.7 2.6 collective-permute-start.46
  352.5 6.3 collective-permute-done.44
  362.4 3.1 collective-permute-done.42
  366.4 5.6 collective-permute-done.27
  373.0 3.9 collective-permute-start.29
  378.6 3.3 collective-permute-done.30
  383.1 4.0 collective-permute-start.32
  387.3 4.1 collective-permute-start.64
  395.2 9.6 %collective-permute-done.34 = bf16[512,384]{1,0:T(8,128)(2,1)S(1)} collective-permute-done((bf16[512,384]{1,0:T(8,128)(2,1)S(1)}, bf16[512,384]{1,0:T(8,128)(2,1)S(1)}, u32[]{:S(2)}, u32[]{:S(2)}) %collective-permute-start.34) | collective-permute-done | bytes 393248 | tf_op jit(solution)/shard_map/ppermute | solution.py:34
  405.3 4.4 collective-permute-done.52
  411.6 3.1 collective-permute-start.54
  414.8 3.7 collective-permute-done.54
  419.9 3.3 collective-permute-start.57
  431.3 4.7 collective-permute-done.59
  438.2 20.3 %fusion.8 = f32[1024,1024]{1,0:T(8,128)} fusion(f32[2048,1024]{1,0:T(8,128)} %fusion.115, bf16[1024,1024]{1,0:T(8,128)(2,1)} %param.14, bf16[512,1024]{1,0:T(8,128)(2,1)} %collective-permute-done.65, bf16[512,1024]{1,0:T(8,128)(2,1)} %copy-done.47, bf16[512,1024]{1,0:T(8,128)(2,1)} %copy-done.49, bf16[512,1024]{1,0:T(8,128)(2,1)} %add_convert_fusion.4, ...), kind=kOutput, calls=%fused_computation.14 | convolution fusion | flops 8665432064 | bytes 23068672 | tf_op jit(solution)/shard_map/dot_general | solution.py:23
  461.1 9.6 %fusion.7 = f32[1024,1024]{1,0:T(8,128)S(1)} fusion(f32[2048,1024]{1,0:T(8,128)} %fusion.115, bf16[512,1024]{1,0:T(8,128)(2,1)} %collective-permute-done.65, bf16[512,1024]{1,0:T(8,128)(2,1)S(1)} %copy-done.48, bf16[512,1024]{1,0:T(8,128)(2,1)} %copy-done.49, bf16[512,1024]{1,0:T(8,128)(2,1)S(1)} %copy-done.25), kind=kOutput, calls=%fused_computation.13 | convolution fusion | flops 4330618880 | bytes 16777216 | tf_op jit(solution)/shard_map/dot_general | solution.py:23
  472.5 2.5 fusion.28
  477.5 9.1 %collective-permute-done.66 = bf16[512,1024]{1,0:T(8,128)(2,1)S(1)} collective-permute-done((bf16[512,1024]{1,0:T(8,128)(2,1)S(1)}, bf16[512,1024]{1,0:T(8,128)(2,1)S(1)}, u32[]{:S(2)}, u32[]{:S(2)}) %collective-permute-start.66) | collective-permute-done | bytes 1048608 | tf_op jit(solution)/shard_map/ppermute | solution.py:34
  488.1 3.5 collective-permute-start.68
  491.6 16.0 %collective-permute-done.74 = bf16[512,1024]{1,0:T(8,128)(2,1)S(1)} collective-permute-done((bf16[512,1024]{1,0:T(8,128)(2,1)S(1)}, bf16[512,1024]{1,0:T(8,128)(2,1)S(1)}, u32[]{:S(2)}, u32[]{:S(2)}) %collective-permute-start.74) | collective-permute-done | bytes 1048608 | tf_op jit(solution)/shard_map/ppermute | solution.py:34
  509.8 3.5 copy.25
  514.6 4.0 collective-permute-start.76
  519.8 3.5 collective-permute-start.71
  523.2 4.4 collective-permute-done.77
  527.7 15.4 %collective-permute-done.76 = bf16[128,1024]{1,0:T(8,128)(2,1)S(1)} collective-permute-done((bf16[128,1024]{1,0:T(8,128)(2,1)S(1)}, bf16[128,1024]{1,0:T(8,128)(2,1)S(1)}, u32[]{:S(2)}, u32[]{:S(2)}) %collective-permute-start.76) | collective-permute-done | bytes 262176 | tf_op jit(solution)/shard_map/ppermute | solution.py:34
  544.8 8.5 %collective-permute-done.70 = bf16[128,1024]{1,0:T(8,128)(2,1)S(1)} collective-permute-done((bf16[128,1024]{1,0:T(8,128)(2,1)S(1)}, bf16[128,1024]{1,0:T(8,128)(2,1)S(1)}, u32[]{:S(2)}, u32[]{:S(2)}) %collective-permute-start.70) | collective-permute-done | bytes 262176 | tf_op jit(solution)/shard_map/ppermute | solution.py:34
  554.4 5.9 collective-permute-done.71
  560.3 3.4 collective-permute-start.79
  563.9 9.5 %collective-permute-done.78 = bf16[128,1024]{1,0:T(8,128)(2,1)S(1)} collective-permute-done((bf16[128,1024]{1,0:T(8,128)(2,1)S(1)}, bf16[128,1024]{1,0:T(8,128)(2,1)S(1)}, u32[]{:S(2)}, u32[]{:S(2)}) %collective-permute-start.78) | collective-permute-done | bytes 262176 | tf_op jit(solution)/shard_map/ppermute | solution.py:34
  573.4 3.2 collective-permute-done.79
  576.6 3.1 collective-permute-start.89
  586.2 19.9 %collective-permute-done.85 = f32[2,1024]{1,0:T(2,128)S(1)} collective-permute-done((f32[2,1024]{1,0:T(2,128)S(1)}, f32[2,1024]{1,0:T(2,128)S(1)}, u32[]{:S(2)}, u32[]{:S(2)}) %collective-permute-start.85) | collective-permute-done | bytes 8224 | tf_op jit(solution)/shard_map/ppermute | solution.py:34
  608.0 2.4 maximum_convert_fusion
  610.4 15.8 %collective-permute-done.81 = bf16[512,1024]{1,0:T(8,128)(2,1)S(1)} collective-permute-done((bf16[512,1024]{1,0:T(8,128)(2,1)S(1)}, bf16[512,1024]{1,0:T(8,128)(2,1)S(1)}, u32[]{:S(2)}, u32[]{:S(2)}) %collective-permute-start.81) | collective-permute-done | bytes 1048608 | tf_op jit(solution)/shard_map/ppermute | solution.py:34
  626.9 2.4 maximum_convert_fusion.1
  (408 shorter events, 131.3 us)
Async XLA Ops:
  7.1 25.2 %collective-permute-start.1 = (bf16[512,1024]{1,0:T(8,128)(2,1)}, bf16[512,1024]{1,0:T(8,128)(2,1)}, u32[]{:S(2)}, u32[]{:S(2)}) collective-permute-start(bf16[512,1024]{1,0:T(8,128)(2,1)} %fusion.24), channel_id=1, source_target_pairs={{0,2},{1,3},{2,0},{3,1},{4,6},{5,7},{6,4},{7,5},{8,10},{9,11},{10,... | collective-permute-start | bytes 3145736 | tf_op jit(solution)/shard_map/ppermute | solution.py:34
  7.6 41.3 %collective-permute-start = (bf16[512,1024]{1,0:T(8,128)(2,1)}, bf16[512,1024]{1,0:T(8,128)(2,1)}, u32[]{:S(2)}, u32[]{:S(2)}) collective-permute-start(bf16[512,1024]{1,0:T(8,128)(2,1)} %fusion.24), channel_id=1, source_target_pairs={{0,1},{1,0},{2,3},{3,2},{4,5},{5,4},{6,7},{7,6},{8,9},{9,8},{10,11... | collective-permute-start | bytes 3145736 | tf_op jit(solution)/shard_map/ppermute | solution.py:34
  32.3 16.7 %collective-permute-start.2 = (bf16[512,1024]{1,0:T(8,128)(2,1)}, bf16[512,1024]{1,0:T(8,128)(2,1)}, u32[]{:S(2)}, u32[]{:S(2)}) collective-permute-start(bf16[512,1024]{1,0:T(8,128)(2,1)} %collective-permute-done.1), channel_id=1, source_target_pairs={{0,1},{1,0},{2,3},{3,2},{4,5},{5,4},{6,7},{7,6},{8,9},{9,8},{10,11... | collective-permute-start | bytes 3145736 | tf_op jit(solution)/shard_map/ppermute | solution.py:34
  32.3 12.0 %collective-permute-start.9 = (bf16[256,1024]{1,0:T(8,128)(2,1)S(1)}, bf16[256,1024]{1,0:T(8,128)(2,1)}, u32[]{:S(2)}, u32[]{:S(2)}) collective-permute-start(bf16[256,1024]{1,0:T(8,128)(2,1)S(1)} %copy-done.26), channel_id=1, source_target_pairs={{0,1},{1,0},{2,3},{3,2},{4,5},{5,4},{6,7},{7,6},{8,9},{9,8},{10,11... | collective-permute-start | bytes 1572872 | tf_op jit(solution)/shard_map/ppermute | solution.py:34
  32.9 14.9 %collective-permute-start.10 = (bf16[256,1024]{1,0:T(8,128)(2,1)S(1)}, bf16[256,1024]{1,0:T(8,128)(2,1)}, u32[]{:S(2)}, u32[]{:S(2)}) collective-permute-start(bf16[256,1024]{1,0:T(8,128)(2,1)S(1)} %copy-done.26), channel_id=1, source_target_pairs={{0,2},{1,3},{2,0},{3,1},{4,6},{5,7},{6,4},{7,5},{8,10},{9,11},{10,... | collective-permute-start | bytes 1572872 | tf_op jit(solution)/shard_map/ppermute | solution.py:34
  42.6 115.6 %collective-permute-start.15 = (bf16[1024,1024]{1,0:T(8,128)(2,1)}, bf16[1024,1024]{1,0:T(8,128)(2,1)S(1)}, u32[]{:S(2)}, u32[]{:S(2)}) collective-permute-start(bf16[1024,1024]{1,0:T(8,128)(2,1)} %param.14), channel_id=1, source_target_pairs={{0,2},{1,3},{2,0},{3,1},{4,6},{5,7},{6,4},{7,5},{8,10},{9,11},{10,... | collective-permute-start | bytes 6291464 | tf_op jit(solution)/shard_map/ppermute | solution.py:34
  44.3 136.8 %collective-permute-start.13 = (bf16[1024,1024]{1,0:T(8,128)(2,1)}, bf16[1024,1024]{1,0:T(8,128)(2,1)S(1)}, u32[]{:S(2)}, u32[]{:S(2)}) collective-permute-start(bf16[1024,1024]{1,0:T(8,128)(2,1)} %param.14), channel_id=1, source_target_pairs={{0,1},{1,0},{2,3},{3,2},{4,5},{5,4},{6,7},{7,6},{8,9},{9,8},{10,11... | collective-permute-start | bytes 6291464 | tf_op jit(solution)/shard_map/ppermute | solution.py:34
  47.8 109.1 %collective-permute-start.14 = (bf16[1024,1024]{1,0:T(8,128)(2,1)S(1)}, bf16[1024,1024]{1,0:T(8,128)(2,1)S(1)}, u32[]{:S(2)}, u32[]{:S(2)}) collective-permute-start(bf16[1024,1024]{1,0:T(8,128)(2,1)S(1)} %copy-done.37), channel_id=1, source_target_pairs={{0,2},{1,3},{2,0},{3,1},{4,6},{5,7},{6,4},{7,5},{8,10},{9,11},{10,... | collective-permute-start | bytes 6291464 | tf_op jit(solution)/shard_map/ppermute | solution.py:34
  48.9 42.4 %collective-permute-start.11 = (bf16[256,1024]{1,0:T(8,128)(2,1)}, bf16[256,1024]{1,0:T(8,128)(2,1)S(1)}, u32[]{:S(2)}, u32[]{:S(2)}) collective-permute-start(bf16[256,1024]{1,0:T(8,128)(2,1)} %collective-permute-done.10), channel_id=1, source_target_pairs={{0,1},{1,0},{2,3},{3,2},{4,5},{5,4},{6,7},{7,6},{8,9},{9,8},{10,11... | collective-permute-start | bytes 1572872 | tf_op jit(solution)/shard_map/ppermute | solution.py:34
  92.2 48.1 %collective-permute-start.5 = (bf16[512,128]{1,0:T(8,128)(2,1)S(1)}, bf16[512,128]{1,0:T(8,128)(2,1)S(1)}, u32[]{:S(2)}, u32[]{:S(2)}) collective-permute-start(bf16[512,128]{1,0:T(8,128)(2,1)S(1)} %get-tuple-element.135), channel_id=1, source_target_pairs={{0,2},{1,3},{2,0},{3,1},{4,6},{5,7},{6,4},{7,5},{8,10},{9,11},{10,... | collective-permute-start | bytes 393224 | tf_op jit(solution)/shard_map/ppermute | solution.py:34
  94.3 48.0 %collective-permute-start.6 = (bf16[512,128]{1,0:T(8,128)(2,1)S(1)}, bf16[512,128]{1,0:T(8,128)(2,1)S(1)}, u32[]{:S(2)}, u32[]{:S(2)}) collective-permute-start(bf16[512,128]{1,0:T(8,128)(2,1)S(1)} %get-tuple-element.131), channel_id=1, source_target_pairs={{0,2},{1,3},{2,0},{3,1},{4,6},{5,7},{6,4},{7,5},{8,10},{9,11},{10,... | collective-permute-start | bytes 393224 | tf_op jit(solution)/shard_map/ppermute | solution.py:34
  145.4 33.8 %collective-permute-start.12 = (bf16[1024,1024]{1,0:T(8,128)(2,1)S(1)}, bf16[1024,1024]{1,0:T(8,128)(2,1)S(1)}, u32[]{:S(2)}, u32[]{:S(2)}) collective-permute-start(bf16[1024,1024]{1,0:T(8,128)(2,1)S(1)} %copy-done.37), channel_id=1, source_target_pairs={{0,1},{1,0},{2,3},{3,2},{4,5},{5,4},{6,7},{7,6},{8,9},{9,8},{10,11... | collective-permute-start | bytes 6291464 | tf_op jit(solution)/shard_map/ppermute | solution.py:34
  152.9 24.9 %collective-permute-start.61 = (bf16[512,1024]{1,0:T(8,128)(2,1)S(1)}, bf16[512,1024]{1,0:T(8,128)(2,1)S(1)}, u32[]{:S(2)}, u32[]{:S(2)}) collective-permute-start(bf16[512,1024]{1,0:T(8,128)(2,1)S(1)} %add_convert_fusion.6), channel_id=1, source_target_pairs={{0,2},{1,3},{2,0},{3,1},{4,6},{5,7},{6,4},{7,5},{8,10},{9,11},{10,... | collective-permute-start | bytes 3145736 | tf_op jit(solution)/shard_map/ppermute | solution.py:34
  156.8 26.2 %collective-permute-start.60 = (bf16[512,1024]{1,0:T(8,128)(2,1)S(1)}, bf16[512,1024]{1,0:T(8,128)(2,1)S(1)}, u32[]{:S(2)}, u32[]{:S(2)}) collective-permute-start(bf16[512,1024]{1,0:T(8,128)(2,1)S(1)} %add_convert_fusion.6), channel_id=1, source_target_pairs={{0,1},{1,0},{2,3},{3,2},{4,5},{5,4},{6,7},{7,6},{8,9},{9,8},{10,11... | collective-permute-start | bytes 3145736 | tf_op jit(solution)/shard_map/ppermute | solution.py:34
  158.2 35.8 %collective-permute-start.16 = (bf16[1024,1024]{1,0:T(8,128)(2,1)S(1)}, bf16[1024,1024]{1,0:T(8,128)(2,1)S(1)}, u32[]{:S(2)}, u32[]{:S(2)}) collective-permute-start(bf16[1024,1024]{1,0:T(8,128)(2,1)S(1)} %collective-permute-done.14), channel_id=1, source_target_pairs={{0,1},{1,0},{2,3},{3,2},{4,5},{5,4},{6,7},{7,6},{8,9},{9,8},{10,11... | collective-permute-start | bytes 6291464 | tf_op jit(solution)/shard_map/ppermute | solution.py:34
  179.2 16.2 %collective-permute-start.17 = (bf16[1024,1024]{1,0:T(8,128)(2,1)S(1)}, bf16[1024,1024]{1,0:T(8,128)(2,1)S(1)}, u32[]{:S(2)}, u32[]{:S(2)}) collective-permute-start(bf16[1024,1024]{1,0:T(8,128)(2,1)S(1)} %collective-permute-done.15), channel_id=1, source_target_pairs={{0,1},{1,0},{2,3},{3,2},{4,5},{5,4},{6,7},{7,6},{8,9},{9,8},{10,11... | collective-permute-start | bytes 6291464 | tf_op jit(solution)/shard_map/ppermute | solution.py:34
  247.6 9.5 %collective-permute-start.100 = (f32[6,1024]{1,0:T(8,128)S(1)}, f32[6,1024]{1,0:T(8,128)S(1)}, u32[]{:S(2)}, u32[]{:S(2)}) collective-permute-start(f32[6,1024]{1,0:T(8,128)S(1)} %add_add_fusion.7), channel_id=1, source_target_pairs={{0,24},{4,28},{8,16},{12,20},{16,8},{20,12},{24,0},{28,4},{1,25},{... | collective-permute-start | bytes 73736 | tf_op jit(solution)/shard_map/ppermute | solution.py:34
  248.2 9.9 %collective-permute-start.101 = (f32[6,1024]{1,0:T(8,128)S(1)}, f32[6,1024]{1,0:T(8,128)S(1)}, u32[]{:S(2)}, u32[]{:S(2)}) collective-permute-start(f32[6,1024]{1,0:T(8,128)S(1)} %add_add_fusion.7), channel_id=1, source_target_pairs={{0,28},{4,24},{8,20},{12,16},{16,12},{20,8},{24,4},{28,0},{1,29},{... | collective-permute-start | bytes 73736 | tf_op jit(solution)/shard_map/ppermute | solution.py:34
  261.9 29.1 %collective-permute-start.23 = (bf16[512,128]{1,0:T(8,128)(2,1)S(1)}, bf16[512,128]{1,0:T(8,128)(2,1)S(1)}, u32[]{:S(2)}, u32[]{:S(2)}) collective-permute-start(bf16[512,128]{1,0:T(8,128)(2,1)S(1)} %get-tuple-element.116), channel_id=1, source_target_pairs={{0,3},{1,2},{2,1},{3,0},{4,7},{5,6},{6,5},{7,4},{8,11},{9,10},{10,... | collective-permute-start | bytes 393224 | tf_op jit(solution)/shard_map/ppermute | solution.py:34
  262.3 28.8 %collective-permute-start.22 = (bf16[512,128]{1,0:T(8,128)(2,1)S(1)}, bf16[512,128]{1,0:T(8,128)(2,1)S(1)}, u32[]{:S(2)}, u32[]{:S(2)}) collective-permute-start(bf16[512,128]{1,0:T(8,128)(2,1)S(1)} %get-tuple-element.117), channel_id=1, source_target_pairs={{0,2},{1,3},{2,0},{3,1},{4,6},{5,7},{6,4},{7,5},{8,10},{9,11},{10,... | collective-permute-start | bytes 393224 | tf_op jit(solution)/shard_map/ppermute | solution.py:34
  264.6 26.5 %collective-permute-start.21 = (bf16[512,128]{1,0:T(8,128)(2,1)S(1)}, bf16[512,128]{1,0:T(8,128)(2,1)S(1)}, u32[]{:S(2)}, u32[]{:S(2)}) collective-permute-start(bf16[512,128]{1,0:T(8,128)(2,1)S(1)} %get-tuple-element.118), channel_id=1, source_target_pairs={{0,1},{1,0},{2,3},{3,2},{4,5},{5,4},{6,7},{7,6},{8,9},{9,8},{10,11... | collective-permute-start | bytes 393224 | tf_op jit(solution)/shard_map/ppermute | solution.py:34
  319.2 16.2 %collective-permute-start.41 = (bf16[128,384]{1,0:T(8,128)(2,1)S(1)}, bf16[128,384]{1,0:T(8,128)(2,1)S(1)}, u32[]{:S(2)}, u32[]{:S(2)}) collective-permute-start(bf16[128,384]{1,0:T(8,128)(2,1)S(1)} %get-tuple-element.92), channel_id=1, source_target_pairs={{0,28},{4,24},{8,20},{12,16},{16,12},{20,8},{24,4},{28,0},{1,29},{... | collective-permute-start | bytes 294920 | tf_op jit(solution)/shard_map/ppermute | solution.py:34
  320.7 15.6 %collective-permute-start.40 = (bf16[128,384]{1,0:T(8,128)(2,1)S(1)}, bf16[128,384]{1,0:T(8,128)(2,1)S(1)}, u32[]{:S(2)}, u32[]{:S(2)}) collective-permute-start(bf16[128,384]{1,0:T(8,128)(2,1)S(1)} %get-tuple-element.93), channel_id=1, source_target_pairs={{0,24},{4,28},{8,16},{12,20},{16,8},{20,12},{24,0},{28,4},{1,25},{... | collective-permute-start | bytes 294920 | tf_op jit(solution)/shard_map/ppermute | solution.py:34
  322.1 15.8 %collective-permute-start.39 = (bf16[128,384]{1,0:T(8,128)(2,1)S(1)}, bf16[128,384]{1,0:T(8,128)(2,1)S(1)}, u32[]{:S(2)}, u32[]{:S(2)}) collective-permute-start(bf16[128,384]{1,0:T(8,128)(2,1)S(1)} %get-tuple-element.94), channel_id=1, source_target_pairs={{0,20},{4,16},{8,28},{12,24},{16,4},{20,0},{24,12},{28,8},{1,21},{... | collective-permute-start | bytes 294920 | tf_op jit(solution)/shard_map/ppermute | solution.py:34
  325.1 12.8 %collective-permute-start.38 = (bf16[128,384]{1,0:T(8,128)(2,1)S(1)}, bf16[128,384]{1,0:T(8,128)(2,1)S(1)}, u32[]{:S(2)}, u32[]{:S(2)}) collective-permute-start(bf16[128,384]{1,0:T(8,128)(2,1)S(1)} %get-tuple-element.95), channel_id=1, source_target_pairs={{0,16},{4,20},{8,24},{12,28},{16,0},{20,4},{24,8},{28,12},{1,17},{... | collective-permute-start | bytes 294920 | tf_op jit(solution)/shard_map/ppermute | solution.py:34
  325.1 12.8 %collective-permute-start.37 = (bf16[128,384]{1,0:T(8,128)(2,1)S(1)}, bf16[128,384]{1,0:T(8,128)(2,1)S(1)}, u32[]{:S(2)}, u32[]{:S(2)}) collective-permute-start(bf16[128,384]{1,0:T(8,128)(2,1)S(1)} %get-tuple-element.96), channel_id=1, source_target_pairs={{0,12},{4,8},{8,4},{12,0},{16,28},{20,24},{24,20},{28,16},{1,13},{... | collective-permute-start | bytes 294920 | tf_op jit(solution)/shard_map/ppermute | solution.py:34
  346.5 12.3 %collective-permute-start.44 = (bf16[128,384]{1,0:T(8,128)(2,1)S(1)}, bf16[128,384]{1,0:T(8,128)(2,1)S(1)}, u32[]{:S(2)}, u32[]{:S(2)}) collective-permute-start(bf16[128,384]{1,0:T(8,128)(2,1)S(1)} %add_convert_fusion.11), channel_id=1, source_target_pairs={{0,20},{4,16},{8,28},{12,24},{16,4},{20,0},{24,12},{28,8},{1,21},{... | collective-permute-start | bytes 294920 | tf_op jit(solution)/shard_map/ppermute | solution.py:34
  348.4 12.6 %collective-permute-start.45 = (bf16[128,384]{1,0:T(8,128)(2,1)S(1)}, bf16[128,384]{1,0:T(8,128)(2,1)S(1)}, u32[]{:S(2)}, u32[]{:S(2)}) collective-permute-start(bf16[128,384]{1,0:T(8,128)(2,1)S(1)} %add_convert_fusion.11), channel_id=1, source_target_pairs={{0,16},{4,20},{8,24},{12,28},{16,0},{20,4},{24,8},{28,12},{1,17},{... | collective-permute-start | bytes 294920 | tf_op jit(solution)/shard_map/ppermute | solution.py:34
  349.5 16.0 %collective-permute-start.42 = (bf16[128,384]{1,0:T(8,128)(2,1)S(1)}, bf16[128,384]{1,0:T(8,128)(2,1)S(1)}, u32[]{:S(2)}, u32[]{:S(2)}) collective-permute-start(bf16[128,384]{1,0:T(8,128)(2,1)S(1)} %add_convert_fusion.11), channel_id=1, source_target_pairs={{0,28},{4,24},{8,20},{12,16},{16,12},{20,8},{24,4},{28,0},{1,29},{... | collective-permute-start | bytes 294920 | tf_op jit(solution)/shard_map/ppermute | solution.py:34
  351.0 14.7 %collective-permute-start.43 = (bf16[128,384]{1,0:T(8,128)(2,1)S(1)}, bf16[128,384]{1,0:T(8,128)(2,1)S(1)}, u32[]{:S(2)}, u32[]{:S(2)}) collective-permute-start(bf16[128,384]{1,0:T(8,128)(2,1)S(1)} %add_convert_fusion.11), channel_id=1, source_target_pairs={{0,24},{4,28},{8,16},{12,20},{16,8},{20,12},{24,0},{28,4},{1,25},{... | collective-permute-start | bytes 294920 | tf_op jit(solution)/shard_map/ppermute | solution.py:34
  352.5 24.5 %collective-permute-start.50 = (bf16[256,1024]{1,0:T(8,128)(2,1)S(1)}, bf16[256,1024]{1,0:T(8,128)(2,1)S(1)}, u32[]{:S(2)}, u32[]{:S(2)}) collective-permute-start(bf16[256,1024]{1,0:T(8,128)(2,1)S(1)} %get-tuple-element.84), channel_id=1, source_target_pairs={{0,1},{1,0},{2,3},{3,2},{4,5},{5,4},{6,7},{7,6},{8,9},{9,8},{10,11... | collective-permute-start | bytes 1572872 | tf_op jit(solution)/shard_map/ppermute | solution.py:34
  358.8 34.0 %collective-permute-start.49 = (bf16[256,1024]{1,0:T(8,128)(2,1)S(1)}, bf16[256,1024]{1,0:T(8,128)(2,1)S(1)}, u32[]{:S(2)}, u32[]{:S(2)}) collective-permute-start(bf16[256,1024]{1,0:T(8,128)(2,1)S(1)} %get-tuple-element.83), channel_id=1, source_target_pairs={{0,1},{1,0},{2,3},{3,2},{4,5},{5,4},{6,7},{7,6},{8,9},{9,8},{10,11... | collective-permute-start | bytes 1572872 | tf_op jit(solution)/shard_map/ppermute | solution.py:34
  360.9 11.1 %collective-permute-start.27 = (bf16[512,384]{1,0:T(8,128)(2,1)S(1)}, bf16[512,384]{1,0:T(8,128)(2,1)S(1)}, u32[]{:S(2)}, u32[]{:S(2)}) collective-permute-start(bf16[512,384]{1,0:T(8,128)(2,1)S(1)} %dynamic-slice_convert_fusion.2), channel_id=1, source_target_pairs={{0,4},{4,0},{8,12},{12,8},{16,20},{20,16},{24,28},{28,24},{1,5},{5... | collective-permute-start | bytes 1179656 | tf_op jit(solution)/shard_map/ppermute | solution.py:34
  372.2 9.6 %collective-permute-start.30 = (bf16[128,384]{1,0:T(8,128)(2,1)S(1)}, bf16[128,384]{1,0:T(8,128)(2,1)S(1)}, u32[]{:S(2)}, u32[]{:S(2)}) collective-permute-start(bf16[128,384]{1,0:T(8,128)(2,1)S(1)} %get-tuple-element.143), channel_id=1, source_target_pairs={{0,24},{4,28},{8,16},{12,20},{16,8},{20,12},{24,0},{28,4},{1,25},{... | collective-permute-start | bytes 294920 | tf_op jit(solution)/shard_map/ppermute | solution.py:34
  377.1 15.7 %collective-permute-start.51 = (bf16[256,1024]{1,0:T(8,128)(2,1)S(1)}, bf16[256,1024]{1,0:T(8,128)(2,1)S(1)}, u32[]{:S(2)}, u32[]{:S(2)}) collective-permute-start(bf16[256,1024]{1,0:T(8,128)(2,1)S(1)} %fusion.76), channel_id=1, source_target_pairs={{0,2},{1,3},{2,0},{3,1},{4,6},{5,7},{6,4},{7,5},{8,10},{9,11},{10,... | collective-permute-start | bytes 1572872 | tf_op jit(solution)/shard_map/ppermute | solution.py:34
  387.3 37.7 %collective-permute-start.64 = (bf16[512,1024]{1,0:T(8,128)(2,1)S(1)}, bf16[512,1024]{1,0:T(8,128)(2,1)S(1)}, u32[]{:S(2)}, u32[]{:S(2)}) collective-permute-start(bf16[512,1024]{1,0:T(8,128)(2,1)S(1)} %copy-done.24), channel_id=1, source_target_pairs={{0,2},{1,3},{2,0},{3,1},{4,6},{5,7},{6,4},{7,5},{8,10},{9,11},{10,... | collective-permute-start | bytes 3145736 | tf_op jit(solution)/shard_map/ppermute | solution.py:34
  392.4 35.7 %collective-permute-start.25 = (bf16[512,1024]{1,0:T(8,128)(2,1)S(1)}, bf16[512,1024]{1,0:T(8,128)(2,1)S(1)}, u32[]{:S(2)}, u32[]{:S(2)}) collective-permute-start(bf16[512,1024]{1,0:T(8,128)(2,1)S(1)} %convolution_convert_fusion), channel_id=1, source_target_pairs={{0,1},{1,0},{2,3},{3,2},{4,5},{5,4},{6,7},{7,6},{8,9},{9,8},{10,11... | collective-permute-start | bytes 3145736 | tf_op jit(solution)/shard_map/ppermute | solution.py:34
  392.7 12.0 %collective-permute-start.34 = (bf16[512,384]{1,0:T(8,128)(2,1)S(1)}, bf16[512,384]{1,0:T(8,128)(2,1)S(1)}, u32[]{:S(2)}, u32[]{:S(2)}) collective-permute-start(bf16[512,384]{1,0:T(8,128)(2,1)S(1)} %pad_maximum_fusion.16), channel_id=1, source_target_pairs={{0,4},{4,0},{8,12},{12,8},{16,20},{20,16},{24,28},{28,24},{1,5},{5... | collective-permute-start | bytes 1179656 | tf_op jit(solution)/shard_map/ppermute | solution.py:34
  393.1 16.6 %collective-permute-start.52 = (bf16[128,1024]{1,0:T(8,128)(2,1)S(1)}, bf16[128,1024]{1,0:T(8,128)(2,1)S(1)}, u32[]{:S(2)}, u32[]{:S(2)}) collective-permute-start(bf16[128,1024]{1,0:T(8,128)(2,1)S(1)} %dynamic-slice_convert_fusion.3), channel_id=1, source_target_pairs={{0,4},{4,0},{8,12},{12,8},{16,20},{20,16},{24,28},{28,24},{1,5},{5... | collective-permute-start | bytes 786440 | tf_op jit(solution)/shard_map/ppermute | solution.py:34
  425.0 12.2 %collective-permute-start.63 = (bf16[512,1024]{1,0:T(8,128)(2,1)S(1)}, bf16[512,1024]{1,0:T(8,128)(2,1)S(1)}, u32[]{:S(2)}, u32[]{:S(2)}) collective-permute-start(bf16[512,1024]{1,0:T(8,128)(2,1)S(1)} %copy-done.24), channel_id=1, source_target_pairs={{0,1},{1,0},{2,3},{3,2},{4,5},{5,4},{6,7},{7,6},{8,9},{9,8},{10,11... | collective-permute-start | bytes 3145736 | tf_op jit(solution)/shard_map/ppermute | solution.py:34
  425.0 47.4 %collective-permute-start.24 = (bf16[512,1024]{1,0:T(8,128)(2,1)}, bf16[512,1024]{1,0:T(8,128)(2,1)}, u32[]{:S(2)}, u32[]{:S(2)}) collective-permute-start(bf16[512,1024]{1,0:T(8,128)(2,1)} %convolution_convert_fusion.1), channel_id=1, source_target_pairs={{0,1},{1,0},{2,3},{3,2},{4,5},{5,4},{6,7},{7,6},{8,9},{9,8},{10,11... | collective-permute-start | bytes 3145736 | tf_op jit(solution)/shard_map/ppermute | solution.py:34
  427.2 11.0 %collective-permute-start.65 = (bf16[512,1024]{1,0:T(8,128)(2,1)S(1)}, bf16[512,1024]{1,0:T(8,128)(2,1)}, u32[]{:S(2)}, u32[]{:S(2)}) collective-permute-start(bf16[512,1024]{1,0:T(8,128)(2,1)S(1)} %collective-permute-done.64), channel_id=1, source_target_pairs={{0,1},{1,0},{2,3},{3,2},{4,5},{5,4},{6,7},{7,6},{8,9},{9,8},{10,11... | collective-permute-start | bytes 3145736 | tf_op jit(solution)/shard_map/ppermute | solution.py:34
  430.0 42.4 %collective-permute-start.26 = (bf16[512,1024]{1,0:T(8,128)(2,1)}, bf16[512,1024]{1,0:T(8,128)(2,1)}, u32[]{:S(2)}, u32[]{:S(2)}) collective-permute-start(bf16[512,1024]{1,0:T(8,128)(2,1)} %add_convert_fusion.2), channel_id=1, source_target_pairs={{0,2},{1,3},{2,0},{3,1},{4,6},{5,7},{6,4},{7,5},{8,10},{9,11},{10,... | collective-permute-start | bytes 3145736 | tf_op jit(solution)/shard_map/ppermute | solution.py:34
  460.5 26.2 %collective-permute-start.66 = (bf16[512,1024]{1,0:T(8,128)(2,1)S(1)}, bf16[512,1024]{1,0:T(8,128)(2,1)S(1)}, u32[]{:S(2)}, u32[]{:S(2)}) collective-permute-start(bf16[512,1024]{1,0:T(8,128)(2,1)S(1)} %dynamic-slice_convert_fusion.1), channel_id=1, source_target_pairs={{0,4},{4,0},{8,12},{12,8},{16,20},{20,16},{24,28},{28,24},{1,5},{5... | collective-permute-start | bytes 3145736 | tf_op jit(solution)/shard_map/ppermute | solution.py:34
  470.9 36.7 %collective-permute-start.74 = (bf16[512,1024]{1,0:T(8,128)(2,1)S(1)}, bf16[512,1024]{1,0:T(8,128)(2,1)S(1)}, u32[]{:S(2)}, u32[]{:S(2)}) collective-permute-start(bf16[512,1024]{1,0:T(8,128)(2,1)S(1)} %dynamic-slice_convert_fusion), channel_id=1, source_target_pairs={{0,4},{4,0},{8,12},{12,8},{16,20},{20,16},{24,28},{28,24},{1,5},{5... | collective-permute-start | bytes 3145736 | tf_op jit(solution)/shard_map/ppermute | solution.py:34
  476.1 37.1 %collective-permute-start.83 = (f32[2,1024]{1,0:T(2,128)S(1)}, f32[2,1024]{1,0:T(2,128)S(1)}, u32[]{:S(2)}, u32[]{:S(2)}) collective-permute-start(f32[2,1024]{1,0:T(2,128)S(1)} %pad_maximum_fusion.20), channel_id=1, source_target_pairs={{0,2},{1,3},{2,0},{3,1},{4,6},{5,7},{6,4},{7,5},{8,10},{9,11},{10,... | collective-permute-start | bytes 24584 | tf_op jit(solution)/shard_map/ppermute | solution.py:34
  487.1 26.2 %collective-permute-start.69 = (bf16[128,1024]{1,0:T(8,128)(2,1)S(1)}, bf16[128,1024]{1,0:T(8,128)(2,1)S(1)}, u32[]{:S(2)}, u32[]{:S(2)}) collective-permute-start(bf16[128,1024]{1,0:T(8,128)(2,1)S(1)} %get-tuple-element.113), channel_id=1, source_target_pairs={{0,24},{4,28},{8,16},{12,20},{16,8},{20,12},{24,0},{28,4},{1,25},{... | collective-permute-start | bytes 786440 | tf_op jit(solution)/shard_map/ppermute | solution.py:34
  488.1 26.5 %collective-permute-start.68 = (bf16[128,1024]{1,0:T(8,128)(2,1)S(1)}, bf16[128,1024]{1,0:T(8,128)(2,1)S(1)}, u32[]{:S(2)}, u32[]{:S(2)}) collective-permute-start(bf16[128,1024]{1,0:T(8,128)(2,1)S(1)} %get-tuple-element.114), channel_id=1, source_target_pairs={{0,16},{4,20},{8,24},{12,28},{16,0},{20,4},{24,8},{28,12},{1,17},{... | collective-permute-start | bytes 786440 | tf_op jit(solution)/shard_map/ppermute | solution.py:34
  491.6 27.0 %collective-permute-start.67 = (bf16[128,1024]{1,0:T(8,128)(2,1)S(1)}, bf16[128,1024]{1,0:T(8,128)(2,1)S(1)}, u32[]{:S(2)}, u32[]{:S(2)}) collective-permute-start(bf16[128,1024]{1,0:T(8,128)(2,1)S(1)} %get-tuple-element.112), channel_id=1, source_target_pairs={{0,8},{4,12},{8,0},{12,4},{16,24},{20,28},{24,16},{28,20},{1,9},{5... | collective-permute-start | bytes 786440 | tf_op jit(solution)/shard_map/ppermute | solution.py:34
  508.1 19.6 %collective-permute-start.77 = (bf16[128,1024]{1,0:T(8,128)(2,1)S(1)}, bf16[128,1024]{1,0:T(8,128)(2,1)S(1)}, u32[]{:S(2)}, u32[]{:S(2)}) collective-permute-start(bf16[128,1024]{1,0:T(8,128)(2,1)S(1)} %get-tuple-element.106), channel_id=1, source_target_pairs={{0,24},{4,28},{8,16},{12,20},{16,8},{20,12},{24,0},{28,4},{1,25},{... | collective-permute-start | bytes 786440 | tf_op jit(solution)/shard_map/ppermute | solution.py:34
  514.6 28.5 %collective-permute-start.76 = (bf16[128,1024]{1,0:T(8,128)(2,1)S(1)}, bf16[128,1024]{1,0:T(8,128)(2,1)S(1)}, u32[]{:S(2)}, u32[]{:S(2)}) collective-permute-start(bf16[128,1024]{1,0:T(8,128)(2,1)S(1)} %get-tuple-element.107), channel_id=1, source_target_pairs={{0,16},{4,20},{8,24},{12,28},{16,0},{20,4},{24,8},{28,12},{1,17},{... | collective-permute-start | bytes 786440 | tf_op jit(solution)/shard_map/ppermute | solution.py:34
  518.6 25.5 %collective-permute-start.75 = (bf16[128,1024]{1,0:T(8,128)(2,1)S(1)}, bf16[128,1024]{1,0:T(8,128)(2,1)S(1)}, u32[]{:S(2)}, u32[]{:S(2)}) collective-permute-start(bf16[128,1024]{1,0:T(8,128)(2,1)S(1)} %get-tuple-element.105), channel_id=1, source_target_pairs={{0,8},{4,12},{8,0},{12,4},{16,24},{20,28},{24,16},{28,20},{1,9},{5... | collective-permute-start | bytes 786440 | tf_op jit(solution)/shard_map/ppermute | solution.py:34
  518.8 34.6 %collective-permute-start.70 = (bf16[128,1024]{1,0:T(8,128)(2,1)S(1)}, bf16[128,1024]{1,0:T(8,128)(2,1)S(1)}, u32[]{:S(2)}, u32[]{:S(2)}) collective-permute-start(bf16[128,1024]{1,0:T(8,128)(2,1)S(1)} %add_convert_fusion.9), channel_id=1, source_target_pairs={{0,24},{4,28},{8,16},{12,20},{16,8},{20,12},{24,0},{28,4},{1,25},{... | collective-permute-start | bytes 786440 | tf_op jit(solution)/shard_map/ppermute | solution.py:34
  519.8 40.5 %collective-permute-start.71 = (bf16[128,1024]{1,0:T(8,128)(2,1)S(1)}, bf16[128,1024]{1,0:T(8,128)(2,1)S(1)}, u32[]{:S(2)}, u32[]{:S(2)}) collective-permute-start(bf16[128,1024]{1,0:T(8,128)(2,1)S(1)} %add_convert_fusion.9), channel_id=1, source_target_pairs={{0,16},{4,20},{8,24},{12,28},{16,0},{20,4},{24,8},{28,12},{1,17},{... | collective-permute-start | bytes 786440 | tf_op jit(solution)/shard_map/ppermute | solution.py:34
  527.7 36.0 %collective-permute-start.72 = (bf16[128,1024]{1,0:T(8,128)(2,1)S(1)}, bf16[128,1024]{1,0:T(8,128)(2,1)S(1)}, u32[]{:S(2)}, u32[]{:S(2)}) collective-permute-start(bf16[128,1024]{1,0:T(8,128)(2,1)S(1)} %add_convert_fusion.9), channel_id=1, source_target_pairs={{0,8},{4,12},{8,0},{12,4},{16,24},{20,28},{24,16},{28,20},{1,9},{5... | collective-permute-start | bytes 786440 | tf_op jit(solution)/shard_map/ppermute | solution.py:34
  543.1 38.3 %collective-permute-start.90 = (f32[2,1024]{1,0:T(2,128)S(1)}, f32[2,1024]{1,0:T(2,128)S(1)}, u32[]{:S(2)}, u32[]{:S(2)}) collective-permute-start(f32[2,1024]{1,0:T(2,128)S(1)} %add_add_fusion.9), channel_id=1, source_target_pairs={{0,24},{4,28},{8,16},{12,20},{16,8},{20,12},{24,0},{28,4},{1,25},{... | collective-permute-start | bytes 24584 | tf_op jit(solution)/shard_map/ppermute | solution.py:34
  544.1 37.4 %collective-permute-start.91 = (f32[2,1024]{1,0:T(2,128)S(1)}, f32[2,1024]{1,0:T(2,128)S(1)}, u32[]{:S(2)}, u32[]{:S(2)}) collective-permute-start(f32[2,1024]{1,0:T(2,128)S(1)} %add_add_fusion.9), channel_id=1, source_target_pairs={{0,28},{4,24},{8,20},{12,16},{16,12},{20,8},{24,4},{28,0},{1,29},{... | collective-permute-start | bytes 24584 | tf_op jit(solution)/shard_map/ppermute | solution.py:34
  553.3 20.0 %collective-permute-start.78 = (bf16[128,1024]{1,0:T(8,128)(2,1)S(1)}, bf16[128,1024]{1,0:T(8,128)(2,1)S(1)}, u32[]{:S(2)}, u32[]{:S(2)}) collective-permute-start(bf16[128,1024]{1,0:T(8,128)(2,1)S(1)} %add_convert_fusion.8), channel_id=1, source_target_pairs={{0,24},{4,28},{8,16},{12,20},{16,8},{20,12},{24,0},{28,4},{1,25},{... | collective-permute-start | bytes 786440 | tf_op jit(solution)/shard_map/ppermute | solution.py:34
  560.3 16.3 %collective-permute-start.79 = (bf16[128,1024]{1,0:T(8,128)(2,1)S(1)}, bf16[128,1024]{1,0:T(8,128)(2,1)S(1)}, u32[]{:S(2)}, u32[]{:S(2)}) collective-permute-start(bf16[128,1024]{1,0:T(8,128)(2,1)S(1)} %add_convert_fusion.8), channel_id=1, source_target_pairs={{0,16},{4,20},{8,24},{12,28},{16,0},{20,4},{24,8},{28,12},{1,17},{... | collective-permute-start | bytes 786440 | tf_op jit(solution)/shard_map/ppermute | solution.py:34
  563.7 16.0 %collective-permute-start.80 = (bf16[128,1024]{1,0:T(8,128)(2,1)S(1)}, bf16[128,1024]{1,0:T(8,128)(2,1)S(1)}, u32[]{:S(2)}, u32[]{:S(2)}) collective-permute-start(bf16[128,1024]{1,0:T(8,128)(2,1)S(1)} %add_convert_fusion.8), channel_id=1, source_target_pairs={{0,8},{4,12},{8,0},{12,4},{16,24},{20,28},{24,16},{28,20},{1,9},{5... | collective-permute-start | bytes 786440 | tf_op jit(solution)/shard_map/ppermute | solution.py:34
  573.4 10.0 %collective-permute-start.88 = (f32[2,1024]{1,0:T(2,128)S(1)}, f32[2,1024]{1,0:T(2,128)S(1)}, u32[]{:S(2)}, u32[]{:S(2)}) collective-permute-start(f32[2,1024]{1,0:T(2,128)S(1)} %add_add_fusion.9), channel_id=1, source_target_pairs={{0,16},{4,20},{8,24},{12,28},{16,0},{20,4},{24,8},{28,12},{1,17},{... | collective-permute-start | bytes 24584 | tf_op jit(solution)/shard_map/ppermute | solution.py:34
  579.6 27.7 %collective-permute-start.73 = (bf16[512,1024]{1,0:T(8,128)(2,1)S(1)}, bf16[512,1024]{1,0:T(8,128)(2,1)S(1)}, u32[]{:S(2)}, u32[]{:S(2)}) collective-permute-start(bf16[512,1024]{1,0:T(8,128)(2,1)S(1)} %pad_maximum_fusion.4), channel_id=1, source_target_pairs={{0,4},{4,0},{8,12},{12,8},{16,20},{20,16},{24,28},{28,24},{1,5},{5... | collective-permute-start | bytes 3145736 | tf_op jit(solution)/shard_map/ppermute | solution.py:34
  583.3 22.8 %collective-permute-start.85 = (f32[2,1024]{1,0:T(2,128)S(1)}, f32[2,1024]{1,0:T(2,128)S(1)}, u32[]{:S(2)}, u32[]{:S(2)}) collective-permute-start(f32[2,1024]{1,0:T(2,128)S(1)} %add_add_fusion.9), channel_id=1, source_target_pairs={{0,4},{4,0},{8,12},{12,8},{16,20},{20,16},{24,28},{28,24},{1,5},{5... | collective-permute-start | bytes 24584 | tf_op jit(solution)/shard_map/ppermute | solution.py:34
  585.1 41.2 %collective-permute-start.81 = (bf16[512,1024]{1,0:T(8,128)(2,1)S(1)}, bf16[512,1024]{1,0:T(8,128)(2,1)S(1)}, u32[]{:S(2)}, u32[]{:S(2)}) collective-permute-start(bf16[512,1024]{1,0:T(8,128)(2,1)S(1)} %pad_maximum_fusion.5), channel_id=1, source_target_pairs={{0,4},{4,0},{8,12},{12,8},{16,20},{20,16},{24,28},{28,24},{1,5},{5... | collective-permute-start | bytes 3145736 | tf_op jit(solution)/shard_map/ppermute | solution.py:34
  (92 other events, 678.8 us)

commit v2 on v1

--- a/solution.py
+++ b/solution.py
@@ -12,6 +12,7 @@
 EPSILON = 1e-05
 ROPE_BASE = 10000.0
 NEG = -1e30
+MESH = pl.DeviceIdType.MESH
 BF = jnp.bfloat16
 F32 = jnp.float32
 NT = (((1,), (1,)), ((), ()))
@@ -47,19 +48,32 @@
     return parts
 
 
-def reduce_scatter_tensor(parts):
-    size = lax.axis_size("tensor")
-    terms = {d: parts[d] for d in range(size)}
-    step = 1
-    while step < size:
-        kept = {}
-        for d in sorted(terms):
-            if d & step == 0:
-                got = swap(terms[d ^ step].astype(BF), "tensor", step)
-                kept[d] = terms[d].astype(F32) + got.astype(F32)
-        terms = kept
-        step *= 2
-    return terms[0]
+def flip(index, offset):
+    bit = 1
+    while bit <= offset:
+        if offset & bit:
+            index = index + bit - 2 * bit * lax.rem(lax.div(index, bit), 2)
+        bit *= 2
+    return index
+
+
+def xor(a, b, size):
+    total, bit = 0, 1
+    while bit < size:
+        total = total + bit * lax.rem(lax.div(a, bit) + lax.div(b, bit), 2)
+        bit *= 2
+    return total
+
+
+def greet(axes):
+    barrier = pltpu.get_barrier_semaphore()
+    count = 0
+    for axis in axes:
+        index = lax.axis_index(axis)
+        for d in range(1, lax.axis_size(axis)):
+            pl.semaphore_signal(barrier, inc=1, device_id={axis: flip(index, d)}, device_id_type=MESH)
+            count += 1
+    pl.semaphore_wait(barrier, count)
 
 
 def tree_sum(parts):
@@ -69,51 +83,15 @@
     return parts[0]
 
 
-def sum_all(value):
-    for axis in ("tensor", "dp"):
-        size = lax.axis_size(axis)
-        value = tree_sum([value] + [swap(value, axis, d) for d in range(1, size)])
-    return value
-
-
-def in_order(parts, index):
-    size = len(parts)
-    step = 1
-    while step < size:
-        flip = (index & step) != 0
-        parts = [jnp.where(flip, parts[d ^ step], parts[d]) for d in range(size)]
-        step *= 2
-    return parts
-
-
-def reduce_dp(partial, direct):
-    size = lax.axis_size("dp")
-    index = lax.axis_index("dp")
-    rows = partial.shape[0]
-    shift = 0
-    if not direct:
-        half = rows // 2
-        bit = index & 1
-        there = lax.dynamic_slice_in_dim(partial, (1 - bit) * half, half, 0).astype(BF)
-        here = lax.dynamic_slice_in_dim(partial, bit * half, half, 0)
-        got = swap(there, "dp", 1)
-        partial = (here.astype(F32) + got.astype(F32)).astype(BF)
-        rows, shift = half, 1
-    group = size >> shift
-    place = index >> shift
-    piece = rows // group
-    parts = [lax.dynamic_slice_in_dim(partial, place * piece, piece, 0)]
-    for d in range(1, group):
-        part = lax.dynamic_slice_in_dim(partial, (place ^ d) * piece, piece, 0).astype(BF)
-        parts.append(swap(part, "dp", d << shift))
-    total = tree_sum(parts).astype(BF)
-    parts = [total] + [swap(total, "dp", d << shift) for d in range(1, group)]
-    full = jnp.concatenate(in_order(parts, place), axis=0)
-    if not direct:
-        got = swap(full, "dp", 1)
-        flip = (index & 1) != 0
-        full = jnp.concatenate([jnp.where(flip, got, full), jnp.where(flip, full, got)], axis=0)
-    return full.astype(F32)
+def push(src, dst, sems, slot, axis, offset):
+    return pltpu.make_async_remote_copy(
+        src_ref=src,
+        dst_ref=dst,
+        send_sem=sems.at[0, slot],
+        recv_sem=sems.at[1, slot],
+        device_id={axis: flip(lax.axis_index(axis), offset)},
+        device_id_type=MESH,
+    )
 
 
 def turn(values, cosine, signed_sine):
@@ -242,19 +220,82 @@
 
 
 def backward_kernel(
-    block, blocks, place_ref, q_ref, k_ref, v_ref, do_ref, o_ref, log_ref, start_ref, cos_ref, sin_ref, out_ref, dq_ref, inner_ref
+    block, blocks, pairs, chunks, *refs
 ):
-    mine = place_ref[0]
-    step = pl.program_id(0)
-    key_block = step ^ mine
+    (qkv_ref, gh_ref, o_ref, log_ref, start_ref, cos_ref, sin_ref, shared_ref, *refs) = refs
+    terms, refs = refs[: chunks - 1], refs[chunks - 1 :]
+    (out_ref, *refs) = refs
+    pieces, refs = refs[:chunks], refs[chunks:]
+    dq_ref, inner_ref, do_ref, *refs = refs
+    got_x, refs = refs[:chunks], refs[chunks:]
+    half, refs = refs[:chunks], refs[chunks:]
+    got_z, refs = refs[:chunks], refs[chunks:]
+    got_core, core_sum, got_y, own_ref, head_sems, x_sems, z_sems, core_sems, y_sems = refs
+    terms = [*terms, own_ref]
+
+    mine = lax.axis_index("tensor")
+    rank = lax.axis_index("dp")
+    group = lax.axis_size("dp") // 2
+    x_bit, z_place = lax.rem(rank, 2), lax.div(rank, 2)
     heads = PAIR // HD
-
-    @pl.when(step == 0)
-    def _():
+    greet(("tensor", "dp"))
+
+    head_copies = {}
+    for pair in range(pairs):
+        for d in range(1, blocks):
+            copy = push(
+                gh_ref.at[d * pairs + pair], do_ref.at[pair, d], head_sems, pair * (blocks - 1) + d - 1, "tensor", d
+            )
+            copy.start()
+            head_copies[pair, d] = copy
+    core_copies = [
+        push(shared_ref.at[d + 1], got_core.at[d // 2], core_sems, d // 2, "tensor", 1) for d in range(0, blocks, 2)
+    ]
+    y_copies = [
+        push(core_sum.at[h], got_y.at[h - 1], y_sems, h - 1, "tensor", 2 * h) for h in range(1, blocks // 2)
+    ]
+    x_copies = [push(terms[c].at[1 - x_bit], got_x[c], x_sems, c, "dp", 1) for c in range(chunks)]
+    for copy in [*core_copies, *x_copies[:-1]]:
+        copy.start()
+    z_copies = {}
+    for c in range(chunks):
+        for d in range(1, group):
+            z_copies[c, d] = push(
+                half[c].at[xor(z_place, d, group)], got_z[c].at[d - 1], z_sems, c * (group - 1) + d - 1, "dp", 2 * d
+            )
+
+    def halve(c):
+        x_copies[c].wait_recv()
+        for g in range(group):
+            half[c][g] = (terms[c][x_bit, g].astype(F32) + got_x[c][g].astype(F32)).astype(BF)
+        for d in range(1, group):
+            z_copies[c, d].start()
+
+    def pair_up():
+        for h in range(blocks // 2):
+            core_copies[h].wait_recv()
+            core_sum[h] = (shared_ref[2 * h].astype(F32) + got_core[h].astype(F32)).astype(BF)
+        for copy in y_copies:
+            copy.start()
+
+    def settle():
+        total = core_sum[0].astype(F32)
+        for h in range(1, blocks // 2):
+            y_copies[h - 1].wait_recv()
+            total = total + got_y[h - 1].astype(F32)
+        own_ref[...] = total.astype(BF)
+        x_copies[-1].start()
+
+    for pair in range(pairs):
+        do_ref[pair, 0] = gh_ref[pair]
+
+    def prepare(pair):
+        for d in range(1, blocks):
+            head_copies[pair, d].wait_recv()
         dq_ref[...] = jnp.zeros_like(dq_ref)
         for b in range(blocks):
             rows = pl.ds(b * block, block)
-            product = do_ref[rows, :].astype(F32) * o_ref[rows, :].astype(F32)
+            product = do_ref[pair, b].astype(F32) * o_ref[pair, rows, :].astype(F32)
             high = product.astype(BF)
             low = (product - high.astype(F32)).astype(BF)
             for head in range(heads):
@@ -262,79 +303,254 @@
                 inner = dot(ones, high, NT) + dot(ones, low, NT)
                 inner_ref[head : head + 1, rows] = inner[0:1, :]
 
-    here = pl.ds(pl.multiple_of(step * block, block), block)
-    keys = k_ref[here, :]
-    values = v_ref[here, :]
-    dk = jnp.zeros((block, PAIR), F32)
-    dv = jnp.zeros((block, PAIR), F32)
-    for head in range(heads):
-        mask = head_mask(keys.shape, head)
-        key = jnp.where(mask, keys * HD**-0.5, jnp.zeros_like(keys))
-        value = jnp.where(mask, values, jnp.zeros_like(values))
-
-        def one(i, carry, first):
-            dk, dv = carry
-            rows = pl.ds(pl.multiple_of((i ^ mine) * block, block), block)
-            real = pl.ds(pl.multiple_of(i * block, block), block)
-            query = q_ref[rows, :]
-            grad = do_ref[rows, :]
-            s = dot(key, query, NT)
-            row = lax.broadcasted_iota(jnp.int32, s.shape, 0)
-            visible = row >= start_ref[0:1, real] - key_block * block
-            if first:
-                visible &= row <= lax.broadcasted_iota(jnp.int32, s.shape, 1)
-            probs = jnp.where(visible, jnp.exp(s - log_ref[head : head + 1, rows]), 0.0)
-            grad_probs = dot(value, grad, NT)
-            ds = (probs * (grad_probs - inner_ref[head : head + 1, rows])).astype(BF)
-            zero = jnp.zeros_like(query)
-            dv = dv + dot(probs.astype(BF), jnp.where(mask, grad, zero))
-            dk = dk + dot(ds, jnp.where(mask, query, zero))
-            dq_ref[rows, :] += dot(ds, key, TN)
-            return dk, dv
-
-        dk, dv = one(key_block, (dk, dv), True)
-        dk, dv = lax.fori_loop(key_block + 1, blocks, lambda i, carry: one(i, carry, False), (dk, dv))
-    real = pl.ds(pl.multiple_of(key_block * block, block), block)
-    out_ref[1, here, :] = turn(dk * HD**-0.5, cos_ref[real, :], -sin_ref[real, :]).astype(BF)
-    out_ref[2, here, :] = dv.astype(BF)
-
-    @pl.when(step == blocks - 1)
-    def _():
+    def unit(pair, key_block):
+        slot = xor(key_block, mine, blocks)
+        here = pl.ds(pl.multiple_of(slot * block, block), block)
+        keys = qkv_ref[pairs + pair, here, :]
+        values = qkv_ref[2 * pairs + pair, here, :]
+        dk = jnp.zeros((block, PAIR), F32)
+        dv = jnp.zeros((block, PAIR), F32)
+        for head in range(heads):
+            mask = head_mask(keys.shape, head)
+            key = jnp.where(mask, keys * HD**-0.5, jnp.zeros_like(keys))
+            value = jnp.where(mask, values, jnp.zeros_like(values))
+
+            def one(i, carry, first):
+                dk, dv = carry
+                place = xor(i, mine, blocks)
+                rows = pl.ds(pl.multiple_of(place * block, block), block)
+                real = pl.ds(pl.multiple_of(i * block, block), block)
+                query = qkv_ref[pair, rows, :]
+                grad = do_ref[pair, place]
+                s = dot(key, query, NT)
+                row = lax.broadcasted_iota(jnp.int32, s.shape, 0)
+                visible = row >= start_ref[0:1, real] - key_block * block
+                if first:
+                    visible &= row <= lax.broadcasted_iota(jnp.int32, s.shape, 1)
+                probs = jnp.where(visible, jnp.exp(s - log_ref[pair, head : head + 1, rows]), 0.0)
+                grad_probs = dot(value, grad, NT)
+                ds = (probs * (grad_probs - inner_ref[head : head + 1, rows])).astype(BF)
+                zero = jnp.zeros_like(query)
+                dv = dv + dot(probs.astype(BF), jnp.where(mask, grad, zero))
+                dk = dk + dot(ds, jnp.where(mask, query, zero))
+                dq_ref[rows, :] += dot(ds, key, TN)
+                return dk, dv
+
+            dk, dv = one(key_block, (dk, dv), True)
+            dk, dv = lax.fori_loop(key_block + 1, blocks, lambda i, carry: one(i, carry, False), (dk, dv))
+        real = pl.ds(pl.multiple_of(key_block * block, block), block)
+        out_ref[pairs + pair, here, :] = turn(dk * HD**-0.5, cos_ref[real, :], -sin_ref[real, :]).astype(BF)
+        out_ref[2 * pairs + pair, here, :] = dv.astype(BF)
+
+    def finish(pair):
         for b in range(blocks):
             rows = pl.ds(b * block, block)
-            real = pl.ds(pl.multiple_of((b ^ mine) * block, block), block)
-            out_ref[0, rows, :] = turn(dq_ref[rows, :], cos_ref[real, :], -sin_ref[real, :]).astype(BF)
-
-
-def attend_backward(place, qkv, pair, grad_heads, heads_out, logs, start_row, cosine, sine, block):
+            real = pl.ds(pl.multiple_of(flip(mine, b) * block, block), block)
+            out_ref[pair, rows, :] = turn(dq_ref[rows, :], cos_ref[real, :], -sin_ref[real, :]).astype(BF)
+
+    slots = pairs * blocks
+
+    @pl.loop(0, slots)
+    def _(u):
+        pair, key_block = lax.div(u, blocks), lax.rem(u, blocks)
+        for p in range(pairs):
+            pl.when(u == p * blocks)(functools.partial(prepare, p))
+        unit(pair, key_block)
+        pl.when(key_block == blocks - 1)(functools.partial(finish, pair))
+        pl.when(u == 0)(pair_up)
+        pl.when(u == slots // 2)(settle)
+        for c in range(chunks):
+            pl.when(u == min(slots - 1, 2 * c + 1))(functools.partial(halve, c))
+
+    for c in range(chunks):
+        for d in range(1, group):
+            z_copies[c, d].wait_recv()
+        parts = [half[c][z_place]] + [got_z[c][d] for d in range(group - 1)]
+        pieces[c][...] = tree_sum(parts).astype(BF)
+    for copy in [*head_copies.values(), *core_copies, *y_copies, *x_copies, *z_copies.values()]:
+        copy.wait_send()
+
+
+def attend_backward(qkv, grad_heads, heads_out, logs, start_row, cosine, sine, shared, terms, block):
     pairs3, length, _ = qkv.shape
     pairs = pairs3 // 3
     blocks = length // block
-    whole = lambda d, place: (0, 0)
+    group = terms[0].shape[1]
+    vmem = pl.BlockSpec(memory_space=pltpu.VMEM)
+    inner = [term.shape[1:] for term in terms] + [shared.shape[2:]]
+    chunks = len(inner)
+    copies = pltpu.SemaphoreType.DMA
     return pl.pallas_call(
-        functools.partial(backward_kernel, block, blocks),
-        out_shape=jax.ShapeDtypeStruct((3, length, PAIR), BF),
-        grid_spec=pltpu.PrefetchScalarGridSpec(
-            num_scalar_prefetch=1,
-            grid=(blocks,),
-            in_specs=[
-                pl.BlockSpec((None, length, PAIR), lambda d, place: (pair, 0, 0)),
-                pl.BlockSpec((None, length, PAIR), lambda d, place: (pairs + pair, 0, 0)),
-                pl.BlockSpec((None, length, PAIR), lambda d, place: (2 * pairs + pair, 0, 0)),
-                pl.BlockSpec((length, PAIR), whole),
-                pl.BlockSpec((length, PAIR), whole),
-                pl.BlockSpec((8, length), whole),
-                pl.BlockSpec((1, length), whole),
-                pl.BlockSpec((length, PAIR), whole),
-                pl.BlockSpec((length, PAIR), whole),
-            ],
-            out_specs=pl.BlockSpec((3, length, PAIR), lambda d, place: (0, 0, 0)),
-            scratch_shapes=[pltpu.VMEM((length, PAIR), F32), pltpu.VMEM((8, length), F32)],
-        ),
-        compiler_params=pltpu.CompilerParams(vmem_limit_bytes=40 << 20),
-        cost_estimate=pl.CostEstimate(flops=50 * length * length * PAIR, bytes_accessed=8 * length * PAIR * 2, transcendentals=length * length),
+        functools.partial(backward_kernel, block, blocks, pairs, chunks),
+        out_shape=[jax.ShapeDtypeStruct((pairs3, length, PAIR), BF)]
+        + [jax.ShapeDtypeStruct(shape[1:], BF) for shape in inner],
+        in_specs=[vmem] * (8 + len(terms)),
+        out_specs=[vmem] * (1 + chunks),
+        scratch_shapes=[
+            pltpu.VMEM((length, PAIR), F32),
+            pltpu.VMEM((8, length), F32),
+            pltpu.VMEM((pairs, blocks, block, PAIR), BF),
+            *[pltpu.VMEM(shape, BF) for shape in inner],
+            *[pltpu.VMEM(shape, BF) for shape in inner],
+            *[pltpu.VMEM((group - 1, *shape[1:]), BF) for shape in inner],
+            pltpu.VMEM((blocks // 2, *shared.shape[1:]), BF),
+            pltpu.VMEM((blocks // 2, *shared.shape[1:]), BF),
+            pltpu.VMEM((blocks // 2 - 1, *shared.shape[1:]), BF),
+            pltpu.VMEM(shared.shape[1:], BF),
+            copies((2, pairs * (blocks - 1))),
+            copies((2, chunks)),
+            copies((2, chunks * (group - 1))),
+            copies((2, blocks // 2)),
+            copies((2, blocks // 2 - 1)),
+        ],
+        compiler_params=pltpu.CompilerParams(vmem_limit_bytes=56 << 20, collective_id=0, has_side_effects=True),
+        cost_estimate=pl.CostEstimate(flops=100 * length * length * PAIR, bytes_accessed=16 * length * PAIR * 2, transcendentals=length * length),
         name="attend_backward",
-    )(place, qkv, qkv, qkv, grad_heads, heads_out, logs, start_row, cosine, sine)
+    )(qkv, grad_heads, heads_out, logs, start_row, cosine, sine, shared, *terms)
+
+
+def last_kernel(ranks, pieces_count, *refs):
+    x_ref, gain_ref, rest_ref, early_ref, tokens_ref, qkv_ref, *refs = refs
+    pieces, refs = refs[:pieces_count], refs[pieces_count:]
+    input_ref, sums_ref, qkv_out, *refs = refs
+    outs, refs = refs[:pieces_count], refs[pieces_count:]
+    (got_core, token_sum, got_y, terms, got_t, sum_t, got_d, got_x, half, got_z, own_piece, *refs) = refs
+    (core_sems, y_sems, t_sems, d_sems, x_sems, z_sems, zg_sems, xg_sems) = refs
+    rank = lax.axis_index("dp")
+    group = lax.axis_size("dp") // 2
+    x_bit, z_place = lax.rem(rank, 2), lax.div(rank, 2)
+    started = []
+
+    def start(copy):
+        copy.start()
+        started.append(copy)
+        return copy
+
+    greet(("tensor", "dp"))
+    core = [
+        start(push(tokens_ref.at[d + 1], got_core.at[d // 2], core_sems, d // 2, "tensor", 1)) for d in range(0, ranks, 2)
+    ]
+    x_copy = start(push(qkv_ref.at[1 - x_bit], got_x, x_sems, 0, "dp", 1))
+    gathers = {}
+
+    def spread(k, src, out):
+        out[x_bit, z_place] = src[...]
+        for d in range(1, group):
+            gathers[k, d] = start(
+                push(src, out.at[x_bit, z_place], zg_sems, k * (group - 1) + d - 1, "dp", 2 * d)
+            )
+
+    def share(k, out):
+        for d in range(1, group):
+            gathers[k, d].wait_recv()
+        return start(push(out.at[x_bit], out.at[x_bit], xg_sems, k, "dp", 1))
+
+    for k in range(pieces_count):
+        spread(k, pieces[k], outs[k])
+
+    for d in range(0, ranks, 2):
+        core[d // 2].wait_recv()
+        token_sum[d // 2] = (tokens_ref[d].astype(F32) + got_core[d // 2].astype(F32)).astype(BF)
+    ys = [start(push(token_sum.at[h], got_y.at[h - 1], y_sems, h - 1, "tensor", 2 * h)) for h in range(1, ranks // 2)]
+
+    x_copy.wait_recv()
+    for g in range(group):
+        half[g] = (qkv_ref[x_bit, g].astype(F32) + got_x[g].astype(F32)).astype(BF)
+    zs = [
+        start(push(half.at[xor(z_place, d, group)], got_z.at[d - 1], z_sems, d - 1, "dp", 2 * d)) for d in range(1, group)
+    ]
+
+    for copy in ys:
+        copy.wait_recv()
+    rows = 64
+    count = x_ref.shape[0] // rows
+    gain = gain_ref[...]
+
+    def norm(r, carry):
+        gain_term, shift_term = carry
+        at = pl.ds(pl.multiple_of(r * rows, rows), rows)
+        grad = token_sum[0, at, :].astype(F32)
+        for h in range(ranks // 2 - 1):
+            grad = grad + got_y[h, at, :].astype(F32)
+        x = x_ref[at, :].astype(F32)
+        centre = x - jnp.mean(x, axis=-1, keepdims=True)
+        scale = lax.rsqrt(jnp.mean(centre * centre, axis=-1, keepdims=True) + EPSILON)
+        unit = centre * scale
+        inside = grad * gain
+        first = jnp.mean(inside, axis=-1, keepdims=True)
+        second = jnp.mean(inside * unit, axis=-1, keepdims=True)
+        input_ref[at, :] = rest_ref[at, :] + scale * (inside - first - unit * second)
+        return (
+            gain_term + jnp.sum(grad * unit, axis=0, keepdims=True),
+            shift_term + jnp.sum(grad, axis=0, keepdims=True),
+        )
+
+    zero = jnp.zeros(gain.shape, F32)
+    gain_term, shift_term = lax.fori_loop(0, count, norm, (zero, zero))
+    terms[...] = early_ref[...]
+    terms[0:1, :] = gain_term
+    terms[4:5, :] = shift_term
+    ts = [start(push(terms, got_t.at[d - 1], t_sems, d - 1, "tensor", d)) for d in range(1, ranks)]
+    xs = [share(k, outs[k]) for k in range(pieces_count)]
+    for copy in zs:
+        copy.wait_recv()
+    own_piece[...] = tree_sum([half[z_place]] + [got_z[d] for d in range(group - 1)]).astype(BF)
+    spread(pieces_count, own_piece, qkv_out)
+    for copy in ts:
+        copy.wait_recv()
+    sum_t[...] = tree_sum([terms[...]] + [got_t[d] for d in range(ranks - 1)])
+    ds = [start(push(sum_t, got_d.at[d - 1], d_sems, d - 1, "dp", d)) for d in range(1, 2 * group)]
+    xs.append(share(pieces_count, qkv_out))
+    for copy in ds:
+        copy.wait_recv()
+    sums_ref[...] = tree_sum([sum_t[...]] + [got_d[d] for d in range(2 * group - 1)])
+    for copy in xs:
+        copy.wait_recv()
+    for copy in started:
+        copy.wait_send()
+
+
+def last_stage(block_rows, gain, rest, early, token_terms, qkv_terms, pieces):
+    block, width = block_rows.shape
+    ranks = token_terms.shape[0]
+    group = qkv_terms.shape[1]
+    vmem = pl.BlockSpec(memory_space=pltpu.VMEM)
+    copies = pltpu.SemaphoreType.DMA
+    count = len(pieces)
+    return pl.pallas_call(
+        functools.partial(last_kernel, ranks, count),
+        out_shape=[
+            jax.ShapeDtypeStruct((block, width), F32),
+            jax.ShapeDtypeStruct((8, width), F32),
+            jax.ShapeDtypeStruct(qkv_terms.shape, BF),
+        ]
+        + [jax.ShapeDtypeStruct((2, group, *piece.shape), BF) for piece in pieces],
+        in_specs=[vmem] * (6 + count),
+        out_specs=[vmem] * (3 + count),
+        scratch_shapes=[
+            pltpu.VMEM((ranks // 2, block, width), BF),
+            pltpu.VMEM((ranks // 2, block, width), BF),
+            pltpu.VMEM((ranks // 2 - 1, block, width), BF),
+            pltpu.VMEM((8, width), F32),
+            pltpu.VMEM((ranks - 1, 8, width), F32),
+            pltpu.VMEM((8, width), F32),
+            pltpu.VMEM((2 * group - 1, 8, width), F32),
+            pltpu.VMEM(qkv_terms.shape[1:], BF),
+            pltpu.VMEM(qkv_terms.shape[1:], BF),
+            pltpu.VMEM((group - 1, *qkv_terms.shape[2:]), BF),
+            pltpu.VMEM(qkv_terms.shape[2:], BF),
+            copies((2, ranks // 2)),
+            copies((2, ranks // 2 - 1)),
+            copies((2, ranks - 1)),
+            copies((2, 2 * group - 1)),
+            copies((2, 1)),
+            copies((2, group - 1)),
+            copies((2, (count + 1) * (group - 1))),
+            copies((2, count + 1)),
+        ],
+        compiler_params=pltpu.CompilerParams(vmem_limit_bytes=56 << 20, collective_id=1, has_side_effects=True),
+        name="last_stage",
+    )(block_rows, gain, rest, early, token_terms, qkv_terms, *pieces)
 
 
 def body(block_in, lengths, qkv_weight, out_weight, up_weight, down_weight, norm_gain, norm_bias, cotangent):
@@ -426,42 +642,39 @@
     hidden_own, gelu_own_pull = jax.vjp(jax.nn.gelu, upward_own)
     grad_hidden_own = dot(grad_mlp_full, down_weight, NT)
     grad_upward_own = gelu_own_pull(grad_hidden_own)[0].astype(BF)
-    down_grad = reduce_dp(dot(hidden_own.astype(BF), grad_mlp_full, TN), False)
-    up_grad = reduce_dp(dot(mlp_full, grad_upward_own, TN), False)
-
-    out_partial = dot(heads_local, grad_attn_low, TN)
-    out_terms = [out_partial[d * local : (d + 1) * local] for d in range(ranks)]
-    out_grad = reduce_dp(reduce_scatter_tensor(out_terms), False)
-
-    grad_project, qkv_grads = [], []
-    for pair in range(pairs):
-        parts = []
-        for d in range(ranks):
-            column = d * local + pair * PAIR
-            piece = grad_heads[:, column : column + PAIR]
-            parts.append(piece if d == 0 else swap(piece, "tensor", d))
-        got = jnp.concatenate(parts, axis=0)
-        grads = attend_backward(place, qkv, pair, got, heads_mixed[pair], logs[pair], start_row, cosine, sine, block)
-        grad_project += [grads[c] for c in range(3)]
-        wide = jnp.concatenate([grads[c] for c in range(3)], axis=1)
-        qkv_grads.append(reduce_dp(dot(attn_full, wide, TN), pair == pairs - 1))
-    order = [pair * 3 + c for c in range(3) for pair in range(pairs)]
-    grad_wide = jnp.concatenate([grad_project[i] for i in order], axis=1)
+    group = lax.axis_size("dp") // 2
+    down_term = dot(hidden_own.astype(BF), grad_mlp_full, TN).astype(BF)
+    up_term = dot(mlp_full, grad_upward_own, TN).astype(BF)
+
+    out_partial = dot(heads_local, grad_attn_low, TN).astype(BF)
+    shared = out_partial.reshape(ranks, 2, group, local // (2 * group), width)
+    terms = []
+    half_columns = width // 2
+    for term in (down_term, up_term):
+        cut = term.reshape(2, group, term.shape[0] // (2 * group), width)
+        terms += [cut[..., :half_columns], cut[..., half_columns:]]
+
+    grad_parts = jnp.stack(
+        [grad_heads[:, i * PAIR : (i + 1) * PAIR] for i in range(width // PAIR)], axis=0
+    )
+    grads, *pieces = attend_backward(
+        qkv, grad_parts, jnp.stack(heads_mixed), jnp.stack(logs), start_row, cosine, sine, shared, terms, block
+    )
+    wide = jnp.concatenate([grads[i] for i in range(3 * pairs)], axis=1)
     qkv_flat = qkv_weight.reshape(width, 3 * local)
-    terms = [
-        dot(grad_wide[d * block : (d + 1) * block], qkv_flat, NT) for d in range(ranks)
+    token_terms = dot(wide, qkv_flat, NT).astype(BF).reshape(ranks, block, width)
+    qkv_term = dot(attn_full, wide, TN).astype(BF).reshape(2, group, width // (2 * group), 3 * local)
+    early = jnp.stack([gain_one, gain_one, gain_two, gain_three, shift_one, shift_one, shift_two, shift_three])
+    input_grad, sums, qkv_sum, *wholes = last_stage(
+        block_in.reshape(block, width), norm_gain[0:1], grad_middle, early, token_terms, qkv_term, pieces
+    )
+    down_grad, up_grad = [
+        jnp.concatenate([left.reshape(-1, half_columns), right.reshape(-1, half_columns)], axis=1).astype(F32)
+        for left, right in (wholes[0:2], wholes[2:4])
     ]
-    grad_attn_norm = reduce_scatter_tensor(terms)
-    grad_from_first, gain_zero, shift_zero = attn_norm_pull(grad_attn_norm)
-    input_grad = grad_middle + grad_from_first
-
-    late = sum_all(jnp.stack([gain_zero, shift_zero]))
-    early = sum_all(jnp.stack([gain_one, gain_two, gain_three, shift_one, shift_two, shift_three]))
-    gain_grad = jnp.concatenate([late[0:1], early[0:3]], axis=0)
-    bias_grad = jnp.concatenate([late[1:2], early[3:6]], axis=0)
-    qkv_grad = jnp.stack(
-        [jnp.concatenate([g[:, c * PAIR : (c + 1) * PAIR] for g in qkv_grads], axis=1) for c in range(3)], axis=1
-    )
+    qkv_grad = qkv_sum.reshape(width, 3, local).astype(F32)
+    gain_grad, bias_grad = sums[0:4], sums[4:8]
+    out_grad = wholes[4].reshape(local, width).astype(F32)
     return (
         block_out.reshape(block_in.shape),
         input_grad.reshape(block_in.shape),

time: 639 us -> 538 us (0.84)
  waiting for transfers between devices: 263 us -> 97.1 us
  Pallas kernels: 85.2 us -> 243 us
  starting transfers between devices: 110 us -> 11.6 us
  local copies, waits for them, and re-layouts: 18.6 us -> 38.9 us
  other arithmetic: 46.4 us -> 33.2 us
    ppermute x102 -> x24, waiting for transfers between devices: 263 us -> 97.1 us  [swap(): return lax.ppermute(value, axis, [(i, i ^ offset) for i in range(size)])]
    pallas_call x2, Pallas kernels: 46.2 us -> 204 us  [the longest x1 119 us: last_stage(): pl.pallas_call(functools.partial(last_kernel, ranks, count), out_shape=[j...]
    ppermute x102 -> x24, starting transfers between devices: 110 us -> 11.6 us  [swap(): return lax.ppermute(value, axis, [(i, i ^ offset) for i in range(size)])]
    unnamed x123 -> x113, local copies, waits for them, and re-layouts: 13 us -> 28 us
    dot_general x24 -> x20, matrix products: 103 us -> 102 us  [dot(): return lax.dot_general(a, b, dims, preferred_element_type=F32)]
  transfers between devices with their start and end apart: 102 -> 24, of which waited for: 41 -> 7; matrix products, arithmetic and copies ran while one was open for 17% -> 15% of each run, Pallas kernels for 10% -> 7%
where the time goes in v2:
time: 538 us; the launch traced here: 527 us
  Pallas kernels  243 us (45%)
  matrix products  102 us (19%)
  waiting for transfers between devices  97.1 us (18%)
  local copies, waits for them, and re-layouts  38.9 us (7%)
  other arithmetic  33.2 us (6%)
  starting transfers between devices  11.6 us (2%)
    pallas_call x1, Pallas kernels, last_stage(): pl.pallas_call(functools.partial(last_kernel, ranks, count), out_shape=[j...  119 us
    dot_general x20, matrix products, dot(): return lax.dot_general(a, b, dims, preferred_element_type=F32)  102 us
    ppermute x24, waiting for transfers between devices, swap(): return lax.ppermute(value, axis, [(i, i ^ offset) for i in range(size)])  97.1 us
    pallas_call x1, Pallas kernels, attend_backward(): pl.pallas_call(functools.partial(backward_kernel, block, blocks, pairs, c...  85.5 us
    pallas_call x2, Pallas kernels, attend_forward(): pl.pallas_call(functools.partial(forward_kernel, block), out_shape=(jax.S...  33.9 us
    unnamed x113, local copies, waits for them, and re-layouts  28 us
    ppermute x24, starting transfers between devices, swap(): return lax.ppermute(value, axis, [(i, i ^ offset) for i in range(size)])  11.6 us
  transfers between devices with their start and end apart: 24, of which 7 were waited for; matrix products, arithmetic and copies ran while one was open for 15% of the time, Pallas kernels for 7%

profile of v2, /device:TPU:20, one launch (start us, length us, event | category | flops | bytes accessed | tf_op | source)
XLA Modules:
  0.0 527.3 jit_solution(7826887083788835736)
XLA Ops:
  2.5 1.5 convert_reduce_fusion
  4.0 1.6 fusion.17
  5.6 1.4 fusion.20
  8.0 24.3 %collective-permute-done.1 = bf16[512,1024]{1,0:T(8,128)(2,1)} collective-permute-done((bf16[512,1024]{1,0:T(8,128)(2,1)}, bf16[512,1024]{1,0:T(8,128)(2,1)}, u32[]{:S(2)}, u32[]{:S(2)}) %collective-permute-start.1) | collective-permute-done | bytes 1048608 | tf_op jit(solution)/shard_map/ppermute | solution.py:35
  33.4 5.6 %fusion.55 = (f32[2048,128]{1,0:T(8,128)}, f32[2048,128]{1,0:T(8,128)}) fusion(f32[128]{0:T(128)S(1)} %get-tuple-element.121, f32[128]{0:T(128)S(1)} %get-tuple-element.122, f32[2048]{0:T(1024)S(1)} %subtract_convert_fusion), kind=kLoop, calls=%fused_computation.99 | loop fusion | flops 524288 | bytes 2106368 | tf_op jit(solution)/shard_map/mul | solution.py:587
  39.3 1.8 copy.27
  41.1 1.6 convert_reduce_fusion.1
  42.7 1.6 collective-permute-start.15
  44.4 1.1 constant_dynamic-update-slice_fusion.8
  45.4 2.3 collective-permute-done.10
  47.7 1.1 constant_dynamic-update-slice_fusion.7
  48.9 2.6 pad_maximum_fusion.x_ref
  51.6 4.9 project_qkv.1.q_ref.k_ref.v_ref.refs_0_
  56.6 16.9 %attend_forward.3 = (bf16[2048,128]{1,0:T(8,128)(2,1)S(1)}, f32[8,2048]{1,0:T(8,128)S(1)}) custom-call(s32[1]{0:T(128)} %bitcast.1.place_ref, bf16[6,2048,128]{2,1,0:T(8,128)(2,1)S(1)} %project_qkv.1.q_ref.k_ref.v_ref.refs_0_, bf16[6,2048,128]{2,1,0:T(8,128)(2,1)S(1)} %project_qkv.1.q_ref.k_ref.v_ref.refs_0_, ...), custom_call_target="tpu_custom_call" | custom-call | flops 10737418240 | bytes 2097152 | tf_op jit(solution)/shard_map/attend_forward/pallas_call | solution.py:195
  73.5 17.0 %attend_forward.2 = (bf16[2048,128]{1,0:T(8,128)(2,1)S(1)}, f32[8,2048]{1,0:T(8,128)S(1)}) custom-call(s32[1]{0:T(128)} %bitcast.1.place_ref, bf16[6,2048,128]{2,1,0:T(8,128)(2,1)S(1)} %project_qkv.1.q_ref.k_ref.v_ref.refs_0_, bf16[6,2048,128]{2,1,0:T(8,128)(2,1)S(1)} %project_qkv.1.q_ref.k_ref.v_ref.refs_0_, ...), custom_call_target="tpu_custom_call" | custom-call | flops 10737418240 | bytes 2097152 | tf_op jit(solution)/shard_map/attend_forward/pallas_call | solution.py:195
  91.1 1.1 pad_maximum_fusion.3.refs_2_
  93.0 2.1 collective-permute-start.5
  95.2 1.0 collective-permute-start.6
  96.2 44.1 %collective-permute-done.5 = bf16[512,128]{1,0:T(8,128)(2,1)S(1)} collective-permute-done((bf16[512,128]{1,0:T(8,128)(2,1)S(1)}, bf16[512,128]{1,0:T(8,128)(2,1)S(1)}, u32[]{:S(2)}, u32[]{:S(2)}) %collective-permute-start.5) | collective-permute-done | bytes 131104 | tf_op jit(solution)/shard_map/ppermute | solution.py:35
  140.4 1.9 collective-permute-done.6
  142.3 3.1 collective-permute-done.7
  145.5 2.4 collective-permute-done.8
  147.9 1.4 fusion.173
  149.7 1.6 copy-done.7
  152.8 1.3 collective-permute-start.19
  154.1 1.3 fusion.183
  155.4 1.4 fusion.56
  157.0 1.3 fusion.185
  158.8 18.9 %collective-permute-done.19 = bf16[512,1024]{1,0:T(8,128)(2,1)S(1)} collective-permute-done((bf16[512,1024]{1,0:T(8,128)(2,1)S(1)}, bf16[512,1024]{1,0:T(8,128)(2,1)S(1)}, u32[]{:S(2)}, u32[]{:S(2)}) %collective-permute-start.19) | collective-permute-done | bytes 1048608 | tf_op jit(solution)/shard_map/ppermute | solution.py:35
  177.7 1.4 fusion.58
  179.8 1.3 fusion.184
  181.1 1.4 fusion.57
  183.1 11.1 %fusion.90 = f32[2048,1024]{1,0:T(8,128)} fusion(bf16[1024,1024]{1,0:T(8,128)(2,1)S(1)} %copy-done.30, bf16[512,1024]{1,0:T(8,128)(2,1)S(1)} %collective-permute-done.20, bf16[512,1024]{1,0:T(8,128)(2,1)S(1)} %collective-permute-done.19, bf16[512,1024]{1,0:T(8,128)(2,1)S(1)} %collective-permute-done.18, bf16[512,1024]{1,0:T(8,128)(2,1)S(1)} %add_convert_fusion.3), kind=kOutput, calls=%fused_computation.131 | convolution fusion | flops 4311744512 | bytes 14680064 | tf_op jit(solution)/shard_map/dot_general | solution.py:24
  194.3 1.3 fusion.186
  195.6 1.6 fusion.174
  199.7 1.9 fusion.164
  201.7 1.2 add_convert_fusion.1
  202.8 7.4 %fusion.87 = f32[512,1024]{1,0:T(8,128)} fusion(bf16[1024,1024]{1,0:T(8,128)(2,1)} %param.13, f32[512,1024]{1,0:T(8,128)} %copy-done.43, bf16[512,1024]{1,0:T(8,128)(2,1)} %add_convert_fusion.1, bf16[1024,1024]{1,0:T(8,128)(2,1)} %param.14), kind=kOutput, calls=%fused_computation.129 | convolution fusion | flops 2157969408 | bytes 9437184 | tf_op jit(solution)/shard_map/dot_general | solution.py:24
  210.3 1.6 collective-permute-start.22
  211.9 7.4 %fusion.83 = f32[512,1024]{1,0:T(8,128)} fusion(bf16[1024,1024]{1,0:T(8,128)(2,1)} %copy-done.34, f32[512,1024]{1,0:T(8,128)} %copy-done.42, bf16[512,1024]{1,0:T(8,128)(2,1)} %add_convert_fusion.1, bf16[1024,1024]{1,0:T(8,128)(2,1)} %copy-done.32), kind=kOutput, calls=%fused_computation.127 | convolution fusion | flops 2157969408 | bytes 9437184 | tf_op jit(solution)/shard_map/dot_general | solution.py:24
  219.2 7.6 %fusion.85 = f32[512,1024]{1,0:T(8,128)} fusion(bf16[1024,1024]{1,0:T(8,128)(2,1)} %copy-done.35, f32[512,1024]{1,0:T(8,128)} %copy-done.44, bf16[512,1024]{1,0:T(8,128)(2,1)} %add_convert_fusion.1, bf16[1024,1024]{1,0:T(8,128)(2,1)} %copy-done.33), kind=kOutput, calls=%fused_computation.128 | convolution fusion | flops 2157969408 | bytes 9437184 | tf_op jit(solution)/shard_map/dot_general | solution.py:24
  226.8 9.6 %multiply_reduce_fusion.1 = (f32[1024]{0:T(1024)S(1)}, f32[512]{0:T(512)S(1)}, f32[1024]{0:T(1024)S(1)}, f32[512,1024]{1,0:T(8,128)}) fusion(f32[512,1024]{1,0:T(8,128)S(1)} %get-tuple-element.90, f32[512]{0:T(512)S(1)} %fusion.100, f32[512]{0:T(512)S(1)} %broadcast_multiply_fusion.1, f32[1024]{0:T(1024)S(1)} %bitcast.180, ...), kind=kOutput, calls=%fused_computation.77 | convolution fusion | flops 2163734016 | bytes 17844224 | tf_op jit(solution)/shard_map/dot_general | solution.py:24
  236.5 2.4 fusion.163
  238.9 1.1 multiply_reduce_fusion
  241.3 1.0 copy-done.25
  242.4 1.3 convolution_convert_fusion.3
  250.4 4.0 convolution_convert_fusion.1
  254.4 10.1 %fusion.54 = bf16[1024,1024]{1,0:T(8,128)(2,1)S(1)} fusion(f32[2048,1024]{1,0:T(8,128)} %fusion.90, bf16[512,1024]{1,0:T(8,128)(2,1)S(1)} %collective-permute-done.23, bf16[512,1024]{1,0:T(8,128)(2,1)} %collective-permute-done.22, bf16[512,1024]{1,0:T(8,128)(2,1)} %collective-permute-done.21, bf16[512,1024]{1,0:T(8,128)(2,1)S(1)} %copy-done.17), kind=kOutput, calls=%fused_computation.94 | convolution fusion | flops 4331667456 | bytes 14680064 | tf_op jit(solution)/shard_map/dot_general | solution.py:24
  264.5 1.6 fusion.167
  266.1 18.8 %fusion.51 = bf16[1024,1024]{1,0:T(8,128)(2,1)S(1)} fusion(f32[2048,1024]{1,0:T(8,128)} %fusion.90, bf16[1024,1024]{1,0:T(8,128)(2,1)} %param.14, bf16[512,1024]{1,0:T(8,128)(2,1)} %copy-done.40, bf16[512,1024]{1,0:T(8,128)(2,1)} %collective-permute-done.22, bf16[512,1024]{1,0:T(8,128)(2,1)} %collective-permute-done.21, ...), kind=kOutput, calls=%fused_computation.93 | convolution fusion | flops 8666480640 | bytes 20971520 | tf_op jit(solution)/shard_map/dot_general | solution.py:24
  284.9 1.6 fusion.166
  286.5 85.5 %attend_backward.1 = (bf16[6,2048,128]{2,1,0:T(8,128)(2,1)}, bf16[128,512]{1,0:T(8,128)(2,1)}, bf16[128,512]{1,0:T(8,128)(2,1)}, bf16[128,512]{1,0:T(8,128)(2,1)...) custom-call(bf16[6,2048,128]{2,1,0:T(8,128)(2,1)} %copy-done.3, bf16[8,512,128]{2,1,0:T(8,128)(2,1)} %fusion.91.refs_1_, ...), custom_call_target="tpu_custom_call" | custom-call | flops 53687091200 | bytes 8388608 | tf_op jit(solution)/shard_map/attend_backward/pallas_call | solution.py:383
  372.1 1.3 bitcast_dynamic-update-slice_fusion.5
  373.4 1.2 bitcast_dynamic-update-slice_fusion.4
  374.6 1.3 bitcast_dynamic-update-slice_fusion.3
  376.3 5.1 convolution_convert_fusion
  381.4 6.9 %convolution_convert_fusion.2 = bf16[1024,768]{1,0:T(8,128)(2,1)} fusion(bf16[2048,768]{1,0:T(8,128)(2,1)S(1)} %bitcast_dynamic-update-slice_fusion, bf16[512,1024]{1,0:T(8,128)(2,1)} %collective-permute-done.2, bf16[512,1024]{1,0:T(8,128)(2,1)} %collective-permute-done.1, bf16[512,1024]{1,0:T(8,128)(2,1)} %collective-permute-done, ...), kind=kOutput, calls=%fused_computation.95 | convolution fusion | flops 3238789120 | bytes 8912896 | tf_op jit(solution)/shard_map/dot_general | solution.py:24
  388.3 118.9 %last_stage.1 = (f32[512,1024]{1,0:T(8,128)}, f32[8,1024]{1,0:T(8,128)}, bf16[2,4,128,768]{3,2,1,0:T(8,128)(2,1)}, bf16[2,4,128,512]{3,2,1,0:T(8,128)(2,1)}, bf1...) custom-call(bf16[512,1024]{1,0:T(8,128)(2,1)} %bitcast.156, ...), custom_call_target="tpu_custom_call" | custom-call | tf_op jit(solution)/shard_map/last_stage/pallas_call | solution.py:520
  507.2 5.2 copy.29
  512.4 3.2 reshape.252
  515.6 4.6 copy.30
  520.2 1.1 bitcast_convert_fusion
  521.9 2.6 maximum_convert_fusion
  524.5 2.6 maximum_convert_fusion.1
  (178 shorter events, 21.3 us)
Async XLA Ops:
  0.6 5.0 copy-start.6
  2.4 4.6 copy-start.27
  2.4 5.1 copy-start.41
  2.4 29.8 %copy-start.23 = (bf16[256,1024]{1,0:T(8,128)(2,1)S(1)}, bf16[256,1024]{1,0:T(8,128)(2,1)}, u32[]{:S(2)}) copy-start(bf16[256,1024]{1,0:T(8,128)(2,1)} %param.12) | copy-start | bytes 1572868
  7.0 32.3 %copy-start = (bf16[1024,3,256]{2,0,1:T(8,128)(2,1)S(1)}, bf16[1024,3,256]{2,0,1:T(8,128)(2,1)}, u32[]{:S(2)}) copy-start(bf16[1024,3,256]{2,0,1:T(8,128)(2,1)} %param.11) | copy-start | bytes 4718596
  7.0 25.2 %collective-permute-start.1 = (bf16[512,1024]{1,0:T(8,128)(2,1)}, bf16[512,1024]{1,0:T(8,128)(2,1)}, u32[]{:S(2)}, u32[]{:S(2)}) collective-permute-start(bf16[512,1024]{1,0:T(8,128)(2,1)} %fusion.20), channel_id=1, source_target_pairs={{0,2},{1,3},{2,0},{3,1},{4,6},{5,7},{6,4},{7,5},{8,10},{9,11},{10,... | collective-permute-start | bytes 3145736 | tf_op jit(solution)/shard_map/ppermute | solution.py:35
  7.5 41.3 %collective-permute-start = (bf16[512,1024]{1,0:T(8,128)(2,1)}, bf16[512,1024]{1,0:T(8,128)(2,1)}, u32[]{:S(2)}, u32[]{:S(2)}) collective-permute-start(bf16[512,1024]{1,0:T(8,128)(2,1)} %fusion.20), channel_id=1, source_target_pairs={{0,1},{1,0},{2,3},{3,2},{4,5},{5,4},{6,7},{7,6},{8,9},{9,8},{10,11... | collective-permute-start | bytes 3145736 | tf_op jit(solution)/shard_map/ppermute | solution.py:35
  7.9 33.2 %copy-start.26 = (s32[2048]{0:T(1024)}, s32[2048]{0:T(1024)S(1)}, u32[]{:S(2)}) copy-start(s32[2048]{0:T(1024)S(1)} %select_reduce_fusion) | copy-start | bytes 24580
  32.3 16.7 %collective-permute-start.2 = (bf16[512,1024]{1,0:T(8,128)(2,1)}, bf16[512,1024]{1,0:T(8,128)(2,1)}, u32[]{:S(2)}, u32[]{:S(2)}) collective-permute-start(bf16[512,1024]{1,0:T(8,128)(2,1)} %collective-permute-done.1), channel_id=1, source_target_pairs={{0,1},{1,0},{2,3},{3,2},{4,5},{5,4},{6,7},{7,6},{8,9},{9,8},{10,11... | collective-permute-start | bytes 3145736 | tf_op jit(solution)/shard_map/ppermute | solution.py:35
  32.3 12.0 %collective-permute-start.9 = (bf16[256,1024]{1,0:T(8,128)(2,1)S(1)}, bf16[256,1024]{1,0:T(8,128)(2,1)}, u32[]{:S(2)}, u32[]{:S(2)}) collective-permute-start(bf16[256,1024]{1,0:T(8,128)(2,1)S(1)} %copy-done.23), channel_id=1, source_target_pairs={{0,1},{1,0},{2,3},{3,2},{4,5},{5,4},{6,7},{7,6},{8,9},{9,8},{10,11... | collective-permute-start | bytes 1572872 | tf_op jit(solution)/shard_map/ppermute | solution.py:35
  32.8 14.9 %collective-permute-start.10 = (bf16[256,1024]{1,0:T(8,128)(2,1)S(1)}, bf16[256,1024]{1,0:T(8,128)(2,1)}, u32[]{:S(2)}, u32[]{:S(2)}) collective-permute-start(bf16[256,1024]{1,0:T(8,128)(2,1)S(1)} %copy-done.23), channel_id=1, source_target_pairs={{0,2},{1,3},{2,0},{3,1},{4,6},{5,7},{6,4},{7,5},{8,10},{9,11},{10,... | collective-permute-start | bytes 1572872 | tf_op jit(solution)/shard_map/ppermute | solution.py:35
  41.1 6.6 %copy-start.30 = (bf16[1024,1024]{1,0:T(8,128)(2,1)S(1)}, bf16[1024,1024]{1,0:T(8,128)(2,1)}, u32[]{:S(2)}) copy-start(bf16[1024,1024]{1,0:T(8,128)(2,1)} %param.13) | copy-start | bytes 6291460
  42.7 115.6 %collective-permute-start.15 = (bf16[1024,1024]{1,0:T(8,128)(2,1)}, bf16[1024,1024]{1,0:T(8,128)(2,1)S(1)}, u32[]{:S(2)}, u32[]{:S(2)}) collective-permute-start(bf16[1024,1024]{1,0:T(8,128)(2,1)} %param.14), channel_id=1, source_target_pairs={{0,2},{1,3},{2,0},{3,1},{4,6},{5,7},{6,4},{7,5},{8,10},{9,11},{10,... | collective-permute-start | bytes 6291464 | tf_op jit(solution)/shard_map/ppermute | solution.py:35
  44.3 136.8 %collective-permute-start.13 = (bf16[1024,1024]{1,0:T(8,128)(2,1)}, bf16[1024,1024]{1,0:T(8,128)(2,1)S(1)}, u32[]{:S(2)}, u32[]{:S(2)}) collective-permute-start(bf16[1024,1024]{1,0:T(8,128)(2,1)} %param.14), channel_id=1, source_target_pairs={{0,1},{1,0},{2,3},{3,2},{4,5},{5,4},{6,7},{7,6},{8,9},{9,8},{10,11... | collective-permute-start | bytes 6291464 | tf_op jit(solution)/shard_map/ppermute | solution.py:35
  47.7 109.1 %collective-permute-start.14 = (bf16[1024,1024]{1,0:T(8,128)(2,1)S(1)}, bf16[1024,1024]{1,0:T(8,128)(2,1)S(1)}, u32[]{:S(2)}, u32[]{:S(2)}) collective-permute-start(bf16[1024,1024]{1,0:T(8,128)(2,1)S(1)} %copy-done.30), channel_id=1, source_target_pairs={{0,2},{1,3},{2,0},{3,1},{4,6},{5,7},{6,4},{7,5},{8,10},{9,11},{10,... | collective-permute-start | bytes 6291464 | tf_op jit(solution)/shard_map/ppermute | solution.py:35
  48.8 2.7 copy-start.1
  48.8 2.8 copy-start.2
  48.8 44.0 %collective-permute-start.11 = (bf16[256,1024]{1,0:T(8,128)(2,1)}, bf16[256,1024]{1,0:T(8,128)(2,1)S(1)}, u32[]{:S(2)}, u32[]{:S(2)}) collective-permute-start(bf16[256,1024]{1,0:T(8,128)(2,1)} %collective-permute-done.10), channel_id=1, source_target_pairs={{0,1},{1,0},{2,3},{3,2},{4,5},{5,4},{6,7},{7,6},{8,9},{9,8},{10,11... | collective-permute-start | bytes 1572872 | tf_op jit(solution)/shard_map/ppermute | solution.py:35
  56.6 16.9 %copy-start.3 = (bf16[6,2048,128]{2,1,0:T(8,128)(2,1)}, bf16[6,2048,128]{2,1,0:T(8,128)(2,1)S(1)}, u32[]{:S(2)}) copy-start(bf16[6,2048,128]{2,1,0:T(8,128)(2,1)S(1)} %project_qkv.1.q_ref.k_ref.v_ref.refs_0_) | copy-start | bytes 9437188
  90.6 2.4 collective-permute-start.3
  92.8 2.3 collective-permute-start.4
  93.0 56.3 %copy-start.24 = (bf16[1024,1024]{1,0:T(8,128)(2,1)}, bf16[1024,1024]{1,0:T(8,128)(2,1)S(1)}, u32[]{:S(2)}) copy-start(bf16[1024,1024]{1,0:T(8,128)(2,1)S(1)} %constant_dynamic-update-slice_fusion.6) | copy-start | bytes 6291460
  93.0 47.3 %collective-permute-start.5 = (bf16[512,128]{1,0:T(8,128)(2,1)S(1)}, bf16[512,128]{1,0:T(8,128)(2,1)S(1)}, u32[]{:S(2)}, u32[]{:S(2)}) collective-permute-start(bf16[512,128]{1,0:T(8,128)(2,1)S(1)} %get-tuple-element.101), channel_id=1, source_target_pairs={{0,2},{1,3},{2,0},{3,1},{4,6},{5,7},{6,4},{7,5},{8,10},{9,11},{10,... | collective-permute-start | bytes 393224 | tf_op jit(solution)/shard_map/ppermute | solution.py:35
  95.2 47.1 %collective-permute-start.6 = (bf16[512,128]{1,0:T(8,128)(2,1)S(1)}, bf16[512,128]{1,0:T(8,128)(2,1)S(1)}, u32[]{:S(2)}, u32[]{:S(2)}) collective-permute-start(bf16[512,128]{1,0:T(8,128)(2,1)S(1)} %get-tuple-element.97), channel_id=1, source_target_pairs={{0,2},{1,3},{2,0},{3,1},{4,6},{5,7},{6,4},{7,5},{8,10},{9,11},{10,... | collective-permute-start | bytes 393224 | tf_op jit(solution)/shard_map/ppermute | solution.py:35
  140.3 5.1 collective-permute-start.7
  142.3 5.6 %collective-permute-start.8 = (bf16[512,128]{1,0:T(8,128)(2,1)S(1)}, bf16[512,128]{1,0:T(8,128)(2,1)S(1)}, u32[]{:S(2)}, u32[]{:S(2)}) collective-permute-start(bf16[512,128]{1,0:T(8,128)(2,1)S(1)} %get-tuple-element.96), channel_id=1, source_target_pairs={{0,3},{1,2},{2,1},{3,0},{4,7},{5,6},{6,5},{7,4},{8,11},{9,10},{10,... | collective-permute-start | bytes 393224 | tf_op jit(solution)/shard_map/ppermute | solution.py:35
  145.4 33.7 %collective-permute-start.12 = (bf16[1024,1024]{1,0:T(8,128)(2,1)S(1)}, bf16[1024,1024]{1,0:T(8,128)(2,1)S(1)}, u32[]{:S(2)}, u32[]{:S(2)}) collective-permute-start(bf16[1024,1024]{1,0:T(8,128)(2,1)S(1)} %copy-done.30), channel_id=1, source_target_pairs={{0,1},{1,0},{2,3},{3,2},{4,5},{5,4},{6,7},{7,6},{8,9},{9,8},{10,11... | collective-permute-start | bytes 6291464 | tf_op jit(solution)/shard_map/ppermute | solution.py:35
  149.3 2.7 copy-start.4
  149.3 2.0 copy-start.7
  152.8 41.5 %copy-start.15 = (bf16[512,1024]{1,0:T(8,128)(2,1)}, bf16[512,1024]{1,0:T(8,128)(2,1)S(1)}, u32[]{:S(2)}) copy-start(bf16[512,1024]{1,0:T(8,128)(2,1)S(1)} %add_convert_fusion.3) | copy-start | bytes 3145732
  152.8 2.6 copy-start.31
  152.8 24.9 %collective-permute-start.19 = (bf16[512,1024]{1,0:T(8,128)(2,1)S(1)}, bf16[512,1024]{1,0:T(8,128)(2,1)S(1)}, u32[]{:S(2)}, u32[]{:S(2)}) collective-permute-start(bf16[512,1024]{1,0:T(8,128)(2,1)S(1)} %add_convert_fusion.3), channel_id=1, source_target_pairs={{0,2},{1,3},{2,0},{3,1},{4,6},{5,7},{6,4},{7,5},{8,10},{9,11},{10,... | collective-permute-start | bytes 3145736 | tf_op jit(solution)/shard_map/ppermute | solution.py:35
  155.4 1.4 copy-start.43
  156.9 26.2 %collective-permute-start.18 = (bf16[512,1024]{1,0:T(8,128)(2,1)S(1)}, bf16[512,1024]{1,0:T(8,128)(2,1)S(1)}, u32[]{:S(2)}, u32[]{:S(2)}) collective-permute-start(bf16[512,1024]{1,0:T(8,128)(2,1)S(1)} %add_convert_fusion.3), channel_id=1, source_target_pairs={{0,1},{1,0},{2,3},{3,2},{4,5},{5,4},{6,7},{7,6},{8,9},{9,8},{10,11... | collective-permute-start | bytes 3145736 | tf_op jit(solution)/shard_map/ppermute | solution.py:35
  158.2 20.9 %copy-start.42 = (f32[512,1024]{1,0:T(8,128)}, f32[512,1024]{1,0:T(8,128)S(1)}, u32[]{:S(2)}) copy-start(f32[512,1024]{1,0:T(8,128)S(1)} %fusion.185) | copy-start | bytes 6291460
  158.3 20.9 %copy-start.32 = (bf16[1024,1024]{1,0:T(8,128)(2,1)}, bf16[1024,1024]{1,0:T(8,128)(2,1)S(1)}, u32[]{:S(2)}) copy-start(bf16[1024,1024]{1,0:T(8,128)(2,1)S(1)} %collective-permute-done.15) | copy-start | bytes 6291460
  158.3 36.0 %collective-permute-start.16 = (bf16[1024,1024]{1,0:T(8,128)(2,1)S(1)}, bf16[1024,1024]{1,0:T(8,128)(2,1)S(1)}, u32[]{:S(2)}, u32[]{:S(2)}) collective-permute-start(bf16[1024,1024]{1,0:T(8,128)(2,1)S(1)} %collective-permute-done.14), channel_id=1, source_target_pairs={{0,1},{1,0},{2,3},{3,2},{4,5},{5,4},{6,7},{7,6},{8,9},{9,8},{10,11... | collective-permute-start | bytes 6291464 | tf_op jit(solution)/shard_map/ppermute | solution.py:35
  177.7 5.4 %copy-start.37 = (bf16[512,1024]{1,0:T(8,128)(2,1)}, bf16[512,1024]{1,0:T(8,128)(2,1)S(1)}, u32[]{:S(2)}) copy-start(bf16[512,1024]{1,0:T(8,128)(2,1)S(1)} %collective-permute-done.19) | copy-start | bytes 3145732
  177.7 5.4 %collective-permute-start.20 = (bf16[512,1024]{1,0:T(8,128)(2,1)S(1)}, bf16[512,1024]{1,0:T(8,128)(2,1)S(1)}, u32[]{:S(2)}, u32[]{:S(2)}) collective-permute-start(bf16[512,1024]{1,0:T(8,128)(2,1)S(1)} %collective-permute-done.19), channel_id=1, source_target_pairs={{0,1},{1,0},{2,3},{3,2},{4,5},{5,4},{6,7},{7,6},{8,9},{9,8},{10,11... | collective-permute-start | bytes 3145736 | tf_op jit(solution)/shard_map/ppermute | solution.py:35
  179.2 1.8 copy-start.35
  179.2 16.4 %collective-permute-start.17 = (bf16[1024,1024]{1,0:T(8,128)(2,1)S(1)}, bf16[1024,1024]{1,0:T(8,128)(2,1)S(1)}, u32[]{:S(2)}, u32[]{:S(2)}) collective-permute-start(bf16[1024,1024]{1,0:T(8,128)(2,1)S(1)} %collective-permute-done.15), channel_id=1, source_target_pairs={{0,1},{1,0},{2,3},{3,2},{4,5},{5,4},{6,7},{7,6},{8,9},{9,8},{10,11... | collective-permute-start | bytes 6291464 | tf_op jit(solution)/shard_map/ppermute | solution.py:35
  181.0 1.5 copy-start.44
  181.1 2.0 copy-start.33
  183.1 11.2 %copy-start.38 = (bf16[512,1024]{1,0:T(8,128)(2,1)}, bf16[512,1024]{1,0:T(8,128)(2,1)S(1)}, u32[]{:S(2)}) copy-start(bf16[512,1024]{1,0:T(8,128)(2,1)S(1)} %collective-permute-done.18) | copy-start | bytes 3145732
  183.1 11.1 %copy-start.39 = (bf16[512,1024]{1,0:T(8,128)(2,1)}, bf16[512,1024]{1,0:T(8,128)(2,1)S(1)}, u32[]{:S(2)}) copy-start(bf16[512,1024]{1,0:T(8,128)(2,1)S(1)} %collective-permute-done.20) | copy-start | bytes 3145732
  195.6 1.7 copy-start.12
  195.6 2.0 copy-start.11
  210.3 37.6 %collective-permute-start.22 = (bf16[512,1024]{1,0:T(8,128)(2,1)}, bf16[512,1024]{1,0:T(8,128)(2,1)}, u32[]{:S(2)}, u32[]{:S(2)}) collective-permute-start(bf16[512,1024]{1,0:T(8,128)(2,1)} %add_convert_fusion.1), channel_id=1, source_target_pairs={{0,2},{1,3},{2,0},{3,1},{4,6},{5,7},{6,4},{7,5},{8,10},{9,11},{10,... | collective-permute-start | bytes 3145736 | tf_op jit(solution)/shard_map/ppermute | solution.py:35
  211.9 42.5 %collective-permute-start.21 = (bf16[512,1024]{1,0:T(8,128)(2,1)}, bf16[512,1024]{1,0:T(8,128)(2,1)}, u32[]{:S(2)}, u32[]{:S(2)}) collective-permute-start(bf16[512,1024]{1,0:T(8,128)(2,1)} %add_convert_fusion.1), channel_id=1, source_target_pairs={{0,1},{1,0},{2,3},{3,2},{4,5},{5,4},{6,7},{7,6},{8,9},{9,8},{10,11... | collective-permute-start | bytes 3145736 | tf_op jit(solution)/shard_map/ppermute | solution.py:35
  236.5 2.4 copy-start.5
  240.0 2.3 copy-start.25
  247.8 6.6 %collective-permute-start.23 = (bf16[512,1024]{1,0:T(8,128)(2,1)}, bf16[512,1024]{1,0:T(8,128)(2,1)S(1)}, u32[]{:S(2)}, u32[]{:S(2)}) collective-permute-start(bf16[512,1024]{1,0:T(8,128)(2,1)} %collective-permute-done.22), channel_id=1, source_target_pairs={{0,1},{1,0},{2,3},{3,2},{4,5},{5,4},{6,7},{7,6},{8,9},{9,8},{10,11... | collective-permute-start | bytes 3145736 | tf_op jit(solution)/shard_map/ppermute | solution.py:35
  250.4 4.0 copy-start.17
  254.4 10.1 %copy-start.40 = (bf16[512,1024]{1,0:T(8,128)(2,1)}, bf16[512,1024]{1,0:T(8,128)(2,1)S(1)}, u32[]{:S(2)}) copy-start(bf16[512,1024]{1,0:T(8,128)(2,1)S(1)} %collective-permute-done.23) | copy-start | bytes 3145732
  264.5 1.6 copy-start.16
  372.1 3.8 copy-start.10
  374.5 1.7 copy-start.13
  507.2 5.2 copy-start.14
  515.6 4.6 copy-start.22
  515.6 5.7 %copy-start.28 = (f32[8,1024]{1,0:T(8,128)S(1)}, f32[8,1024]{1,0:T(8,128)}, u32[]{:S(2)}) copy-start(f32[8,1024]{1,0:T(8,128)} %get-tuple-element.49) | copy-start | bytes 98308
  515.6 6.3 %copy-start.21 = (bf16[2,4,128,512]{3,2,1,0:T(8,128)(2,1)S(1)}, bf16[2,4,128,512]{3,2,1,0:T(8,128)(2,1)}, u32[]{:S(2)}) copy-start(bf16[2,4,128,512]{3,2,1,0:T(8,128)(2,1)} %get-tuple-element.46) | copy-start | bytes 3145732
  520.1 1.7 copy-start.20
  521.9 2.6 copy-start.18
  521.9 2.6 copy-start.19
  (5 other events, 6.6 us)

commit v3 on v2

--- a/solution.py
+++ b/solution.py
@@ -100,123 +100,288 @@
     return values * cosine + other * signed_sine
 
 
-def qkv_kernel(pairs, place_ref, x_ref, w_ref, cos_ref, sin_ref, out_ref):
-    x = x_ref[...]
-    for part in range(3):
-        project = dot(x, w_ref[part])
-        for pair in range(pairs):
-            piece = project[:, pair * PAIR : (pair + 1) * PAIR]
-            if part < 2:
-                piece = turn(piece, cos_ref[...], sin_ref[...])
-            out_ref[part * pairs + pair] = piece.astype(BF)
-
-
-def project_qkv(place, tokens, weight, cosine, sine, block):
-    length, width = tokens.shape
-    columns = weight.shape[2]
-    pairs = columns // PAIR
-    real = lambda d, place: (d ^ place[0], 0)
-    return pl.pallas_call(
-        functools.partial(qkv_kernel, pairs),
-        out_shape=jax.ShapeDtypeStruct((3 * pairs, length, PAIR), BF),
-        grid_spec=pltpu.PrefetchScalarGridSpec(
-            num_scalar_prefetch=1,
-            grid=(length // block,),
-            in_specs=[
-                pl.BlockSpec((block, width), lambda d, place: (d, 0)),
-                pl.BlockSpec((3, width, columns), lambda d, place: (0, 0, 0)),
-                pl.BlockSpec((block, PAIR), real),
-                pl.BlockSpec((block, PAIR), real),
-            ],
-            out_specs=pl.BlockSpec((3 * pairs, block, PAIR), lambda d, place: (0, d, 0)),
-        ),
-        compiler_params=pltpu.CompilerParams(vmem_limit_bytes=40 << 20),
-        cost_estimate=pl.CostEstimate(flops=2 * length * width * 3 * columns, bytes_accessed=2 * length * width, transcendentals=0),
-        name="project_qkv",
-    )(place, tokens, weight, cosine, sine)
-
-
 def head_mask(shape, head):
     lane = lax.broadcasted_iota(jnp.int32, shape, 1)
     return lane // HD == head
 
 
-def forward_kernel(block, place_ref, q_ref, k_ref, v_ref, start_ref, out_ref, log_ref, scores_ref):
-    mine = place_ref[0]
-    row_block = pl.program_id(0) ^ mine
-    queries = q_ref[...] * HD**-0.5
-    start = start_ref[...]
-    mixed = None
-    for head in range(PAIR // HD):
-        mask = head_mask(queries.shape, head)
-        query = jnp.where(mask, queries, jnp.zeros_like(queries))
-
-        def score(j, top, last):
-            keys = k_ref[pl.ds(pl.multiple_of((j ^ mine) * block, block), block), :]
-            s = dot(query, keys, NT)
-            column = lax.broadcasted_iota(jnp.int32, s.shape, 1)
-            visible = column >= start - j * block
-            if last:
-                visible &= column <= lax.broadcasted_iota(jnp.int32, s.shape, 0)
-            s = jnp.where(visible, s, NEG)
-            scores_ref[j] = s
-            for c in range(0, block, 128):
-                top = jnp.maximum(top, s[:, c : c + 128])
-            return top
-
-        top = jnp.full((block, 128), NEG, F32)
-        top = lax.fori_loop(0, row_block, lambda j, top: score(j, top, False), top)
-        top = score(row_block, top, True)
-        top = jnp.max(top, axis=1, keepdims=True)
-
-        def mix(j, carry):
-            total, acc = carry
-            weights = jnp.exp(scores_ref[j] - top)
-            for c in range(0, block, 128):
-                total = total + weights[:, c : c + 128]
-            values = v_ref[pl.ds(pl.multiple_of((j ^ mine) * block, block), block), :]
-            return total, acc + dot(weights.astype(BF), values)
-
-        total, acc = lax.fori_loop(
-            0, row_block + 1, mix, (jnp.zeros((block, 128), F32), jnp.zeros((block, PAIR), F32))
+def forward_kernel(block, ranks, pairs, chunks, *refs):
+    x_ref, gain_ref, shift_ref, w_ref, cos_ref, sin_ref, start_ref, *refs = refs
+    weights, refs = refs[:3], refs[3:]
+    qkv_ref, attn_ref, mixed_ref, log_ref, heads_ref, *refs = refs
+    rests, refs = refs[:3], refs[3:]
+    scores_ref, attn_sems, head_sems, own_sems, y_sems, z_sems, x_sems, core_sems = refs
+
+    mine = lax.axis_index("tensor")
+    rank = lax.axis_index("dp")
+    group = lax.axis_size("dp") // 2
+    x_bit, z_place = lax.rem(rank, 2), lax.div(rank, 2)
+    length = block * ranks
+    started = []
+
+    def start(copy):
+        copy.start()
+        started.append(copy)
+        return copy
+
+    def cut(array, c, *lead):
+        at, (_, low, size) = array.at, chunks[c]
+        return at[(*lead, slice(None), pl.ds(low, size))]
+
+    def every(array, c, *lead):
+        at, (_, low, size) = array.at, chunks[c]
+        return at[(*lead, slice(None), slice(None), pl.ds(low, size))]
+
+    def rest(c):
+        return rests[chunks[c][0]]
+
+    y_copies = [
+        push(
+            cut(weights[chunks[c][0]], c, x_bit, z_place), cut(rest(c), c, 1, x_bit, z_place), y_sems, c, "tensor", 2
         )
-        total = jnp.sum(total, axis=1, keepdims=True)
-        acc = acc / total
-        mixed = acc if mixed is None else jnp.where(mask, acc, mixed)
-        logs = jnp.broadcast_to(top + jnp.log(total), (block, 128))
-        log_ref[head : head + 1, :] = jnp.transpose(logs)[0:1, :]
-    out_ref[...] = mixed.astype(BF)
-
-
-def attend_forward(place, qkv, pair, starts, block):
-    pairs3, length, _ = qkv.shape
-    pairs = pairs3 // 3
-    blocks = length // block
-    return pl.pallas_call(
-        functools.partial(forward_kernel, block),
-        out_shape=(
-            jax.ShapeDtypeStruct((length, PAIR), BF),
-            jax.ShapeDtypeStruct((8, length), F32),
-        ),
-        grid_spec=pltpu.PrefetchScalarGridSpec(
-            num_scalar_prefetch=1,
-            grid=(blocks,),
-            in_specs=[
-                pl.BlockSpec((None, block, PAIR), lambda d, place: (pair, d, 0)),
-                pl.BlockSpec((None, length, PAIR), lambda d, place: (pairs + pair, 0, 0)),
-                pl.BlockSpec((None, length, PAIR), lambda d, place: (2 * pairs + pair, 0, 0)),
-                pl.BlockSpec((block, 1), lambda d, place: (d ^ place[0], 0)),
-            ],
-            out_specs=(
-                pl.BlockSpec((block, PAIR), lambda d, place: (d, 0)),
-                pl.BlockSpec((8, block), lambda d, place: (0, d)),
-            ),
-            scratch_shapes=[pltpu.VMEM((blocks, block, block), F32)],
-        ),
-        compiler_params=pltpu.CompilerParams(vmem_limit_bytes=40 << 20),
-        cost_estimate=pl.CostEstimate(flops=20 * length * length * PAIR, bytes_accessed=4 * length * PAIR * 2, transcendentals=length * length),
+        for c in range(len(chunks))
+    ]
+    z_copies = [
+        [
+            push(
+                cut(rest(c), c, 1, x_bit, z_place),
+                cut(rest(c), c, 1, x_bit, z_place),
+                z_sems,
+                c * (group - 1) + d - 1,
+                "dp",
+                2 * d,
+            )
+            for d in range(1, group)
+        ]
+        for c in range(len(chunks))
+    ]
+    x_copies = [
+        push(every(rest(c), c, 1, x_bit), every(rest(c), c, 1, x_bit), x_sems, c, "dp", 1) for c in range(len(chunks))
+    ]
+    core_copies = [
+        push(
+            rest(c).at[1, :, :, :, pl.ds(chunks[c][1], chunks[c][2])],
+            rest(c).at[2, :, :, :, pl.ds(chunks[c][1], chunks[c][2])],
+            core_sems,
+            c,
+            "tensor",
+            1,
+        )
+        for c in range(len(chunks))
+    ]
+    own_copies = [push(weights[a], rests[a].at[0], own_sems, a, "tensor", 1) for a in range(3)]
+
+    def to_z(c):
+        y_copies[c].wait_recv()
+        for copy in z_copies[c]:
+            copy.start()
+
+    def to_x(c):
+        for copy in z_copies[c]:
+            copy.wait_recv()
+        x_copies[c].start()
+
+    def to_core(c):
+        x_copies[c].wait_recv()
+        core_copies[c].start()
+
+    greet(("tensor", "dp"))
+    early = len(chunks) - 2
+    for c in range(early):
+        y_copies[c].start()
+
+    strips = 4
+    strip = block // strips
+    gain, shift = gain_ref[...], shift_ref[...]
+    across, beside, onward = [], [], []
+    for q in range(strips):
+
+        @pl.loop(0, strip // 64)
+        def _(r):
+            at = pl.ds(pl.multiple_of(q * strip + r * 64, 64), 64)
+            attn_ref[0, at, :] = layer_norm(x_ref[at, :].astype(F32), gain, shift).astype(BF)
+
+        at = pl.ds(q * strip, strip)
+        across.append(start(push(attn_ref.at[0, at], attn_ref.at[2, at], attn_sems, q, "tensor", 2)))
+        beside.append(start(push(attn_ref.at[0, at], attn_ref.at[1, at], attn_sems, strips + q, "tensor", 1)))
+        onward.append(push(attn_ref.at[2, at], attn_ref.at[3, at], attn_sems, 2 * strips + q, "tensor", 1))
+
+    def middle():
+        for c in range(early):
+            to_z(c)
+        for q in range(strips):
+            across[q].wait_recv()
+            onward[q].start()
+        for c in range(early, len(chunks)):
+            y_copies[c].start()
+        for copy in own_copies:
+            copy.start()
+        for c in range(early - 1):
+            to_x(c)
+
+    def beside_here():
+        for copy in beside:
+            copy.wait_recv()
+
+    def onward_here():
+        for copy in onward:
+            copy.wait_recv()
+
+    @pl.loop(0, ranks)
+    def _(d):
+        pl.when(d == 1)(beside_here)
+        pl.when(d == 2)(middle)
+        pl.when(d == 3)(onward_here)
+        x = attn_ref[d]
+        rows = pl.ds(pl.multiple_of(d * block, block), block)
+        real = pl.ds(pl.multiple_of(xor(d, mine, ranks) * block, block), block)
+        for part in range(3):
+            project = dot(x, w_ref[part])
+            for pair in range(pairs):
+                piece = project[:, pair * PAIR : (pair + 1) * PAIR]
+                if part < 2:
+                    piece = turn(piece, cos_ref[real, :], sin_ref[real, :])
+                qkv_ref[part * pairs + pair, rows, :] = piece.astype(BF)
+
+    def unit(pair, d):
+        row_block = xor(d, mine, ranks)
+        rows = pl.ds(pl.multiple_of(d * block, block), block)
+        queries = qkv_ref[pair, rows, :] * HD**-0.5
+        begin = start_ref[pl.ds(pl.multiple_of(row_block * block, block), block), :]
+        mixed = None
+        for head in range(PAIR // HD):
+            mask = head_mask(queries.shape, head)
+            query = jnp.where(mask, queries, jnp.zeros_like(queries))
+
+            def score(j, top, last):
+                at = pl.ds(pl.multiple_of(xor(j, mine, ranks) * block, block), block)
+                s = dot(query, qkv_ref[pairs + pair, at, :], NT)
+                column = lax.broadcasted_iota(jnp.int32, s.shape, 1)
+                visible = column >= begin - j * block
+                if last:
+                    visible &= column <= lax.broadcasted_iota(jnp.int32, s.shape, 0)
+                s = jnp.where(visible, s, NEG)
+                scores_ref[j] = s
+                for c in range(0, block, 128):
+                    top = jnp.maximum(top, s[:, c : c + 128])
+                return top
+
+            top = jnp.full((block, 128), NEG, F32)
+            top = lax.fori_loop(0, row_block, lambda j, top: score(j, top, False), top)
+            top = score(row_block, top, True)
+            top = jnp.max(top, axis=1, keepdims=True)
+
+            def mix(j, carry):
+                total, acc = carry
+                shares = jnp.exp(scores_ref[j] - top)
+                for c in range(0, block, 128):
+                    total = total + shares[:, c : c + 128]
+                at = pl.ds(pl.multiple_of(xor(j, mine, ranks) * block, block), block)
+                return total, acc + dot(shares.astype(BF), qkv_ref[2 * pairs + pair, at, :])
+
+            total, acc = lax.fori_loop(
+                0, row_block + 1, mix, (jnp.zeros((block, 128), F32), jnp.zeros((block, PAIR), F32))
+            )
+            total = jnp.sum(total, axis=1, keepdims=True)
+            acc = acc / total
+            mixed = acc if mixed is None else jnp.where(mask, acc, mixed)
+            logs = jnp.broadcast_to(top + jnp.log(total), (block, 128))
+            log_ref[pair, head : head + 1, rows] = jnp.transpose(logs)[0:1, :]
+        mixed_ref[pair, rows, :] = mixed.astype(BF)
+
+    def head_copy(pair, d):
+        slot = d * pairs + pair
+        return pltpu.make_async_remote_copy(
+            src_ref=mixed_ref.at[pair, pl.ds(pl.multiple_of(d * block, block), block)],
+            dst_ref=heads_ref.at[slot],
+            send_sem=head_sems.at[0, slot],
+            recv_sem=head_sems.at[1, slot],
+            device_id={"tensor": xor(mine, d, ranks)},
+            device_id_type=MESH,
+        )
+
+    last = early - 1
+    units = pairs * ranks
+    events = {
+        0: [lambda: to_x(last), lambda: to_z(early), lambda: to_z(early + 1)],
+        2: [lambda c=c: to_core(c) for c in range(last)],
+        3: [lambda: to_x(early)],
+        4: [lambda: to_core(last)],
+        6: [lambda: to_x(early + 1), lambda: to_core(early)],
+    }
+
+    @pl.loop(0, units)
+    def _(u):
+        pair, d = lax.rem(u, pairs), ranks - 1 - lax.div(u, pairs)
+        unit(pair, d)
+        pl.when(d > 0)(lambda: head_copy(pair, d).start())
+        for when, steps in events.items():
+
+            @pl.when(u == min(when, units - 1))
+            def _():
+                for step in steps:
+                    step()
+
+    for pair in range(pairs):
+        heads_ref[pair] = mixed_ref[pair, 0:block, :]
+    to_core(early + 1)
+
+    @pl.loop(pairs, units)
+    def _(slot):
+        copy = head_copy(lax.rem(slot, pairs), lax.div(slot, pairs))
+        copy.wait_recv()
+        copy.wait_send()
+
+    for copy in [*core_copies, *own_copies]:
+        copy.wait_recv()
+    for copy in [*started, *onward, *own_copies, *y_copies, *x_copies, *core_copies]:
+        copy.wait_send()
+    for copies in z_copies:
+        for copy in copies:
+            copy.wait_send()
+
+
+def attend_forward(tokens, gain, shift, weight, cosine, sine, starts, weights):
+    block, width = tokens.shape
+    ranks = lax.axis_size("tensor")
+    assert ranks == 4
+    length = block * ranks
+    pairs = weight.shape[2] // PAIR
+    group = lax.axis_size("dp") // 2
+    views = [w.reshape(2, group, w.shape[0] // (2 * group), w.shape[1]) for w in weights]
+    chunks = [(0, 0, width)]
+    for a in (1, 2):
+        columns = weights[a].shape[1] // 2
+        chunks += [(a, 0, columns), (a, columns, columns)]
+    vmem = pl.BlockSpec(memory_space=pltpu.VMEM)
+    hbm = pl.BlockSpec(memory_space=pl.ANY)
+    copies = pltpu.SemaphoreType.DMA
+    qkv, attn, mixed, logs, heads, *rests = pl.pallas_call(
+        functools.partial(forward_kernel, block, ranks, pairs, chunks),
+        out_shape=[
+            jax.ShapeDtypeStruct((3 * pairs, length, PAIR), BF),
+            jax.ShapeDtypeStruct((ranks, block, width), BF),
+            jax.ShapeDtypeStruct((pairs, length, PAIR), BF),
+            jax.ShapeDtypeStruct((pairs, 8, length), F32),
+            jax.ShapeDtypeStruct((ranks * pairs, block, PAIR), BF),
+            *[jax.ShapeDtypeStruct((ranks - 1, *view.shape), BF) for view in views],
+        ],
+        in_specs=[vmem] * 7 + [hbm] * 3,
+        out_specs=[vmem] * 5 + [hbm] * 3,
+        scratch_shapes=[
+            pltpu.VMEM((ranks, block, block), F32),
+            copies((2, 12)),
+            copies((2, ranks * pairs)),
+            copies((2, 3)),
+            copies((2, len(chunks))),
+            copies((2, len(chunks) * (group - 1))),
+            copies((2, len(chunks))),
+            copies((2, len(chunks))),
+        ],
+        compiler_params=pltpu.CompilerParams(vmem_limit_bytes=56 << 20, collective_id=2, has_side_effects=True),
         name="attend_forward",
-    )(place, qkv, qkv, qkv, starts)
+    )(tokens, gain, shift, weight, cosine, sine, starts, *views)
+    return qkv, attn, mixed, logs, heads, [r.reshape(ranks - 1, *w.shape) for r, w in zip(rests, weights)]
 
 
 def backward_kernel(
@@ -560,19 +725,7 @@
     length = block * ranks
     local = out_weight.shape[0]
     pairs = local // PAIR
-    mine = lax.axis_index("tensor")
-    place = mine.astype(jnp.int32).reshape(1)
-
     residual_in = block_in.reshape(block, width).astype(F32)
-    attn_norm, attn_norm_pull = jax.vjp(layer_norm, residual_in, norm_gain[0], norm_bias[0])
-    attn_low = attn_norm.astype(BF)
-    attn_parts = gather_tensor(attn_low)
-
-    out_late, up_late, down_late, _ = lax.optimization_barrier((out_weight, up_weight, down_weight, attn_parts[ranks // 2]))
-    up_parts = gather_tensor(up_late)
-    out_parts = gather_tensor(out_late)
-    down_parts = gather_tensor(down_late)
-
     finish = jnp.cumsum(lengths[0])
     begin = finish - lengths[0]
     places = jnp.arange(length, dtype=jnp.int32)
@@ -588,22 +741,22 @@
     start_column = starts.reshape(length, 1)
     start_row = starts.reshape(1, length)
 
-    attn_full = jnp.concatenate(attn_parts, axis=0)
-    qkv_swapped = jnp.transpose(qkv_weight, (1, 0, 2))
-    qkv = project_qkv(place, attn_full, qkv_swapped, cosine, sine, block)
-
-    heads_parts = [[] for _ in range(ranks)]
-    heads_mixed, logs = [], []
-    for pair in range(pairs):
-        mixed, log_total = attend_forward(place, qkv, pair, start_column, block)
-        heads_mixed.append(mixed)
-        logs.append(log_total)
-        for d in range(ranks):
-            piece = mixed[d * block : (d + 1) * block]
-            heads_parts[d].append(piece if d == 0 else swap(piece, "tensor", d))
-    heads_local = jnp.concatenate([piece for parts in heads_parts for piece in parts], axis=1)
-
-    out_full = jnp.concatenate(out_parts, axis=0)
+    qkv, attn_full, heads_mixed, logs, heads_parts, (out_rest, up_rest, down_rest) = attend_forward(
+        block_in.reshape(block, width),
+        norm_gain[0:1],
+        norm_bias[0:1],
+        jnp.transpose(qkv_weight, (1, 0, 2)),
+        cosine,
+        sine,
+        start_column,
+        (out_weight, up_weight, down_weight),
+    )
+    attn_full = attn_full.reshape(length, width)
+    heads_local = jnp.concatenate([heads_parts[i] for i in range(ranks * pairs)], axis=1)
+    up_parts = [up_weight] + [up_rest[d] for d in range(ranks - 1)]
+    down_parts = [down_weight] + [down_rest[d] for d in range(ranks - 1)]
+
+    out_full = jnp.concatenate([out_weight, out_rest.reshape(-1, width)], axis=0)
     attn_proj = dot(heads_local, out_full)
     attn_branch, attn_branch_pull = jax.vjp(layer_norm, attn_proj, norm_gain[1], norm_bias[1])
     middle = residual_in + attn_branch
@@ -658,7 +811,7 @@
         [grad_heads[:, i * PAIR : (i + 1) * PAIR] for i in range(width // PAIR)], axis=0
     )
     grads, *pieces = attend_backward(
-        qkv, grad_parts, jnp.stack(heads_mixed), jnp.stack(logs), start_row, cosine, sine, shared, terms, block
+        qkv, grad_parts, heads_mixed, logs, start_row, cosine, sine, shared, terms, block
     )
     wide = jnp.concatenate([grads[i] for i in range(3 * pairs)], axis=1)
     qkv_flat = qkv_weight.reshape(width, 3 * local)

time: 538 us -> 483 us (0.90); the launches traced: 527 us -> 478 us
  waiting for transfers between devices: 97.1 us -> 0.02 us
  Pallas kernels: 243 us -> 303 us
  starting transfers between devices: 11.6 us -> 2.55 us
  other arithmetic: 33.2 us -> 25 us
  local copies, waits for them, and re-layouts: 38.9 us -> 44.6 us
    ppermute x24 -> x6, waiting for transfers between devices: 97.1 us -> 0.02 us  [swap(): return lax.ppermute(value, axis, [(i, i ^ offset) for i in range(size)])]
    pallas_call x3 -> x1, Pallas kernels: 38.9 us -> 95.6 us  [attend_forward(): pl.pallas_call(functools.partial(forward_kernel, block, ranks, pairs, chu...]
    ppermute x24 -> x6, starting transfers between devices: 11.6 us -> 2.55 us  [swap(): return lax.ppermute(value, axis, [(i, i ^ offset) for i in range(size)])]
    unnamed x113 -> x108, local copies, waits for them, and re-layouts: 28 us -> 30.9 us
  transfers between devices with their start and end apart: 24 -> 6, of which waited for: 7 -> 0; matrix products, arithmetic and copies ran while one was open for 15% -> 16% of each run, Pallas kernels for 7% -> 0%
where the time goes in v3:
time: 483 us; the launch traced here: 478 us
  Pallas kernels  303 us (63%)
  matrix products  102 us (21%)
  local copies, waits for them, and re-layouts  44.6 us (9%)
  other arithmetic  25 us (5%)
    pallas_call x1, Pallas kernels, last_stage(): pl.pallas_call(functools.partial(last_kernel, ranks, count), out_shape=[j...  119 us
    dot_general x20, matrix products, dot(): return lax.dot_general(a, b, dims, preferred_element_type=F32)  102 us
    pallas_call x1, Pallas kernels, attend_forward(): pl.pallas_call(functools.partial(forward_kernel, block, ranks, pairs, chu...  95.6 us
    pallas_call x1, Pallas kernels, attend_backward(): pl.pallas_call(functools.partial(backward_kernel, block, blocks, pairs, c...  88.2 us
    unnamed x108, local copies, waits for them, and re-layouts  30.9 us
  transfers between devices with their start and end apart: 6, of which 0 were waited for; matrix products, arithmetic and copies ran while one was open for 16% of the time, Pallas kernels for 0%

profile of v3, /device:TPU:20, one launch (start us, length us, event | category | flops | bytes accessed | tf_op | source)
XLA Modules:
  0.0 478.1 jit_solution(579087701308751676)
XLA Ops:
  0.6 0.8 reduce-window.4
  2.3 1.3 copy.24.refs_6_
  3.7 1.5 fusion.168
  5.2 5.5 %fusion.50 = (f32[2048,128]{1,0:T(8,128)}, f32[2048,128]{1,0:T(8,128)}) fusion(f32[128]{0:T(128)S(1)} %get-tuple-element.121, f32[128]{0:T(128)S(1)} %get-tuple-element.122, f32[2048]{0:T(1024)S(1)} %subtract_convert_fusion), kind=kLoop, calls=%fused_computation.92 | loop fusion | flops 524288 | bytes 2106368 | tf_op jit(solution)/shard_map/mul | solution.py:740
  10.7 95.6 %attend_forward.1 = (bf16[6,2048,128]{2,1,0:T(8,128)(2,1)}, bf16[4,512,1024]{2,1,0:T(8,128)(2,1)}, bf16[2,2048,128]{2,1,0:T(8,128)(2,1)}, f32[2,8,2048]{2,1,0:T(...) custom-call(bf16[512,1024]{1,0:T(8,128)(2,1)} %bitcast.167, ...), custom_call_target="tpu_custom_call" | custom-call | tf_op jit(solution)/shard_map/attend_forward/pallas_call | solution.py:359
  106.4 1.1 bitcast_dynamic-update-slice_fusion.13
  107.4 0.9 bitcast_dynamic-update-slice_fusion.12
  108.4 0.9 bitcast_dynamic-update-slice_fusion.11
  109.3 0.9 bitcast_dynamic-update-slice_fusion.10
  110.3 0.9 bitcast_dynamic-update-slice_fusion.9
  111.3 0.9 bitcast_dynamic-update-slice_fusion.8
  112.2 0.9 bitcast_dynamic-update-slice_fusion.7
  113.2 0.9 bitcast_dynamic-update-slice_fusion.6
  114.1 1.3 fusion.170
  115.9 1.6 copy-done.4
  117.5 0.7 fusion.162
  118.6 1.4 add_convert_fusion.3
  120.7 2.6 fusion.180
  123.4 1.1 fusion.164
  124.5 1.9 slice-done.1
  126.4 1.1 fusion.163
  127.5 3.3 fusion.183
  130.8 3.3 fusion.182
  134.1 1.4 fusion.51
  135.5 2.5 fusion.181
  138.0 1.4 fusion.53
  139.5 1.8 fusion.52
  141.3 1.6 fusion.171
  143.3 0.9 copy-done.3
  144.2 0.8 fusion.16
  145.0 1.9 fusion.161
  146.9 1.2 add_convert_fusion.1
  148.1 1.4 collective-permute-start.4
  149.6 7.3 %fusion.78 = f32[512,1024]{1,0:T(8,128)} fusion(bf16[1024,1024]{1,0:T(8,128)(2,1)} %bitcast.191, f32[512,1024]{1,0:T(8,128)} %copy-done.37, bf16[512,1024]{1,0:T(8,128)(2,1)} %add_convert_fusion.1, bf16[1024,1024]{1,0:T(8,128)(2,1)} %bitcast.189), kind=kOutput, calls=%fused_computation.119 | convolution fusion | flops 2157969408 | bytes 9437184 | tf_op jit(solution)/shard_map/dot_general | solution.py:24
  156.9 7.3 %fusion.82 = f32[512,1024]{1,0:T(8,128)} fusion(bf16[1024,1024]{1,0:T(8,128)(2,1)} %param.13, f32[512,1024]{1,0:T(8,128)} %copy-done.35, bf16[512,1024]{1,0:T(8,128)(2,1)} %add_convert_fusion.1, bf16[1024,1024]{1,0:T(8,128)(2,1)} %param.14), kind=kOutput, calls=%fused_computation.121 | convolution fusion | flops 2157969408 | bytes 9437184 | tf_op jit(solution)/shard_map/dot_general | solution.py:24
  164.3 7.4 %fusion.80 = f32[512,1024]{1,0:T(8,128)} fusion(bf16[1024,1024]{1,0:T(8,128)(2,1)} %bitcast.187, f32[512,1024]{1,0:T(8,128)} %copy-done.36, bf16[512,1024]{1,0:T(8,128)(2,1)} %add_convert_fusion.1, bf16[1024,1024]{1,0:T(8,128)(2,1)} %bitcast.185), kind=kOutput, calls=%fused_computation.120 | convolution fusion | flops 2157969408 | bytes 9437184 | tf_op jit(solution)/shard_map/dot_general | solution.py:24
  171.8 2.8 copy.25
  174.6 9.7 %multiply_reduce_fusion.1 = (f32[1024]{0:T(1024)S(1)}, f32[512]{0:T(512)S(1)}, f32[1024]{0:T(1024)S(1)}, f32[512,1024]{1,0:T(8,128)}) fusion(f32[512,1024]{1,0:T(8,128)S(1)} %get-tuple-element.92, f32[512]{0:T(512)S(1)} %fusion.95, f32[512]{0:T(512)S(1)} %broadcast_multiply_fusion.1, f32[1024]{0:T(1024)S(1)} %bitcast.211, bf16[1024,1024]{1,0:T(8,128)(2,1)} %bitcast.183, ...), kind=kOutput, calls=%fused_computation.68 | convolution fusion | flops 2163734016 | bytes 17844224 | tf_op jit(solution)/shard_map/dot_general | solution.py:24
  184.3 2.4 fusion.160
  186.7 1.1 multiply_reduce_fusion
  187.9 0.7 fusion.158
  189.3 0.9 copy-done.31
  190.2 1.3 convolution_convert_fusion.3
  191.5 0.7 stack.38.refs_3_
  193.1 4.0 convolution_convert_fusion.1
  197.3 1.0 copy-done.28
  198.2 7.3 %fusion.85 = f32[2048,1024]{1,0:T(8,128)S(1)} fusion(bf16[1024,1024]{1,0:T(8,128)(2,1)S(1)} %copy-done.8, bf16[512,1024]{1,0:T(8,128)(2,1)S(1)} %collective-permute-done.2, bf16[512,1024]{1,0:T(8,128)(2,1)} %collective-permute-done.1, bf16[512,1024]{1,0:T(8,128)(2,1)} %collective-permute-done, bf16[512,1024]{1,0:T(8,128)(2,1)} %add_convert_fusion.3), kind=kOutput, calls=%fused_computation.123 | convolution fusion | flops 4311744512 | bytes 14680064 | tf_op jit(solution)/shard_map/dot_general | solution.py:24
  205.6 9.9 %fusion.48 = bf16[1024,1024]{1,0:T(8,128)(2,1)S(1)} fusion(f32[2048,1024]{1,0:T(8,128)S(1)} %fusion.85, bf16[512,1024]{1,0:T(8,128)(2,1)S(1)} %collective-permute-done.5, bf16[512,1024]{1,0:T(8,128)(2,1)} %collective-permute-done.4, bf16[512,1024]{1,0:T(8,128)(2,1)} %collective-permute-done.3, bf16[512,1024]{1,0:T(8,128)(2,1)} %add_convert_fusion.1), kind=kOutput, calls=%fused_computation.86 | convolution fusion | flops 4331667456 | bytes 14680064 | tf_op jit(solution)/shard_map/dot_general | solution.py:24
  215.5 1.5 fusion.166
  217.1 18.5 %fusion.45 = bf16[1024,1024]{1,0:T(8,128)(2,1)S(1)} fusion(f32[2048,1024]{1,0:T(8,128)} %copy-done.38, bf16[1024,1024]{1,0:T(8,128)(2,1)} %param.14, bf16[512,1024]{1,0:T(8,128)(2,1)} %copy-done.34, bf16[512,1024]{1,0:T(8,128)(2,1)} %collective-permute-done.4, bf16[512,1024]{1,0:T(8,128)(2,1)} %collective-permute-done.3, ...), kind=kOutput, calls=%fused_computation.85 | convolution fusion | flops 8666480640 | bytes 20971520 | tf_op jit(solution)/shard_map/dot_general | solution.py:24
  235.6 1.6 fusion.165
  237.2 88.2 %attend_backward.1 = (bf16[6,2048,128]{2,1,0:T(8,128)(2,1)}, bf16[128,512]{1,0:T(8,128)(2,1)}, bf16[128,512]{1,0:T(8,128)(2,1)}, bf16[128,512]{1,0:T(8,128)(2,1)...) custom-call(bf16[6,2048,128]{2,1,0:T(8,128)(2,1)} %get-tuple-element.34.refs_0_, bf16[8,512,128]{2,1,0:T(8,128)(2,1)} %copy-done.28, ...), custom_call_target="tpu_custom_call" | custom-call | flops 53687091200 | bytes 8388608 | tf_op jit(solution)/shard_map/attend_backward/pallas_call | solution.py:548
  325.4 1.3 bitcast_dynamic-update-slice_fusion.5
  326.7 1.2 bitcast_dynamic-update-slice_fusion.4
  327.8 1.3 bitcast_dynamic-update-slice_fusion.3
  329.6 4.9 %convolution_convert_fusion = bf16[2048,1024]{1,0:T(8,128)(2,1)} fusion(bf16[2048,768]{1,0:T(8,128)(2,1)S(1)} %bitcast_dynamic-update-slice_fusion, bf16[1024,768]{0,1:T(8,128)(2,1)S(1)} %bitcast.192), kind=kOutput, calls=%fused_computation.14 | convolution fusion | flops 3223322624 | bytes 8912896 | tf_op jit(solution)/shard_map/dot_general | solution.py:24
  334.5 4.6 convolution_convert_fusion.2
  339.1 118.8 %last_stage.1 = (f32[512,1024]{1,0:T(8,128)}, f32[8,1024]{1,0:T(8,128)}, bf16[2,4,128,768]{3,2,1,0:T(8,128)(2,1)}, bf16[2,4,128,512]{3,2,1,0:T(8,128)(2,1)}, bf1...) custom-call(bf16[512,1024]{1,0:T(8,128)(2,1)} %bitcast.168, ...), custom_call_target="tpu_custom_call" | custom-call | tf_op jit(solution)/shard_map/last_stage/pallas_call | solution.py:685
  457.9 5.2 %copy.27 = f32[512,1,1024]{2,1,0:T(1,128)} copy(f32[512,1,1024]{2,0,1:T(8,128)} %bitcast.177) | data formatting | bytes 4194304
  463.1 3.2 reshape.267
  466.3 4.6 copy.28
  470.9 1.1 bitcast_convert_fusion
  472.7 2.6 maximum_convert_fusion
  475.3 2.6 maximum_convert_fusion.1
  (127 shorter events, 5.9 us)
Async XLA Ops:
  2.3 104.0 %copy-start.25 = (s32[2048]{0:T(1024)}, s32[2048]{0:T(1024)S(1)}, u32[]{:S(2)}) copy-start(s32[2048]{0:T(1024)S(1)} %select_reduce_fusion) | copy-start | bytes 24580
  106.3 7.8 %copy-start.22 = (bf16[256,1024]{1,0:T(8,128)(2,1)S(1)}, bf16[256,1024]{1,0:T(8,128)(2,1)}, u32[]{:S(2)}) copy-start(bf16[256,1024]{1,0:T(8,128)(2,1)} %param.12) | copy-start | bytes 1572868
  106.4 7.8 %copy-start.30 = (bf16[3,2,4,32,1024]{4,3,2,1,0:T(8,128)(2,1)S(1)}, bf16[3,2,4,32,1024]{4,3,2,1,0:T(8,128)(2,1)}, u32[]{:S(2)}) copy-start(bf16[3,2,4,32,1024]{4,3,2,1,0:T(8,128)(2,1)} %get-tuple-element.31) | copy-start | bytes 4718596
  114.1 1.4 copy-start.27
  115.5 2.7 copy-start
  115.5 2.0 copy-start.4
  117.5 5.9 %slice-start.2 = ((s8[6291456]{0:T(1024)(128)(4,1)}), s8[4194304]{0:T(1024)(128)(4,1)S(1)}, s32[]{:S(2)}) async-start(s8[6291456]{0:T(1024)(128)(4,1)} %bitcast.173), calls=%async_computation.2 | async-start | bytes 8388608
  118.5 2.2 copy-start.7
  118.6 4.8 %slice-start.3 = ((s8[6291456]{0:T(1024)(128)(4,1)}), s8[2097152]{0:T(1024)(128)(4,1)S(1)}, s32[]{:S(2)}) async-start(s8[6291456]{0:T(1024)(128)(4,1)} %bitcast.173), calls=%async_computation.3 | async-start | bytes 4194304
  119.9 72.5 %collective-permute-start.1 = (bf16[512,1024]{1,0:T(8,128)(2,1)}, bf16[512,1024]{1,0:T(8,128)(2,1)}, u32[]{:S(2)}, u32[]{:S(2)}) collective-permute-start(bf16[512,1024]{1,0:T(8,128)(2,1)} %add_convert_fusion.3), channel_id=1, source_target_pairs={{0,2},{1,3},{2,0},{3,1},{4,6},{5,7},{6,4},{7,5},{8,10},{9,11},{10,... | collective-permute-start | bytes 3145736 | tf_op jit(solution)/shard_map/ppermute | solution.py:35
  120.3 78.0 %collective-permute-start = (bf16[512,1024]{1,0:T(8,128)(2,1)}, bf16[512,1024]{1,0:T(8,128)(2,1)}, u32[]{:S(2)}, u32[]{:S(2)}) collective-permute-start(bf16[512,1024]{1,0:T(8,128)(2,1)} %add_convert_fusion.3), channel_id=1, source_target_pairs={{0,1},{1,0},{2,3},{3,2},{4,5},{5,4},{6,7},{7,6},{8,9},{9,8},{10,11... | collective-permute-start | bytes 3145736 | tf_op jit(solution)/shard_map/ppermute | solution.py:35
  120.7 3.8 slice-start
  123.3 10.7 %copy-start.35 = (f32[512,1024]{1,0:T(8,128)}, f32[512,1024]{1,0:T(8,128)S(1)}, u32[]{:S(2)}) copy-start(f32[512,1024]{1,0:T(8,128)S(1)} %fusion.180) | copy-start | bytes 6291460
  123.4 3.0 slice-start.1
  124.5 13.6 %copy-start.14 = (bf16[1,2,4,128,1024]{4,3,2,1,0:T(8,128)(2,1)}, bf16[1,2,4,128,1024]{4,3,2,1,0:T(8,128)(2,1)S(1)}, u32[]{:S(2)}) copy-start(bf16[1,2,4,128,1024]{4,3,2,1,0:T(8,128)(2,1)S(1)} %get-tuple-element.97) | copy-start | bytes 6291460
  124.5 15.0 %copy-start.12 = (bf16[1,2,4,128,1024]{4,3,2,1,0:T(8,128)(2,1)}, bf16[1,2,4,128,1024]{4,3,2,1,0:T(8,128)(2,1)S(1)}, u32[]{:S(2)}) copy-start(bf16[1,2,4,128,1024]{4,3,2,1,0:T(8,128)(2,1)S(1)} %get-tuple-element.98) | copy-start | bytes 6291460
  124.5 16.8 %copy-start.5 = (bf16[1,2,4,128,1024]{4,3,2,1,0:T(8,128)(2,1)}, bf16[1,2,4,128,1024]{4,3,2,1,0:T(8,128)(2,1)S(1)}, u32[]{:S(2)}) copy-start(bf16[1,2,4,128,1024]{4,3,2,1,0:T(8,128)(2,1)S(1)} %get-tuple-element.96) | copy-start | bytes 6291460
  127.5 3.3 copy-start.10
  127.5 3.3 copy-start.15
  127.5 8.0 %copy-start.13 = (bf16[1,2,4,128,1024]{4,3,2,1,0:T(8,128)(2,1)}, bf16[1,2,4,128,1024]{4,3,2,1,0:T(8,128)(2,1)S(1)}, u32[]{:S(2)}) copy-start(bf16[1,2,4,128,1024]{4,3,2,1,0:T(8,128)(2,1)S(1)} %get-tuple-element.95) | copy-start | bytes 6291460
  130.8 10.5 %copy-start.11 = (f32[512,1024]{1,0:T(8,128)}, f32[512,1024]{1,0:T(8,128)S(1)}, u32[]{:S(2)}) copy-start(f32[512,1024]{1,0:T(8,128)S(1)} %fusion.183) | copy-start | bytes 6291460
  130.8 3.3 copy-start.9
  134.1 3.9 copy-start.37
  138.0 1.5 copy-start.36
  142.9 1.2 copy-start.3
  148.1 49.0 %collective-permute-start.4 = (bf16[512,1024]{1,0:T(8,128)(2,1)}, bf16[512,1024]{1,0:T(8,128)(2,1)}, u32[]{:S(2)}, u32[]{:S(2)}) collective-permute-start(bf16[512,1024]{1,0:T(8,128)(2,1)} %add_convert_fusion.1), channel_id=1, source_target_pairs={{0,2},{1,3},{2,0},{3,1},{4,6},{5,7},{6,4},{7,5},{8,10},{9,11},{10,... | collective-permute-start | bytes 3145736 | tf_op jit(solution)/shard_map/ppermute | solution.py:35
  149.5 56.1 %collective-permute-start.3 = (bf16[512,1024]{1,0:T(8,128)(2,1)}, bf16[512,1024]{1,0:T(8,128)(2,1)}, u32[]{:S(2)}, u32[]{:S(2)}) collective-permute-start(bf16[512,1024]{1,0:T(8,128)(2,1)} %add_convert_fusion.1), channel_id=1, source_target_pairs={{0,1},{1,0},{2,3},{3,2},{4,5},{5,4},{6,7},{7,6},{8,9},{9,8},{10,11... | collective-permute-start | bytes 3145736 | tf_op jit(solution)/shard_map/ppermute | solution.py:35
  184.3 2.4 copy-start.1
  187.9 1.3 copy-start.2
  187.9 1.4 copy-start.23
  187.9 2.3 copy-start.31
  192.5 5.8 %collective-permute-start.2 = (bf16[512,1024]{1,0:T(8,128)(2,1)}, bf16[512,1024]{1,0:T(8,128)(2,1)S(1)}, u32[]{:S(2)}, u32[]{:S(2)}) collective-permute-start(bf16[512,1024]{1,0:T(8,128)(2,1)} %collective-permute-done.1), channel_id=1, source_target_pairs={{0,1},{1,0},{2,3},{3,2},{4,5},{5,4},{6,7},{7,6},{8,9},{9,8},{10,11... | collective-permute-start | bytes 3145736 | tf_op jit(solution)/shard_map/ppermute | solution.py:35
  193.1 5.2 %copy-start.8 = (bf16[1024,1024]{1,0:T(8,128)(2,1)S(1)}, bf16[1024,1024]{1,0:T(8,128)(2,1)}, u32[]{:S(2)}) copy-start(bf16[1024,1024]{1,0:T(8,128)(2,1)} %param.13) | copy-start | bytes 6291460
  197.1 8.5 %collective-permute-start.5 = (bf16[512,1024]{1,0:T(8,128)(2,1)}, bf16[512,1024]{1,0:T(8,128)(2,1)S(1)}, u32[]{:S(2)}, u32[]{:S(2)}) collective-permute-start(bf16[512,1024]{1,0:T(8,128)(2,1)} %collective-permute-done.4), channel_id=1, source_target_pairs={{0,1},{1,0},{2,3},{3,2},{4,5},{5,4},{6,7},{7,6},{8,9},{9,8},{10,11... | collective-permute-start | bytes 3145736 | tf_op jit(solution)/shard_map/ppermute | solution.py:35
  197.2 1.0 copy-start.28
  198.2 7.3 %copy-start.32 = (bf16[512,1024]{1,0:T(8,128)(2,1)}, bf16[512,1024]{1,0:T(8,128)(2,1)S(1)}, u32[]{:S(2)}) copy-start(bf16[512,1024]{1,0:T(8,128)(2,1)S(1)} %collective-permute-done.2) | copy-start | bytes 3145732
  205.6 9.9 %copy-start.38 = (f32[2048,1024]{1,0:T(8,128)}, f32[2048,1024]{1,0:T(8,128)S(1)}, u32[]{:S(2)}) copy-start(f32[2048,1024]{1,0:T(8,128)S(1)} %fusion.85) | copy-start | bytes 25165828
  205.6 9.9 %copy-start.34 = (bf16[512,1024]{1,0:T(8,128)(2,1)}, bf16[512,1024]{1,0:T(8,128)(2,1)S(1)}, u32[]{:S(2)}) copy-start(bf16[512,1024]{1,0:T(8,128)(2,1)S(1)} %collective-permute-done.5) | copy-start | bytes 3145732
  215.5 1.6 copy-start.33
  325.4 3.8 copy-start.6
  327.8 1.7 copy-start.16
  329.6 4.9 %copy-start.29 = (bf16[4,512,1024]{2,1,0:T(8,128)(2,1)S(1)}, bf16[4,512,1024]{2,1,0:T(8,128)(2,1)}, u32[]{:S(2)}) copy-start(bf16[4,512,1024]{2,1,0:T(8,128)(2,1)} %get-tuple-element.38) | copy-start | bytes 12582916
  457.9 5.2 %copy-start.17 = (bf16[2,4,128,768]{3,2,1,0:T(8,128)(2,1)S(1)}, bf16[2,4,128,768]{3,2,1,0:T(8,128)(2,1)}, u32[]{:S(2)}) copy-start(bf16[2,4,128,768]{3,2,1,0:T(8,128)(2,1)} %get-tuple-element.45) | copy-start | bytes 4718596
  466.3 4.6 copy-start.24
  466.3 5.7 %copy-start.26 = (f32[8,1024]{1,0:T(8,128)S(1)}, f32[8,1024]{1,0:T(8,128)}, u32[]{:S(2)}) copy-start(f32[8,1024]{1,0:T(8,128)} %get-tuple-element.51) | copy-start | bytes 98308
  466.3 6.3 %copy-start.21 = (bf16[2,4,128,512]{3,2,1,0:T(8,128)(2,1)S(1)}, bf16[2,4,128,512]{3,2,1,0:T(8,128)(2,1)}, u32[]{:S(2)}) copy-start(bf16[2,4,128,512]{3,2,1,0:T(8,128)(2,1)} %get-tuple-element.48) | copy-start | bytes 3145732
  470.9 1.7 copy-start.20
  472.7 2.6 copy-start.18
  472.7 2.6 copy-start.19

commit v4 on v3

--- a/solution.py
+++ b/solution.py
@@ -28,24 +28,6 @@
     centre = values - jnp.mean(values, axis=-1, keepdims=True)
     spread = jnp.mean(centre * centre, axis=-1, keepdims=True)
     return centre * lax.rsqrt(spread + EPSILON) * gain + shift
-
-
-def swap(value, axis, offset):
-    size = lax.axis_size(axis)
-    return lax.ppermute(value, axis, [(i, i ^ offset) for i in range(size)])
-
-
-def gather_tensor(value):
-    parts = [value]
-    size = lax.axis_size("tensor")
-    step = size // 2
-    found = {0: value}
-    while step >= 1:
-        for place in sorted(found):
-            found[place ^ step] = swap(found[place], "tensor", step)
-        step //= 2
-    parts = [found[d] for d in range(size)]
-    return parts
 
 
 def flip(index, offset):
@@ -384,18 +366,286 @@
     return qkv, attn, mixed, logs, heads, [r.reshape(ranks - 1, *w.shape) for r, w in zip(rests, weights)]
 
 
+def unit_scale(values):
+    centre = values - jnp.mean(values, axis=-1, keepdims=True)
+    scale = lax.rsqrt(jnp.mean(centre * centre, axis=-1, keepdims=True) + EPSILON)
+    return centre * scale, scale
+
+
+def norm_pull(grad, unit, scale, gain):
+    inside = grad * gain
+    first = jnp.mean(inside, axis=-1, keepdims=True)
+    second = jnp.mean(inside * unit, axis=-1, keepdims=True)
+    return scale * (inside - first - unit * second)
+
+
+def gelu_both(x):
+    bend = 0.7978845608028654
+    square = x * x
+    t = jnp.tanh(bend * (x + 0.044715 * (square * x)))
+    side = 0.5 * (1.0 + t)
+    return x * side, side + 0.5 * x * (1.0 - t * t) * (bend * (1.0 + 0.134145 * square))
+
+
+def middle_kernel(block, ranks, pairs, *refs):
+    (heads_ref, x_ref, dy_ref, gains_ref, shifts_ref, *refs) = refs
+    sources, refs = refs[:6], refs[6:]
+    (out_ref, rest_ref, do_ref, shared_ref, down_term, up_term, early_ref, *refs) = refs
+    (out_all, up_all, down_all, work_ref, mlp_ref, gmp_ref, middle_ref, proj_ref, acc_ref, gap_ref, gh_ref, *refs) = refs
+    (out_sems, up_sems, down_sems, mlp_sems, gmp_sems, head_sems) = refs
+
+    mine = lax.axis_index("tensor")
+    width = x_ref.shape[1]
+    strips, rows = 4, 64
+    strip = block // strips
+    columns = width // 2
+
+    def loads(own, rest, array, sems):
+        return [
+            pltpu.make_async_copy(own if d == 0 else rest.at[d - 1], array.at[d], sems.at[d]) for d in range(ranks)
+        ]
+
+    out_loads = loads(sources[0], sources[1], out_all, out_sems)
+    up_loads = loads(sources[2], sources[3], up_all, up_sems)
+    down_loads = loads(sources[4], sources[5], down_all, down_sems)
+    for copy in out_loads:
+        copy.start()
+    for d in range(ranks):
+        up_loads[d].start()
+        down_loads[d].start()
+    greet(("tensor",))
+
+    def senders(array, sems):
+        found = []
+        for q in range(strips):
+            at = pl.ds(q * strip, strip)
+            found.append(
+                (
+                    push(array.at[0, at], array.at[2, at], sems, q, "tensor", 2),
+                    push(array.at[0, at], array.at[1, at], sems, strips + q, "tensor", 1),
+                    push(array.at[2, at], array.at[3, at], sems, 2 * strips + q, "tensor", 1),
+                )
+            )
+        return found
+
+    mlp_copies = senders(mlp_ref, mlp_sems)
+    gmp_copies = senders(gmp_ref, gmp_sems)
+
+    def send_strip(copies, q):
+        copies[q][0].start()
+        copies[q][1].start()
+
+    def forward_on(copies):
+        for across, _, onward in copies:
+            across.wait_recv()
+            onward.start()
+
+    for d in range(ranks):
+        out_loads[d].wait()
+    for c in (0, columns):
+        at = pl.ds(c, columns)
+        total = None
+        for d in range(ranks):
+            part = jnp.concatenate([heads_ref[d * pairs + p] for p in range(pairs)], axis=1)
+            term = dot(part, out_all[d, :, at])
+            total = term if total is None else total + term
+        proj_ref[:, at] = total
+
+    gain = [gains_ref[j : j + 1, :] for j in range(4)]
+    shift = [shifts_ref[j : j + 1, :] for j in range(4)]
+
+    for q in range(strips):
+
+        @pl.loop(0, strip // rows)
+        def _(r):
+            at = pl.ds(pl.multiple_of(q * strip + r * rows, rows), rows)
+            unit, _ = unit_scale(proj_ref[at, :])
+            middle = x_ref[at, :].astype(F32) + (unit * gain[1] + shift[1])
+            middle_ref[at, :] = middle
+            unit, _ = unit_scale(middle)
+            mlp_ref[0, at, :] = (unit * gain[2] + shift[2]).astype(BF)
+
+        send_strip(mlp_copies, q)
+
+    acc_ref[...] = jnp.zeros_like(acc_ref)
+
+    @pl.loop(0, ranks)
+    def _(d):
+        pltpu.make_async_copy(up_all.at[d], up_all.at[d], up_sems.at[d]).wait()
+        pltpu.make_async_copy(down_all.at[d], down_all.at[d], down_sems.at[d]).wait()
+        for c in (0, columns):
+            at = pl.ds(c, columns)
+            hidden, slope = gelu_both(dot(mlp_ref[0], up_all[d, :, at]))
+            work_ref[d, :, at] = slope
+            acc_ref[...] += dot(hidden.astype(BF), down_all[d, at, :])
+
+    zero = jnp.zeros((1, width), F32)
+    gain_three, shift_three = zero, zero
+    for q in range(strips):
+
+        def last_norm(r, carry):
+            gain_term, shift_term = carry
+            at = pl.ds(pl.multiple_of(q * strip + r * rows, rows), rows)
+            unit, scale = unit_scale(acc_ref[at, :])
+            out_ref[at, :] = (middle_ref[at, :] + (unit * gain[3] + shift[3])).astype(BF)
+            dy = dy_ref[at, :].astype(F32)
+            gmp_ref[0, at, :] = norm_pull(dy, unit, scale, gain[3]).astype(BF)
+            return (
+                gain_term + jnp.sum(dy * unit, axis=0, keepdims=True),
+                shift_term + jnp.sum(dy, axis=0, keepdims=True),
+            )
+
+        gain_three, shift_three = lax.fori_loop(0, strip // rows, last_norm, (gain_three, shift_three))
+        send_strip(gmp_copies, q)
+
+    acc_ref[...] = jnp.zeros_like(acc_ref)
+
+    @pl.loop(0, ranks)
+    def _(d):
+        for c in (0, columns):
+            at = pl.ds(c, columns)
+            grad = dot(gmp_ref[0], down_all[d, at, :], NT)
+            grad = (grad * work_ref[d, :, at]).astype(BF)
+            acc_ref[...] += dot(grad, up_all[d, :, at], NT)
+
+    forward_on(mlp_copies)
+
+    def inner_norms(r, carry):
+        gain_two, shift_two, gain_one, shift_one = carry
+        at = pl.ds(pl.multiple_of(r * rows, rows), rows)
+        grad = acc_ref[at, :]
+        unit, scale = unit_scale(middle_ref[at, :])
+        gain_two = gain_two + jnp.sum(grad * unit, axis=0, keepdims=True)
+        shift_two = shift_two + jnp.sum(grad, axis=0, keepdims=True)
+        grad = dy_ref[at, :].astype(F32) + norm_pull(grad, unit, scale, gain[2])
+        rest_ref[at, :] = grad
+        unit, scale = unit_scale(proj_ref[at, :])
+        gain_one = gain_one + jnp.sum(grad * unit, axis=0, keepdims=True)
+        shift_one = shift_one + jnp.sum(grad, axis=0, keepdims=True)
+        gap_ref[at, :] = norm_pull(grad, unit, scale, gain[1]).astype(BF)
+        return gain_two, shift_two, gain_one, shift_one
+
+    gain_two, shift_two, gain_one, shift_one = lax.fori_loop(0, block // rows, inner_norms, (zero, zero, zero, zero))
+    early_ref[...] = jnp.concatenate(
+        [zero, gain_one, gain_two, gain_three, zero, shift_one, shift_two, shift_three], axis=0
+    )
+
+    head_copies = []
+    for d in [*range(1, ranks), 0]:
+        grad = dot(gap_ref[...], out_all[d], NT).astype(BF)
+        for pair in range(pairs):
+            piece = grad[:, pair * PAIR : (pair + 1) * PAIR]
+            if d == 0:
+                do_ref[pair, 0] = piece
+            else:
+                slot = d * pairs + pair
+                gh_ref[slot] = piece
+                copy = push(gh_ref.at[slot], do_ref.at[pair, d], head_sems, slot, "tensor", d)
+                copy.start()
+                head_copies.append(copy)
+    for d in range(ranks):
+        part = jnp.concatenate([heads_ref[d * pairs + p] for p in range(pairs)], axis=1)
+        shared_ref[d] = dot(part, gap_ref[...], TN).astype(BF)
+
+    for copies in (mlp_copies, gmp_copies):
+        for _, beside, _ in copies:
+            beside.wait_recv()
+    work_ref[...] = jnp.zeros_like(work_ref)
+
+    def late():
+        forward_on(gmp_copies)
+
+    def latest():
+        for copies in (mlp_copies, gmp_copies):
+            for _, _, onward in copies:
+                onward.wait_recv()
+
+    @pl.loop(0, ranks)
+    def _(b):
+        pl.when(b == 2)(late)
+        pl.when(b == 3)(latest)
+        tokens, grads = mlp_ref[b], gmp_ref[b]
+        for h in range(2):
+            at = pl.ds(h * columns, columns)
+            hidden, slope = gelu_both(dot(tokens, up_all[0, :, at]))
+            grad = (dot(grads, down_all[0, at, :], NT) * slope).astype(BF)
+            work_ref[h] += dot(hidden.astype(BF), grads, TN)
+            work_ref[2, :, at] += dot(tokens[:, 0:columns], grad, TN)
+            work_ref[3, :, at] += dot(tokens[:, columns:], grad, TN)
+
+    for h in range(2):
+        at = pl.ds(h * columns, columns)
+        down_term[at, :] = work_ref[h].astype(BF)
+        up_term[at, :] = work_ref[2 + h].astype(BF)
+    for copy in head_copies:
+        copy.wait_recv()
+        copy.wait_send()
+    for copies in (mlp_copies, gmp_copies):
+        for group in copies:
+            for copy in group:
+                copy.wait_send()
+
+
+def middle_stage(heads, tokens, cotangent, gains, shifts, weights, rests):
+    block, width = tokens.shape
+    ranks = lax.axis_size("tensor")
+    local = weights[0].shape[0]
+    pairs = local // PAIR
+    hidden = weights[2].shape[0]
+    vmem = pl.BlockSpec(memory_space=pltpu.VMEM)
+    hbm = pl.BlockSpec(memory_space=pl.ANY)
+    copies = pltpu.SemaphoreType.DMA
+    assert block * 2 == width and hidden == width
+    operands = [array for pair in zip(weights, rests) for array in pair]
+    return pl.pallas_call(
+        functools.partial(middle_kernel, block, ranks, pairs),
+        out_shape=[
+            jax.ShapeDtypeStruct((block, width), BF),
+            jax.ShapeDtypeStruct((block, width), F32),
+            jax.ShapeDtypeStruct((pairs, ranks, block, PAIR), BF),
+            jax.ShapeDtypeStruct((ranks, local, width), BF),
+            jax.ShapeDtypeStruct((hidden, width), BF),
+            jax.ShapeDtypeStruct((width, hidden), BF),
+            jax.ShapeDtypeStruct((8, width), F32),
+        ],
+        in_specs=[vmem] * 5 + [hbm] * 6,
+        out_specs=[vmem] * 7,
+        scratch_shapes=[
+            pltpu.VMEM((ranks, local, width), BF),
+            pltpu.VMEM((ranks, width, hidden), BF),
+            pltpu.VMEM((ranks, hidden, width), BF),
+            pltpu.VMEM((ranks, block, width), F32),
+            pltpu.VMEM((ranks, block, width), BF),
+            pltpu.VMEM((ranks, block, width), BF),
+            pltpu.VMEM((block, width), F32),
+            pltpu.VMEM((block, width), F32),
+            pltpu.VMEM((block, width), F32),
+            pltpu.VMEM((block, width), BF),
+            pltpu.VMEM((ranks * pairs, block, PAIR), BF),
+            copies((ranks,)),
+            copies((ranks,)),
+            copies((ranks,)),
+            copies((2, 12)),
+            copies((2, 12)),
+            copies((2, ranks * pairs)),
+        ],
+        compiler_params=pltpu.CompilerParams(vmem_limit_bytes=62 << 20, collective_id=3, has_side_effects=True),
+        name="middle_stage",
+    )(heads, tokens, cotangent, gains, shifts, *operands)
+
+
 def backward_kernel(
     block, blocks, pairs, chunks, *refs
 ):
-    (qkv_ref, gh_ref, o_ref, log_ref, start_ref, cos_ref, sin_ref, shared_ref, *refs) = refs
+    (qkv_ref, do_ref, o_ref, log_ref, start_ref, cos_ref, sin_ref, shared_ref, *refs) = refs
     terms, refs = refs[: chunks - 1], refs[chunks - 1 :]
     (out_ref, *refs) = refs
     pieces, refs = refs[:chunks], refs[chunks:]
-    dq_ref, inner_ref, do_ref, *refs = refs
+    dq_ref, inner_ref, *refs = refs
     got_x, refs = refs[:chunks], refs[chunks:]
     half, refs = refs[:chunks], refs[chunks:]
     got_z, refs = refs[:chunks], refs[chunks:]
-    got_core, core_sum, got_y, own_ref, head_sems, x_sems, z_sems, core_sems, y_sems = refs
+    got_core, core_sum, got_y, own_ref, x_sems, z_sems, core_sems, y_sems = refs
     terms = [*terms, own_ref]
 
     mine = lax.axis_index("tensor")
@@ -405,14 +655,6 @@
     heads = PAIR // HD
     greet(("tensor", "dp"))
 
-    head_copies = {}
-    for pair in range(pairs):
-        for d in range(1, blocks):
-            copy = push(
-                gh_ref.at[d * pairs + pair], do_ref.at[pair, d], head_sems, pair * (blocks - 1) + d - 1, "tensor", d
-            )
-            copy.start()
-            head_copies[pair, d] = copy
     core_copies = [
         push(shared_ref.at[d + 1], got_core.at[d // 2], core_sems, d // 2, "tensor", 1) for d in range(0, blocks, 2)
     ]
@@ -451,12 +693,7 @@
         own_ref[...] = total.astype(BF)
         x_copies[-1].start()
 
-    for pair in range(pairs):
-        do_ref[pair, 0] = gh_ref[pair]
-
     def prepare(pair):
-        for d in range(1, blocks):
-            head_copies[pair, d].wait_recv()
         dq_ref[...] = jnp.zeros_like(dq_ref)
         for b in range(blocks):
             rows = pl.ds(b * block, block)
@@ -532,7 +769,7 @@
             z_copies[c, d].wait_recv()
         parts = [half[c][z_place]] + [got_z[c][d] for d in range(group - 1)]
         pieces[c][...] = tree_sum(parts).astype(BF)
-    for copy in [*head_copies.values(), *core_copies, *y_copies, *x_copies, *z_copies.values()]:
+    for copy in [*core_copies, *y_copies, *x_copies, *z_copies.values()]:
         copy.wait_send()
 
 
@@ -554,7 +791,6 @@
         scratch_shapes=[
             pltpu.VMEM((length, PAIR), F32),
             pltpu.VMEM((8, length), F32),
-            pltpu.VMEM((pairs, blocks, block, PAIR), BF),
             *[pltpu.VMEM(shape, BF) for shape in inner],
             *[pltpu.VMEM(shape, BF) for shape in inner],
             *[pltpu.VMEM((group - 1, *shape[1:]), BF) for shape in inner],
@@ -562,7 +798,6 @@
             pltpu.VMEM((blocks // 2, *shared.shape[1:]), BF),
             pltpu.VMEM((blocks // 2 - 1, *shared.shape[1:]), BF),
             pltpu.VMEM(shared.shape[1:], BF),
-            copies((2, pairs * (blocks - 1))),
             copies((2, chunks)),
             copies((2, chunks * (group - 1))),
             copies((2, blocks // 2)),
@@ -725,7 +960,6 @@
     length = block * ranks
     local = out_weight.shape[0]
     pairs = local // PAIR
-    residual_in = block_in.reshape(block, width).astype(F32)
     finish = jnp.cumsum(lengths[0])
     begin = finish - lengths[0]
     places = jnp.arange(length, dtype=jnp.int32)
@@ -741,7 +975,7 @@
     start_column = starts.reshape(length, 1)
     start_row = starts.reshape(1, length)
 
-    qkv, attn_full, heads_mixed, logs, heads_parts, (out_rest, up_rest, down_rest) = attend_forward(
+    qkv, attn_full, heads_mixed, logs, heads_parts, rests = attend_forward(
         block_in.reshape(block, width),
         norm_gain[0:1],
         norm_bias[0:1],
@@ -752,72 +986,30 @@
         (out_weight, up_weight, down_weight),
     )
     attn_full = attn_full.reshape(length, width)
-    heads_local = jnp.concatenate([heads_parts[i] for i in range(ranks * pairs)], axis=1)
-    up_parts = [up_weight] + [up_rest[d] for d in range(ranks - 1)]
-    down_parts = [down_weight] + [down_rest[d] for d in range(ranks - 1)]
-
-    out_full = jnp.concatenate([out_weight, out_rest.reshape(-1, width)], axis=0)
-    attn_proj = dot(heads_local, out_full)
-    attn_branch, attn_branch_pull = jax.vjp(layer_norm, attn_proj, norm_gain[1], norm_bias[1])
-    middle = residual_in + attn_branch
-    mlp_norm, mlp_norm_pull = jax.vjp(layer_norm, middle, norm_gain[2], norm_bias[2])
-    mlp_low = mlp_norm.astype(BF)
-    mlp_parts = gather_tensor(mlp_low)
-
-    upward = [dot(mlp_low, part) for part in up_parts]
-    hidden, gelu_pull = jax.vjp(jax.nn.gelu, upward[0])
-    pulls, mlp_proj = [], 0.0
-    for d in range(ranks):
-        hidden, pull = jax.vjp(jax.nn.gelu, upward[d])
-        pulls.append(pull)
-        mlp_proj = mlp_proj + dot(hidden.astype(BF), down_parts[d])
-    mlp_branch, mlp_branch_pull = jax.vjp(layer_norm, mlp_proj, norm_gain[3], norm_bias[3])
-    block_out = (middle + mlp_branch).astype(BF)
-
-    grad_rows = cotangent.reshape(block, width).astype(F32)
-    grad_mlp_proj, gain_three, shift_three = mlp_branch_pull(grad_rows)
-    grad_mlp_low = grad_mlp_proj.astype(BF)
-    grad_mlp_parts = gather_tensor(grad_mlp_low)
-    grad_mlp_norm = 0.0
-    for d in range(ranks):
-        grad_hidden = dot(grad_mlp_low, down_parts[d], NT)
-        grad_upward = pulls[d](grad_hidden)[0].astype(BF)
-        grad_mlp_norm = grad_mlp_norm + dot(grad_upward, up_parts[d], NT)
-    grad_from_norm, gain_two, shift_two = mlp_norm_pull(grad_mlp_norm)
-    grad_middle = grad_rows + grad_from_norm
-    grad_attn_proj, gain_one, shift_one = attn_branch_pull(grad_middle)
-    grad_attn_low = grad_attn_proj.astype(BF)
-    grad_heads = dot(grad_attn_low, out_full, NT).astype(BF)
-
-    mlp_full = jnp.concatenate(mlp_parts, axis=0)
-    grad_mlp_full = jnp.concatenate(grad_mlp_parts, axis=0)
-    upward_own = dot(mlp_full, up_weight)
-    hidden_own, gelu_own_pull = jax.vjp(jax.nn.gelu, upward_own)
-    grad_hidden_own = dot(grad_mlp_full, down_weight, NT)
-    grad_upward_own = gelu_own_pull(grad_hidden_own)[0].astype(BF)
+    block_out, grad_middle, grad_heads, shared, down_term, up_term, early = middle_stage(
+        heads_parts,
+        block_in.reshape(block, width),
+        cotangent.reshape(block, width),
+        norm_gain,
+        norm_bias,
+        (out_weight, up_weight, down_weight),
+        rests,
+    )
     group = lax.axis_size("dp") // 2
-    down_term = dot(hidden_own.astype(BF), grad_mlp_full, TN).astype(BF)
-    up_term = dot(mlp_full, grad_upward_own, TN).astype(BF)
-
-    out_partial = dot(heads_local, grad_attn_low, TN).astype(BF)
-    shared = out_partial.reshape(ranks, 2, group, local // (2 * group), width)
+    shared = shared.reshape(ranks, 2, group, local // (2 * group), width)
     terms = []
     half_columns = width // 2
     for term in (down_term, up_term):
         cut = term.reshape(2, group, term.shape[0] // (2 * group), width)
         terms += [cut[..., :half_columns], cut[..., half_columns:]]
 
-    grad_parts = jnp.stack(
-        [grad_heads[:, i * PAIR : (i + 1) * PAIR] for i in range(width // PAIR)], axis=0
-    )
     grads, *pieces = attend_backward(
-        qkv, grad_parts, heads_mixed, logs, start_row, cosine, sine, shared, terms, block
+        qkv, grad_heads, heads_mixed, logs, start_row, cosine, sine, shared, terms, block
     )
     wide = jnp.concatenate([grads[i] for i in range(3 * pairs)], axis=1)
     qkv_flat = qkv_weight.reshape(width, 3 * local)
     token_terms = dot(wide, qkv_flat, NT).astype(BF).reshape(ranks, block, width)
     qkv_term = dot(attn_full, wide, TN).astype(BF).reshape(2, group, width // (2 * group), 3 * local)
-    early = jnp.stack([gain_one, gain_one, gain_two, gain_three, shift_one, shift_one, shift_two, shift_three])
     input_grad, sums, qkv_sum, *wholes = last_stage(
         block_in.reshape(block, width), norm_gain[0:1], grad_middle, early, token_terms, qkv_term, pieces
     )

time: 483 us -> 431 us (0.89)
  matrix products: 102 us -> 11.8 us
  Pallas kernels: 303 us -> 367 us
  local copies, waits for them, and re-layouts: 44.6 us -> 26.6 us
  other arithmetic: 25 us -> 15.2 us
    dot_general x20 -> x2, matrix products: 102 us -> 11.8 us  [dot(): return lax.dot_general(a, b, dims, preferred_element_type=F32)]
    pallas_call x0 -> x1, Pallas kernels: none -> 71.3 us  [middle_stage(): pl.pallas_call(functools.partial(middle_kernel, block, ranks, pairs), out...]
    unnamed x108 -> x35, local copies, waits for them, and re-layouts: 30.9 us -> 13.8 us
    reduce_sum x10 -> x0, other arithmetic: 8.91 us -> none  [the longest x4 5.73 us: layer_norm(): centre = values - jnp.mean(values, axis=-1, keepdims=True)]
    pallas_call x1, Pallas kernels: 88.2 us -> 81.4 us  [attend_backward(): pl.pallas_call(functools.partial(backward_kernel, block, blocks, pairs, c...]
  transfers between devices with their start and end apart: 6 -> 0, of which waited for: 0 -> 0; matrix products, arithmetic and copies ran while one was open for 16% -> 0% of each run, Pallas kernels for 0% -> 0%
where the time goes in v4:
time: 431 us; the launch traced here: 422 us
  Pallas kernels  367 us (85%)
  local copies, waits for them, and re-layouts  26.6 us (6%)
  other arithmetic  15.2 us (4%)
  matrix products  11.8 us (3%)
    pallas_call x1, Pallas kernels, last_stage(): pl.pallas_call(functools.partial(last_kernel, ranks, count), out_shape=[j...  119 us
    pallas_call x1, Pallas kernels, attend_forward(): pl.pallas_call(functools.partial(forward_kernel, block, ranks, pairs, chu...  95.6 us
    pallas_call x1, Pallas kernels, attend_backward(): pl.pallas_call(functools.partial(backward_kernel, block, blocks, pairs, c...  81.4 us
    pallas_call x1, Pallas kernels, middle_stage(): pl.pallas_call(functools.partial(middle_kernel, block, ranks, pairs), out...  71.3 us
    unnamed x35, local copies, waits for them, and re-layouts  13.8 us
    dot_general x2, matrix products, dot(): return lax.dot_general(a, b, dims, preferred_element_type=F32)  11.8 us

profile of v4, /device:TPU:20, one launch (start us, length us, event | category | flops | bytes accessed | tf_op | source)
XLA Modules:
  0.0 422.1 jit_solution(8252664957219587667)
XLA Ops:
  0.6 0.8 reduce-window.4
  1.5 0.1 convert_reduce_fusion
  1.6 0.7 fusion.5
  2.2 0.1 select_reduce_fusion
  2.3 0.0 copy-start.10
  2.4 5.6 %fusion = (f32[2048,128]{1,0:T(8,128)}, f32[2048,128]{1,0:T(8,128)}) fusion(f32[128]{0:T(128)S(1)} %get-tuple-element.98, f32[128]{0:T(128)S(1)} %get-tuple-element.99, f32[2048]{0:T(1024)S(1)} %subtract_convert_fusion), kind=kLoop, calls=%fused_computation.6 | loop fusion | flops 524288 | bytes 2106368 | tf_op jit(solution)/shard_map/mul | solution.py:974
  7.9 1.3 copy.24.refs_6_
  9.3 1.3 slice.43.refs_1_
  10.6 1.3 slice.44.refs_2_
  11.9 95.6 %attend_forward.1 = (bf16[6,2048,128]{2,1,0:T(8,128)(2,1)}, bf16[4,512,1024]{2,1,0:T(8,128)(2,1)}, bf16[2,2048,128]{2,1,0:T(8,128)(2,1)}, f32[2,8,2048]{2,1,0:T(...) custom-call(bf16[512,1024]{1,0:T(8,128)(2,1)} %bitcast.53, ...), custom_call_target="tpu_custom_call" | custom-call | tf_op jit(solution)/shard_map/attend_forward/pallas_call | solution.py:341
  107.5 0.0 copy-done.10
  107.5 71.3 %middle_stage.1 = (bf16[512,1024]{1,0:T(8,128)(2,1)}, f32[512,1024]{1,0:T(8,128)}, bf16[2,4,512,128]{3,2,1,0:T(8,128)(2,1)}, bf16[4,256,1024]{2,1,0:T(8,128)(2,1...) custom-call(bf16[8,512,128]{2,1,0:T(8,128)(2,1)} %get-tuple-element.37.refs_0_, ...), custom_call_target="tpu_custom_call" | custom-call | tf_op jit(solution)/shard_map/middle_stage/pallas_call | solution.py:600
  178.9 0.0 copy-start.3
  178.9 3.2 fusion.6
  182.1 0.0 copy-done.3
  182.1 1.6 fusion.7
  183.6 0.0 copy-start.12
  183.6 81.4 %attend_backward.1 = (bf16[6,2048,128]{2,1,0:T(8,128)(2,1)}, bf16[128,512]{1,0:T(8,128)(2,1)}, bf16[128,512]{1,0:T(8,128)(2,1)}, bf16[128,512]{1,0:T(8,128)(2,1)...) custom-call(bf16[6,2048,128]{2,1,0:T(8,128)(2,1)} %get-tuple-element.44.refs_0_, ...), custom_call_target="tpu_custom_call" | custom-call | flops 53687091200 | bytes 8388608 | tf_op jit(solution)/shard_map/attend_backward/pallas_call | solution.py:785
  265.0 0.0 copy-start.1
  265.0 1.3 bitcast_dynamic-update-slice_fusion.5
  266.3 1.2 bitcast_dynamic-update-slice_fusion.4
  267.5 1.2 bitcast_dynamic-update-slice_fusion.3
  268.6 0.0 copy-done.1
  268.7 0.1 bitcast_dynamic-update-slice_fusion.2
  268.8 0.1 bitcast_dynamic-update-slice_fusion.1
  268.9 0.1 bitcast_dynamic-update-slice_fusion
  269.1 0.0 copy-start.9
  269.1 0.0 copy-done.12
  269.1 0.0 copy-start
  269.1 4.7 %convolution_convert_fusion.1 = bf16[1024,768]{1,0:T(8,128)(2,1)} fusion(bf16[2048,1024]{1,0:T(8,128)(2,1)S(1)} %bitcast.78, bf16[2048,768]{1,0:T(8,128)(2,1)S(1)} %bitcast_dynamic-update-slice_fusion), kind=kOutput, calls=%fused_computation.3 | convolution fusion | flops 3222011904 | bytes 8912896 | tf_op jit(solution)/shard_map/dot_general | solution.py:24
  273.8 0.0 copy-done.9
  273.8 0.0 copy-done
  273.8 0.9 copy.25
  274.7 7.1 %convolution_convert_fusion = bf16[2048,1024]{1,0:T(8,128)(2,1)} fusion(bf16[2048,768]{1,0:T(8,128)(2,1)} %copy-done.9, bf16[1024,768]{0,1:T(8,128)(2,1)S(1)} %bitcast.66), kind=kOutput, calls=%fused_computation | convolution fusion | flops 3223322624 | bytes 8912896 | tf_op jit(solution)/shard_map/dot_general | solution.py:24
  281.8 119.0 %last_stage.1 = (f32[512,1024]{1,0:T(8,128)}, f32[8,1024]{1,0:T(8,128)}, bf16[2,4,128,768]{3,2,1,0:T(8,128)(2,1)}, bf16[2,4,128,512]{3,2,1,0:T(8,128)(2,1)}, bf1...) custom-call(bf16[512,1024]{1,0:T(8,128)(2,1)} %bitcast.55, ...), custom_call_target="tpu_custom_call" | custom-call | tf_op jit(solution)/shard_map/last_stage/pallas_call | solution.py:920
  400.7 0.0 copy-start.6
  400.8 0.0 copy-start.7
  400.8 4.3 %maximum_convert_fusion.1 = f32[1024,1024]{1,0:T(8,128)} fusion(bf16[1024,512]{1,0:T(8,128)(2,1)} %bitcast.73, bf16[1024,512]{1,0:T(8,128)(2,1)} %bitcast.72), kind=kLoop, calls=%fused_computation.2 | loop fusion | flops 4194304 | bytes 6291456 | tf_op jit(solution)/shard_map/convert_element_type | solution.py:1017
  405.0 0.0 copy-done.6
  405.0 0.0 copy-done.7
  405.0 0.0 copy-start.4
  405.0 2.6 maximum_convert_fusion
  407.6 0.0 copy-done.4
  407.6 3.3 reshape.159
  410.9 0.0 copy-start.2
  410.9 4.6 %copy.28 = f32[1024,3,256]{2,0,1:T(8,128)} copy(f32[1024,3,256]{2,1,0:T(4,128)} %reshape.159) | data formatting | bytes 6291456
  415.5 0.0 copy-start.8
  415.5 0.0 copy-start.11
  415.5 0.0 copy-start.5
  415.5 0.0 copy-done.2
  415.5 3.5 copy.27
  419.0 0.0 copy-done.8
  419.0 1.1 bitcast_convert_fusion
  420.1 0.0 copy-done.11
  420.1 0.6 fusion.8
  420.7 0.0 copy-done.5
  420.7 1.0 copy.37
  (2 shorter events, 0.0 us)
Async XLA Ops:
  2.3 105.2 %copy-start.10 = (s32[2048]{0:T(1024)}, s32[2048]{0:T(1024)S(1)}, u32[]{:S(2)}) copy-start(s32[2048]{0:T(1024)S(1)} %select_reduce_fusion) | copy-start | bytes 24580
  178.9 3.2 copy-start.3
  183.6 85.5 %copy-start.12 = (bf16[4,512,1024]{2,1,0:T(8,128)(2,1)S(1)}, bf16[4,512,1024]{2,1,0:T(8,128)(2,1)}, u32[]{:S(2)}) copy-start(bf16[4,512,1024]{2,1,0:T(8,128)(2,1)} %get-tuple-element.52) | copy-start | bytes 12582916
  265.0 3.6 copy-start.1
  269.1 4.7 %copy-start.9 = (bf16[2048,768]{1,0:T(8,128)(2,1)}, bf16[2048,768]{1,0:T(8,128)(2,1)S(1)}, u32[]{:S(2)}) copy-start(bf16[2048,768]{1,0:T(8,128)(2,1)S(1)} %bitcast_dynamic-update-slice_fusion) | copy-start | bytes 9437188
  269.1 4.7 %copy-start = (bf16[1024,3,256]{2,0,1:T(8,128)(2,1)S(1)}, bf16[1024,3,256]{2,0,1:T(8,128)(2,1)}, u32[]{:S(2)}) copy-start(bf16[1024,3,256]{2,0,1:T(8,128)(2,1)} %param.11) | copy-start | bytes 4718596
  400.7 4.3 %copy-start.6 = (bf16[2,4,128,512]{3,2,1,0:T(8,128)(2,1)S(1)}, bf16[2,4,128,512]{3,2,1,0:T(8,128)(2,1)}, u32[]{:S(2)}) copy-start(bf16[2,4,128,512]{3,2,1,0:T(8,128)(2,1)} %get-tuple-element.61) | copy-start | bytes 3145732
  400.8 4.3 %copy-start.7 = (bf16[2,4,128,512]{3,2,1,0:T(8,128)(2,1)S(1)}, bf16[2,4,128,512]{3,2,1,0:T(8,128)(2,1)}, u32[]{:S(2)}) copy-start(bf16[2,4,128,512]{3,2,1,0:T(8,128)(2,1)} %get-tuple-element.62) | copy-start | bytes 3145732
  405.0 2.6 copy-start.4
  410.9 4.6 %copy-start.2 = (f32[512,1024]{1,0:T(8,128)S(1)}, f32[512,1024]{1,0:T(8,128)}, u32[]{:S(2)}) copy-start(f32[512,1024]{1,0:T(8,128)} %get-tuple-element.58) | copy-start | bytes 6291460
  415.5 3.5 copy-start.8
  415.5 4.6 %copy-start.11 = (f32[8,1024]{1,0:T(8,128)S(1)}, f32[8,1024]{1,0:T(8,128)}, u32[]{:S(2)}) copy-start(f32[8,1024]{1,0:T(8,128)} %get-tuple-element.65) | copy-start | bytes 98308
  415.5 5.2 %copy-start.5 = (bf16[512,1024]{1,0:T(8,128)(2,1)S(1)}, bf16[512,1024]{1,0:T(8,128)(2,1)}, u32[]{:S(2)}) copy-start(bf16[512,1024]{1,0:T(8,128)(2,1)} %get-tuple-element.41) | copy-start | bytes 3145732
